TPU v7x, 32 devices: a whole 2x2x4 slice. The times are simulated.
32 devices in a mesh: blk: 8 (over z, x), head: 4 (over y, core).
Axes of the slice: x: 2, y: 2, z: 4, core: 2. Of those that a mesh axis runs over, the one named last changes fastest.
Arguments:
- inputs: bfloat16 [16384, 768], P(('blk', 'head')), may hold values from -6 to 6
- segments: int32 [16384], replicated, may hold values from 0 to 15, never falling along the last dimension, each value on 1 to 2048 neighbouring positions
- cotangent: bfloat16 [16384, 768], P(('blk', 'head')), may hold values from -6 to 6
- w_qkv: bfloat16 [768, 2304], P(('blk', 'head')), may hold values from -0.3125 to 0.3125
- q_bias: bfloat16 [768], P(('blk', 'head')), may hold values from -3 to 3
- v_bias: bfloat16 [768], P(('blk', 'head')), may hold values from -3 to 3
- w_out: bfloat16 [768, 768], P(('blk', 'head')), may hold values from -1.25 to 1.25
- out_bias: bfloat16 [768], P(('blk', 'head')), may hold values from -3 to 3
- ln1_gain: bfloat16 [768], P(('blk', 'head')), may hold values from 0.5 to 1.5
- ln1_bias: bfloat16 [768], P(('blk', 'head')), may hold values from -2 to 2
- w_in: bfloat16 [768, 3072], P(('blk', 'head')), may hold values from -0.21875 to 0.21875
- in_bias: bfloat16 [3072], P(('blk', 'head')), may hold values from -3 to 3
- w_down: bfloat16 [3072, 768], P(('blk', 'head')), may hold values from -0.15625 to 0.15625
- down_bias: bfloat16 [768], P(('blk', 'head')), may hold values from -3 to 3
- ln2_gain: bfloat16 [768], P(('blk', 'head')), may hold values from 0.5 to 1.5
- ln2_bias: bfloat16 [768], P(('blk', 'head')), may hold values from -2 to 2
Outputs:
- outputs: bfloat16 [16384, 768], P(('blk', 'head'))
- d_inputs: bfloat16 [16384, 768], P(('blk', 'head'))
- d_w_qkv: float32 [768, 2304], P(('blk', 'head'))
- d_q_bias: float32 [768], P(('blk', 'head'))
- d_v_bias: float32 [768], P(('blk', 'head'))
- d_w_out: float32 [768, 768], P(('blk', 'head'))
- d_out_bias: float32 [768], P(('blk', 'head'))
- d_ln1_gain: float32 [768], P(('blk', 'head'))
- d_ln1_bias: float32 [768], P(('blk', 'head'))
- d_w_in: float32 [768, 3072], P(('blk', 'head'))
- d_in_bias: float32 [3072], P(('blk', 'head'))
- d_w_down: float32 [3072, 768], P(('blk', 'head'))
- d_down_bias: float32 [768], P(('blk', 'head'))
- d_ln2_gain: float32 [768], P(('blk', 'head'))
- d_ln2_bias: float32 [768], P(('blk', 'head'))
Inputs may be any that keep to these rules, and one draw needn't show every extreme that they name: `segments`: segment numbers never fall along the tokens; every number from 0 to 15 has 1 to 2048 tokens, and some number has exactly 2048.
All inputs are finite; a program needn't handle non-finite values.
Results may differ from a plain program's by a relative error of at most 0.017.
The roundings to bfloat16 on the way count: a program that leaves them out, or rounds other values in their place, can miss the bound.
Values may be sent and summed in bfloat16 or wider, within the bound.
A program may use at most 128 MiB of HBM per device.

v0:
```python
import functools
import math

import jax
import jax.numpy as jnp
from jax import lax
from jax.experimental import pallas as pl
from jax.experimental.pallas import tpu as pltpu
from jax.sharding import PartitionSpec as P

HEAD_DIM = 64
F32, BF16 = jnp.float32, jnp.bfloat16
NEG = -1e30
MILD = 60.0
SCALE = HEAD_DIM**-0.5
MESH = pl.DeviceIdType.MESH
BOTH = ("blk", "head")
BIAS_ROWS = 8

VMEM = pl.BlockSpec(memory_space=pltpu.VMEM)
SMEM = pl.BlockSpec(memory_space=pltpu.SMEM)
ANY = pl.BlockSpec(memory_space=pl.ANY)


def mm(a, b):
    return jnp.dot(a, b, preferred_element_type=F32)


def mm_tn(a, b):
    return lax.dot_general(a, b, (((0,), (0,)), ((), ())), preferred_element_type=F32)


def mm_nt(a, b):
    return lax.dot_general(a, b, (((1,), (1,)), ((), ())), preferred_element_type=F32)


def column(row):
    return jnp.broadcast_to(row, (8, row.shape[1])).T[:, :1]


def same_document(seg_ref, keys, queries):
    return column(seg_ref[:, keys]) == seg_ref[:, queries]


def attend_body(lo_ref, hi_ref, qkv_ref, seg_ref, out_ref, lse_ref, *, groups, rows, tile):
    def one_query(i, mild):
        at = pl.ds(pl.multiple_of(i * tile, tile), tile)
        win = pl.ds(pl.multiple_of(rows + i * tile, tile), tile)
        queries = [qkv_ref[h, :, win] * BF16(SCALE) for h in range(groups)]

        def one_key(j, state):
            keys = pl.ds(pl.multiple_of(j * tile, tile), tile)
            same = same_document(seg_ref, keys, win)
            new = []
            ahead = mm_tn(qkv_ref[groups, :, keys], queries[0])
            for h in range(groups):
                scores = jnp.where(same, ahead, NEG)
                if h + 1 < groups:
                    ahead = mm_tn(qkv_ref[groups + h + 1, :, keys], queries[h + 1])
                value = qkv_ref[2 * groups + h, :, keys]
                top, total, acc = state[h]
                if mild:
                    weights = jnp.exp(scores)
                else:
                    peak = jnp.maximum(top, jnp.max(scores, axis=0, keepdims=True))
                    weights = jnp.exp(scores - peak)
                    fade = jnp.exp(top - peak)
                    total, acc, top = total * fade, acc * fade, peak
                total = total + jnp.sum(weights, axis=0, keepdims=True)
                new.append((top, total, acc + mm(value, weights.astype(BF16))))
            return tuple(new)

        zero = tuple(
            (jnp.full((1, tile), 0.0 if mild else NEG, F32), jnp.zeros((1, tile), F32), jnp.zeros((HEAD_DIM, tile), F32))
            for _ in range(groups)
        )
        state = lax.fori_loop(lo_ref[i], hi_ref[i], one_key, zero)
        for h in range(groups):
            top, total, acc = state[h]
            out_ref[i, h * HEAD_DIM : (h + 1) * HEAD_DIM, :] = (acc / total).astype(BF16)
            lse_ref[h : h + 1, at] = top + jnp.log(total)

    def longest(part, first, last):
        def grow(j, best):
            at = pl.ds(pl.multiple_of(j * tile, tile), tile)
            for h in range(groups):
                values = qkv_ref[part * groups + h, :, at].astype(F32)
                best = jnp.maximum(best, jnp.sum(values * values, axis=0, keepdims=True))
            return best

        return jnp.max(lax.fori_loop(first, last, grow, jnp.zeros((1, tile), F32)))

    count = rows // tile
    reach = longest(0, count, 2 * count) * longest(1, lo_ref[0], hi_ref[count - 1])
    is_mild = reach <= (MILD / SCALE) ** 2
    for mild in (True, False):

        @pl.when(is_mild == mild)
        def _():
            @pl.loop(0, rows // tile)
            def _(i):
                one_query(i, mild)


def attend(qkv, seg, lo, hi, groups, rows, tile):
    return pl.pallas_call(
        functools.partial(attend_body, groups=groups, rows=rows, tile=tile),
        out_shape=(
            jax.ShapeDtypeStruct((rows // tile, groups * HEAD_DIM, tile), BF16),
            jax.ShapeDtypeStruct((groups, rows), F32),
        ),
        in_specs=[SMEM, SMEM, VMEM, VMEM],
        out_specs=(VMEM, VMEM),
        compiler_params=pltpu.CompilerParams(vmem_limit_bytes=48 << 20),
        cost_estimate=pl.CostEstimate(flops=30_000_000_000, bytes_accessed=12_000_000, transcendentals=15_000_000),
        name="attend",
    )(lo, hi, qkv, seg)


def own_grads_body(
    lo_ref, hi_ref, qkv_ref, do_ref, lse_ref, delta_ref, seg_ref, dq_ref, dk_ref, dv_ref, acc_ref, *, groups, rows, tile
):
    count = rows // tile
    dk_ref[...] = jnp.zeros_like(dk_ref)
    dv_ref[...] = jnp.zeros_like(dv_ref)

    def one_query(i, _):
        at = pl.ds(pl.multiple_of(i * tile, tile), tile)
        win = pl.ds(pl.multiple_of(rows + i * tile, tile), tile)
        acc_ref[...] = jnp.zeros_like(acc_ref)

        def pair(j, own):
            keys = pl.ds(pl.multiple_of(j * tile, tile), tile)
            mine = pl.ds(pl.multiple_of((j - count) * tile, tile), tile)
            same = same_document(seg_ref, keys, win)

            def products(h):
                query = qkv_ref[h, :, win] * BF16(SCALE)
                return query, mm_tn(qkv_ref[groups + h, :, keys], query), mm_tn(qkv_ref[2 * groups + h, :, keys], do_ref[h * HEAD_DIM : (h + 1) * HEAD_DIM, at])

            ahead = products(0)
            for h in range(groups):
                query, scores, d_weights = ahead
                if h + 1 < groups:
                    ahead = products(h + 1)
                weights = jnp.exp(jnp.where(same, scores - lse_ref[h : h + 1, at], NEG))
                d_scores = (weights * (d_weights - delta_ref[h : h + 1, at])).astype(BF16)
                acc_ref[h] += mm(qkv_ref[groups + h, :, keys], d_scores)
                if own:
                    dv_ref[h, mine, :] += mm_nt(weights.astype(BF16), do_ref[h * HEAD_DIM : (h + 1) * HEAD_DIM, at])
                    dk_ref[h, mine, :] += mm_nt(d_scores, query)

        def inside(j, c):
            pair(j, True)
            return c

        def outside(j, c):
            pair(j, False)
            return c

        lo, hi = lo_ref[i], hi_ref[i]
        lax.fori_loop(jnp.maximum(lo, count), jnp.minimum(hi, 2 * count), inside, 0)
        lax.fori_loop(lo, jnp.minimum(hi, count), outside, 0)
        lax.fori_loop(jnp.maximum(lo, 2 * count), hi, outside, 0)
        dq_ref[:, :, at] = (acc_ref[...] * SCALE).astype(BF16)
        return 0

    lax.fori_loop(0, count, one_query, 0)


def own_grads(qkv, d_out, lse, delta, seg, lo, hi, groups, rows, tile):
    return pl.pallas_call(
        functools.partial(own_grads_body, groups=groups, rows=rows, tile=tile),
        out_shape=(
            jax.ShapeDtypeStruct((groups, HEAD_DIM, rows), BF16),
            jax.ShapeDtypeStruct((groups, rows, HEAD_DIM), F32),
            jax.ShapeDtypeStruct((groups, rows, HEAD_DIM), F32),
        ),
        in_specs=[SMEM, SMEM] + [VMEM] * 5,
        out_specs=(VMEM,) * 3,
        scratch_shapes=[pltpu.VMEM((groups, HEAD_DIM, tile), F32)],
        compiler_params=pltpu.CompilerParams(vmem_limit_bytes=52 << 20),
        cost_estimate=pl.CostEstimate(flops=60_000_000_000, bytes_accessed=20_000_000, transcendentals=15_000_000),
        name="own_grads",
    )(lo, hi, qkv, d_out, lse, delta, seg)


def outer_grads_body(
    lo_ref, hi_ref, qkv_ref, do_lo_ref, do_hi_ref, lse_lo_ref, lse_hi_ref, delta_lo_ref, delta_hi_ref, seg_ref, dq_ref, dk_ref, dv_ref, out_ref, dk_acc,
    dv_acc, *, groups, rows, tile
):
    count = rows // tile
    out_ref[:groups] = dq_ref[...]

    def one_key(j, _):
        mine = pl.ds(pl.multiple_of(j * tile, tile), tile)
        keys = pl.ds(pl.multiple_of(rows + j * tile, tile), tile)
        dk_acc[...] = dk_ref[:, mine, :]
        dv_acc[...] = dv_ref[:, mine, :]

        def pair(i, base, do_ref, lse_ref, delta_ref):
            at = pl.ds(pl.multiple_of((i - base) * tile, tile), tile)
            win = pl.ds(pl.multiple_of(i * tile, tile), tile)
            same = same_document(seg_ref, keys, win)

            def products(h):
                query = qkv_ref[h, :, win] * BF16(SCALE)
                return query, mm_tn(qkv_ref[groups + h, :, keys], query), mm_tn(qkv_ref[2 * groups + h, :, keys], do_ref[h * HEAD_DIM : (h + 1) * HEAD_DIM, at])

            ahead = products(0)
            for h in range(groups):
                query, scores, d_weights = ahead
                if h + 1 < groups:
                    ahead = products(h + 1)
                weights = jnp.exp(jnp.where(same, scores - lse_ref[h : h + 1, at], NEG))
                d_scores = (weights * (d_weights - delta_ref[h : h + 1, at])).astype(BF16)
                dv_acc[h] += mm_nt(weights.astype(BF16), do_ref[h * HEAD_DIM : (h + 1) * HEAD_DIM, at])
                dk_acc[h] += mm_nt(d_scores, query)

        def before(i, c):
            pair(i, 0, do_lo_ref, lse_lo_ref, delta_lo_ref)
            return c

        def after(i, c):
            pair(i, 2 * count, do_hi_ref, lse_hi_ref, delta_hi_ref)
            return c

        lo, hi = lo_ref[j], hi_ref[j]
        lax.fori_loop(lo, jnp.minimum(hi, count), before, 0)
        lax.fori_loop(jnp.maximum(lo, 2 * count), hi, after, 0)
        for h in range(groups):
            out_ref[groups + h, :, mine] = dk_acc[h].T.astype(BF16)
            out_ref[2 * groups + h, :, mine] = dv_acc[h].T.astype(BF16)
        return 0

    lax.fori_loop(0, count, one_key, 0)


def outer_grads(qkv, do_lo, do_hi, lse_lo, lse_hi, delta_lo, delta_hi, seg, dq, dk, dv, lo, hi, groups, rows, tile):
    return pl.pallas_call(
        functools.partial(outer_grads_body, groups=groups, rows=rows, tile=tile),
        out_shape=jax.ShapeDtypeStruct((3 * groups, HEAD_DIM, rows), BF16),
        in_specs=[SMEM, SMEM] + [VMEM] * 11,
        out_specs=VMEM,
        scratch_shapes=[pltpu.VMEM((groups, tile, HEAD_DIM), F32)] * 2,
        compiler_params=pltpu.CompilerParams(vmem_limit_bytes=52 << 20),
        cost_estimate=pl.CostEstimate(flops=20_000_000_000, bytes_accessed=20_000_000, transcendentals=5_000_000),
        name="outer_grads",
    )(lo, hi, qkv, do_lo, do_hi, lse_lo, lse_hi, delta_lo, delta_hi, seg, dq, dk, dv)


def place():
    return lax.axis_index("blk"), lax.axis_index("head")


def greet_cross(n_blk, n_head):
    blk, head = place()
    barrier = pltpu.get_barrier_semaphore()

    def say_head(step, c):
        to = lax.rem(head + step, n_head)
        pl.semaphore_signal(barrier, inc=1, device_id=(blk, to), device_id_type=MESH)
        return c

    def say_blk(step, c):
        to = lax.rem(blk + step, n_blk)
        pl.semaphore_signal(barrier, inc=1, device_id=(to, head), device_id_type=MESH)
        return c

    lax.fori_loop(1, n_head, say_head, 0)
    lax.fori_loop(1, n_blk, say_blk, 0)
    pl.semaphore_wait(barrier, n_blk + n_head - 2)


def spread(axis, count, src_of, dst, send_sems, recv_sems):
    blk, head = place()
    me = blk if axis == 0 else head

    def copy(step):
        to = lax.rem(me + step, count)
        return pltpu.make_async_remote_copy(
            src_ref=src_of(to),
            dst_ref=dst,
            send_sem=send_sems.at[step],
            recv_sem=recv_sems.at[step],
            device_id=(to, head) if axis == 0 else (blk, to),
            device_id_type=MESH,
        )

    def begin(step, c):
        copy(step).start()
        return c

    def end(step, c):
        copy(step).wait()
        return c

    lax.fori_loop(1, count, begin, 0)
    return lambda: lax.fori_loop(1, count, end, 0)


def collect_body(
    n_blk, n_head, chunks, x_ref, w_ref, xw_ref, wr_ref, local_sem, near_send, near_recv, w_send, w_recv, x_send, x_recv
):
    blk, head = place()
    rows = x_ref.shape[0] // chunks
    core, row, far = head ^ 1, head ^ 2, head ^ 3
    greet_cross(n_blk, n_head)
    keep_w = pltpu.make_async_copy(w_ref.at[head], wr_ref.at[blk, head], local_sem.at[1])
    keep_w.start()
    wait_near = spread(1, n_head, lambda h: w_ref.at[h], wr_ref.at[blk, head], near_send, near_recv)

    def part(c):
        return pl.ds(c * rows, rows)

    def send(src, slot, owner, c, n, to):
        return pltpu.make_async_remote_copy(
            src_ref=src,
            dst_ref=xw_ref.at[slot, owner, part(c)],
            send_sem=x_send.at[n, c],
            recv_sem=x_recv.at[slot, owner, c],
            device_id=to,
            device_id_type=MESH,
        )

    def arrived(slot, owner, c):
        here = xw_ref.at[slot, owner, part(c)]
        pltpu.make_async_copy(here, here, x_recv.at[slot, owner, c]).wait()

    own = [x_ref.at[part(c)] for c in range(chunks)]
    started = []

    def go(copy):
        copy.start()
        started.append(copy)

    has_before, has_after = blk > 0, blk < n_blk - 1
    to_row = [send(own[c], 1, head, c, 0, (blk, row)) for c in range(chunks)]
    to_core = [send(own[c], 1, head, c, 1, (blk, core)) for c in range(chunks)]
    to_after = [send(own[c], 0, head, c, 2, (blk + 1, head)) for c in range(chunks)]
    to_before = [send(own[c], 2, head, c, 3, (blk - 1, head)) for c in range(chunks)]
    for c in range(chunks):
        go(to_row[c])

        @pl.when(has_after)
        def _():
            to_after[c].start()

        @pl.when(has_before)
        def _():
            to_before[c].start()

        go(to_core[c])
    keep_x = pltpu.make_async_copy(x_ref, xw_ref.at[1, head], local_sem.at[0])
    keep_x.start()
    keep_w.wait()
    wait_near()
    wait_w = spread(0, n_blk, lambda b: wr_ref.at[blk], wr_ref.at[blk], w_send, w_recv)

    for c in range(chunks):
        arrived(1, row, c)
        go(send(xw_ref.at[1, row, part(c)], 1, row, c, 4, (blk, core)))
    halo = []
    for c in range(chunks):
        for slot, there, n in ((0, has_before, 5), (2, has_after, 8)):
            on_row = send(xw_ref.at[slot, head, part(c)], slot, head, c, n, (blk, row))
            on_core = send(xw_ref.at[slot, head, part(c)], slot, head, c, n + 1, (blk, core))
            halo.append((there, on_row))
            halo.append((there, on_core))

            @pl.when(there)
            def _():
                arrived(slot, head, c)
                on_row.start()
                on_core.start()

    for c in range(chunks):
        for slot, there, n in ((0, has_before, 7), (2, has_after, 10)):
            relay = send(xw_ref.at[slot, row, part(c)], slot, row, c, n, (blk, core))
            halo.append((there, relay))

            @pl.when(there)
            def _():
                arrived(slot, row, c)
                relay.start()

    for c in range(chunks):
        arrived(1, core, c)
        arrived(1, far, c)
        for slot, there in ((0, has_before), (2, has_after)):

            @pl.when(there)
            def _():
                arrived(slot, core, c)
                arrived(slot, far, c)

    keep_x.wait()
    wait_w()
    for copy in started:
        copy.wait_send()
    for there, copies in ((has_after, to_after), (has_before, to_before)):

        @pl.when(there)
        def _():
            for copy in copies:
                copy.wait_send()

    for there, copy in halo:

        @pl.when(there)
        def _():
            copy.wait_send()


def collect(x, w, n_blk, n_head):
    chunks = 2
    return pl.pallas_call(
        functools.partial(collect_body, n_blk, n_head, chunks),
        out_shape=(
            jax.ShapeDtypeStruct((3, n_head, *x.shape), x.dtype),
            jax.ShapeDtypeStruct((n_blk, *w.shape), w.dtype),
        ),
        in_specs=[ANY, ANY],
        out_specs=(ANY, ANY),
        scratch_shapes=[
            pltpu.SemaphoreType.DMA((2,)),
            pltpu.SemaphoreType.DMA((n_head,)),
            pltpu.SemaphoreType.DMA((n_head,)),
            pltpu.SemaphoreType.DMA((n_blk,)),
            pltpu.SemaphoreType.DMA((n_blk,)),
            pltpu.SemaphoreType.DMA((11, chunks)),
            pltpu.SemaphoreType.DMA((3, n_head, chunks)),
        ],
        compiler_params=pltpu.CompilerParams(collective_id=0, has_side_effects=True),
        name="collect",
    )(x, w)


def finish_body(
    n_blk, n_head, part_ref, first_ref, w_ref, t_ref, out_ref, dw_ref, dt_ref, near, mine, far_in, w_in, t_in, w_sum, t_sum, w_end,
    t_end, x_send, x_recv, w_send, w_recv, t_send, t_recv, w_send2, w_recv2, t_send2, t_recv2
):
    blk, head = place()
    core, row, far = head ^ 1, head ^ 2, head ^ 3
    greet_cross(n_blk, n_head)

    def send(src, dst, n, to):
        return pltpu.make_async_remote_copy(
            src_ref=src, dst_ref=dst, send_sem=x_send.at[n], recv_sem=x_recv.at[n], device_id=to, device_id_type=MESH
        )

    for_far = send(part_ref.at[far], near.at[1], 1, (blk, core))
    for_core = send(part_ref.at[core], near.at[0], 0, (blk, core))
    for_far.start()
    for_core.start()
    wait_w = spread(0, n_blk, lambda b: w_ref.at[b], w_in.at[blk], w_send, w_recv)
    wait_t = spread(0, n_blk, lambda b: t_ref.at[b], t_in.at[blk], t_send, t_recv)
    for_far.wait()
    mine[...] = (part_ref[row].astype(F32) + near[1].astype(F32)).astype(BF16)
    for_row = send(mine, far_in, 2, (blk, row))
    for_row.start()
    wait_w()
    wait_t()
    w_sum[...] = w_ref[blk].astype(F32)
    t_sum[...] = t_ref[blk]

    def add(step, c):
        other = lax.rem(blk + step, n_blk)
        w_sum[...] += w_in[other].astype(F32)
        t_sum[...] += t_in[other]
        return c

    lax.fori_loop(1, n_blk, add, 0)
    wait_w2 = spread(1, n_head, lambda h: w_sum.at[h], w_end.at[head], w_send2, w_recv2)
    wait_t2 = spread(1, n_head, lambda h: t_sum.at[h], t_end.at[head], t_send2, t_recv2)
    w_end[head] = w_sum[head]
    t_end[head] = t_sum[head]
    for_core.wait()
    wait_w2()
    wait_t2()
    dt_ref[...] = jnp.sum(t_end[...], axis=0)
    parts, cut = dw_ref.shape[0], dw_ref.shape[2] // n_head
    for h in range(n_head):
        for p in range(parts):
            dw_ref[p, :, h * cut : (h + 1) * cut] = w_end[h, :, p * cut : (p + 1) * cut]
    for_row.wait()
    out_ref[...] = (
        first_ref[...] + part_ref[head].astype(F32) + near[0].astype(F32) + far_in[...].astype(F32)
    ).astype(BF16)


def finish(part, d_first, w, table, n_blk, n_head):
    rows, width = d_first.shape
    _, _, per, wide = w.shape
    return pl.pallas_call(
        functools.partial(finish_body, n_blk, n_head),
        out_shape=(
            jax.ShapeDtypeStruct((rows, width), BF16),
            jax.ShapeDtypeStruct((3, per, width), F32),
            jax.ShapeDtypeStruct(table.shape[2:], F32),
        ),
        in_specs=[VMEM] * 4,
        out_specs=(VMEM,) * 3,
        scratch_shapes=[
            pltpu.VMEM((2, rows, width), BF16),
            pltpu.VMEM((rows, width), BF16),
            pltpu.VMEM((rows, width), BF16),
            pltpu.VMEM(w.shape, w.dtype),
            pltpu.VMEM(table.shape, F32),
            pltpu.VMEM(w.shape[1:], F32),
            pltpu.VMEM(table.shape[1:], F32),
            pltpu.VMEM(w.shape[1:], F32),
            pltpu.VMEM(table.shape[1:], F32),
            pltpu.SemaphoreType.DMA((3,)),
            pltpu.SemaphoreType.DMA((3,)),
        ]
        + [pltpu.SemaphoreType.DMA((n_blk,))] * 4
        + [pltpu.SemaphoreType.DMA((n_head,))] * 4,
        compiler_params=pltpu.CompilerParams(collective_id=1, has_side_effects=True, vmem_limit_bytes=40 << 20),
        name="finish",
    )(part, d_first, w, table)


def greet(n_blk, n_head):
    blk, head = place()
    barrier = pltpu.get_barrier_semaphore()
    for step in range(1, n_head):
        pl.semaphore_signal(barrier, inc=1, device_id=(blk, lax.rem(head + step, n_head)), device_id_type=MESH)

    @pl.when(blk > 0)
    def _():
        pl.semaphore_signal(barrier, inc=1, device_id=(blk - 1, head), device_id_type=MESH)

    @pl.when(blk < n_blk - 1)
    def _():
        pl.semaphore_signal(barrier, inc=1, device_id=(blk + 1, head), device_id_type=MESH)

    pl.semaphore_wait(barrier, n_head - 1 + jnp.where(blk > 0, 1, 0) + jnp.where(blk < n_blk - 1, 1, 0))


def to_neighbours(n_blk, n_head, src, lo, hi, send_sem, recv_sem):
    blk, head = place()
    cases = (
        (blk > 0, blk < n_blk - 1, hi, (blk - 1, head)),
        (blk < n_blk - 1, blk > 0, lo, (blk + 1, head)),
    )

    def copy(n):
        return pltpu.make_async_remote_copy(
            src_ref=src, dst_ref=cases[n][2], send_sem=send_sem.at[n], recv_sem=recv_sem.at[n], device_id=cases[n][3],
            device_id_type=MESH,
        )

    for n in range(2):

        @pl.when(cases[n][0])
        def _():
            copy(n).start()

    def wait():
        for n in range(2):

            @pl.when(cases[n][0])
            def _():
                copy(n).wait_send()

            @pl.when(cases[n][1])
            def _():
                copy(n).wait_recv()

    return wait


def to_tokens_body(
    n_blk, n_head, out_ref, lse_ref, seq_ref, lse_lo_ref, lse_hi_ref, keep_sem, send_sem, recv_sem, lse_send, lse_recv
):
    blk, head = place()
    greet(n_blk, n_head)

    def part(h):
        return out_ref.at[h]

    def copy(step):
        to = lax.rem(head + step, n_head)
        return pltpu.make_async_remote_copy(
            src_ref=part(to), dst_ref=seq_ref.at[head], send_sem=send_sem.at[step], recv_sem=recv_sem.at[step],
            device_id=(blk, to), device_id_type=MESH,
        )

    for step in range(n_head - 1, 0, -1):
        copy(step).start()
    keep = pltpu.make_async_copy(part(head), seq_ref.at[head], keep_sem)
    keep.start()
    wait = to_neighbours(n_blk, n_head, lse_ref, lse_lo_ref, lse_hi_ref, lse_send, lse_recv)
    for step in range(1, n_head):
        copy(step).wait()
    wait()
    keep.wait()


def to_tokens(out, lse, n_blk, n_head):
    stat = jax.ShapeDtypeStruct(lse.shape, lse.dtype)
    return pl.pallas_call(
        functools.partial(to_tokens_body, n_blk, n_head),
        out_shape=(jax.ShapeDtypeStruct(out.shape, out.dtype), stat, stat),
        in_specs=[ANY, ANY],
        out_specs=(ANY,) * 3,
        scratch_shapes=[
            pltpu.SemaphoreType.DMA,
            pltpu.SemaphoreType.DMA((n_head,)),
            pltpu.SemaphoreType.DMA((n_head,)),
            pltpu.SemaphoreType.DMA((2,)),
            pltpu.SemaphoreType.DMA((2,)),
        ],
        compiler_params=pltpu.CompilerParams(collective_id=2, has_side_effects=True),
        name="to_tokens",
    )(out, lse)


def to_heads_body(
    n_blk, n_head, dseq_ref, dpart_ref, do_ref, delta_ref, delta_lo_ref, delta_hi_ref, keep_sem, send_sem, recv_sem, d_send,
    d_recv, n_send, n_recv
):
    blk, head = place()
    tok = dseq_ref.shape[2]
    greet(n_blk, n_head)
    at = pl.ds(pl.multiple_of(head * tok, tok), tok)

    def copy(step):
        to = lax.rem(head + step, n_head)
        return pltpu.make_async_remote_copy(
            src_ref=dseq_ref.at[to], dst_ref=do_ref.at[:, at], send_sem=send_sem.at[step], recv_sem=recv_sem.at[step],
            device_id=(blk, to), device_id_type=MESH,
        )

    def small_copy(step):
        to = lax.rem(head + step, n_head)
        return pltpu.make_async_remote_copy(
            src_ref=dpart_ref.at[to], dst_ref=delta_ref.at[head], send_sem=d_send.at[step], recv_sem=d_recv.at[step],
            device_id=(blk, to), device_id_type=MESH,
        )

    keep = (
        pltpu.make_async_copy(dseq_ref.at[head], do_ref.at[:, at], keep_sem.at[0]),
        pltpu.make_async_copy(dpart_ref.at[head], delta_ref.at[head], keep_sem.at[1]),
    )
    for step in range(n_head - 1, 0, -1):
        small_copy(step).start()
        copy(step).start()
    for local in keep:
        local.start()
    for step in range(1, n_head):
        small_copy(step).wait()
    keep[1].wait()
    wait = to_neighbours(n_blk, n_head, delta_ref, delta_lo_ref, delta_hi_ref, n_send, n_recv)
    for step in range(1, n_head):
        copy(step).wait()
    keep[0].wait()
    wait()


def to_heads(d_seq, d_part, n_blk, n_head):
    _, cut, tok = d_seq.shape
    stat = jax.ShapeDtypeStruct(d_part.shape, F32)
    return pl.pallas_call(
        functools.partial(to_heads_body, n_blk, n_head),
        out_shape=(jax.ShapeDtypeStruct((cut, n_head * tok), BF16), stat, stat, stat),
        in_specs=[ANY, ANY],
        out_specs=(ANY,) * 4,
        scratch_shapes=[
            pltpu.SemaphoreType.DMA((2,)),
            pltpu.SemaphoreType.DMA((n_head,)),
            pltpu.SemaphoreType.DMA((n_head,)),
            pltpu.SemaphoreType.DMA((n_head,)),
            pltpu.SemaphoreType.DMA((n_head,)),
            pltpu.SemaphoreType.DMA((2,)),
            pltpu.SemaphoreType.DMA((2,)),
        ],
        compiler_params=pltpu.CompilerParams(collective_id=3, has_side_effects=True),
        name="to_heads",
    )(d_seq, d_part)


def project_body(x_ref, w_ref, bias_ref, out_ref, turned_ref):
    @pl.when(pl.program_id(0) == 0)
    def _():
        turned_ref[...] = w_ref[...].T

    out_ref[...] = (mm_nt(turned_ref[...], x_ref[...]) + bias_ref[...]).astype(BF16)


def project(x, w, bias, tile):
    rows, width = x.shape
    wide = w.shape[1]
    whole = lambda i: (0, 0)
    return pl.pallas_call(
        project_body,
        grid=(rows // tile,),
        out_shape=(jax.ShapeDtypeStruct((wide, rows), BF16), jax.ShapeDtypeStruct((wide, width), BF16)),
        in_specs=[
            pl.BlockSpec((tile, width), lambda i: (i, 0)),
            pl.BlockSpec((width, wide), whole),
            pl.BlockSpec((wide, 1), whole),
        ],
        out_specs=(pl.BlockSpec((wide, tile), lambda i: (0, i)), pl.BlockSpec((wide, width), whole)),
        compiler_params=pltpu.CompilerParams(vmem_limit_bytes=32 << 20),
        cost_estimate=pl.CostEstimate(flops=2 * rows * width * wide, bytes_accessed=20_000_000, transcendentals=0),
        name="project",
    )(x, w, bias)


def project_back_body(d_ref, x_ref, turned_ref, dw_ref, part_ref, sum_ref, acc_ref):
    step = pl.program_id(0)
    d = d_ref[...]
    part_ref[...] = mm_tn(d, turned_ref[...]).astype(BF16)
    product = mm(d, x_ref[...])
    total = jnp.sum(d.astype(F32), axis=1, keepdims=True)

    @pl.when(step == 0)
    def _():
        acc_ref[...] = product
        sum_ref[...] = total

    @pl.when(step > 0)
    def _():
        acc_ref[...] += product
        sum_ref[...] += total

    @pl.when(step == pl.num_programs(0) - 1)
    def _():
        dw_ref[...] = acc_ref[...].T.astype(BF16)


def project_back(d_qkv, x_win, turned, tile):
    wide, rows = d_qkv.shape
    width = x_win.shape[1]
    whole = lambda i: (0, 0)
    return pl.pallas_call(
        project_back_body,
        grid=(rows // tile,),
        out_shape=(
            jax.ShapeDtypeStruct((width, wide), BF16),
            jax.ShapeDtypeStruct((rows, width), BF16),
            jax.ShapeDtypeStruct((wide, 1), F32),
        ),
        in_specs=[
            pl.BlockSpec((wide, tile), lambda i: (0, i)),
            pl.BlockSpec((tile, width), lambda i: (rows // tile + i, 0)),
            pl.BlockSpec((wide, width), whole),
        ],
        out_specs=(
            pl.BlockSpec((width, wide), whole),
            pl.BlockSpec((tile, width), lambda i: (i, 0)),
            pl.BlockSpec((wide, 1), whole),
        ),
        scratch_shapes=[pltpu.VMEM((wide, width), F32)],
        compiler_params=pltpu.CompilerParams(vmem_limit_bytes=32 << 20),
        cost_estimate=pl.CostEstimate(flops=4 * rows * width * wide, bytes_accessed=12_000_000, transcendentals=0),
        name="project_back",
    )(d_qkv, x_win, turned)


def normalize(values):
    centre = jnp.mean(values, axis=-1, keepdims=True)
    centered = values - centre
    r = lax.rsqrt(jnp.mean(centered * centered, axis=-1, keepdims=True) + 1e-05)
    return centered * r, r


def normalize_back(d_values, unit, r, gain):
    scaled = d_values * gain
    return r * (
        scaled - jnp.mean(scaled, axis=-1, keepdims=True) - unit * jnp.mean(scaled * unit, axis=-1, keepdims=True)
    )


def over_rows(values):
    return jnp.sum(values, axis=0, keepdims=True)


def dense_body(
    x_ref, seq_ref, cot_ref, vec_ref, inb_ref, w_hbm, out_ref, first_ref, dseq_ref, delta_ref, dvec_ref, dinb_ref, grad_hbm, w, grad,
    unit_ref, r_ref, normed_ref, low_ref, acc_ref, slope_ref, act_ref, e_ref, w_sem, grad_sem, *, blocks
):
    width = x_ref.shape[1]
    out_at, down_at = blocks * width, (blocks + 1) * width

    def fetch(first, size, n):
        at = pl.ds(first, size)
        copy = pltpu.make_async_copy(w_hbm.at[:, at], w.at[:, at], w_sem.at[n])
        copy.start()
        return copy

    def cols(first, c):
        return pl.ds(pl.multiple_of(first + c * width, 128), width)

    def put(first, c, n):
        at = cols(first, c)
        return pltpu.make_async_copy(grad.at[:, at], grad_hbm.at[:, at], grad_sem.at[n])

    w_out_here = fetch(out_at, width, 0)
    w_in_here = fetch(0, out_at, 1)
    w_down_here = fetch(down_at, blocks * width, 2)
    out_bias, ln1_gain, ln1_bias, down_bias, ln2_gain, ln2_bias = (vec_ref[n : n + 1] for n in range(6))
    w_out_here.wait()
    unit, r = normalize(x_ref[...].astype(F32) + mm_tn(seq_ref[...], w[:, out_at:down_at]) + out_bias)
    unit_ref[...] = unit
    r_ref[...] = r
    normed = unit * ln1_gain + ln1_bias
    normed_ref[...] = normed
    low_ref[...] = normed.astype(BF16)
    acc_ref[...] = normed + down_bias
    w_in_here.wait()
    w_down_here.wait()

    def up_down(c, carry):
        at = cols(0, c)
        hidden = mm(low_ref[...], w[:, at]) + inb_ref[:, at]
        phi = 0.5 + 0.5 * lax.erf(hidden * (2.0**-0.5))
        act = (hidden * phi).astype(BF16)
        act_ref[:, at] = act
        slope_ref[:, at] = phi + hidden * (jnp.exp(-0.5 * hidden * hidden) * ((2.0 * math.pi) ** -0.5))
        acc_ref[...] += mm(act, w[:, cols(down_at, c)])
        return carry

    lax.fori_loop(0, blocks, up_down, 0)
    unit2, r2 = normalize(acc_ref[...])
    out_ref[...] = (unit2 * ln2_gain + ln2_bias).astype(BF16)
    dy = cot_ref[...].astype(F32)
    dvec_ref[4:5] = over_rows(dy * unit2)
    dvec_ref[5:6] = over_rows(dy)
    d_second = normalize_back(dy, unit2, r2, ln2_gain)
    e_ref[...] = d_second.astype(BF16)
    dvec_ref[3:4] = over_rows(e_ref[...].astype(F32))
    acc_ref[...] = d_second

    def back(c, carry):
        at, down = cols(0, c), cols(down_at, c)
        e = e_ref[...]
        d_hidden = (mm_nt(e, w[:, down]) * slope_ref[:, at]).astype(BF16)
        dinb_ref[:, at] = over_rows(d_hidden.astype(F32))
        acc_ref[...] += mm_nt(d_hidden, w[:, at])
        grad[:, at] = mm_tn(low_ref[...], d_hidden).astype(BF16)
        put(0, c, c).start()
        grad[:, down] = mm_tn(act_ref[:, at], e).astype(BF16)
        put(down_at, c, blocks + c).start()
        return carry

    lax.fori_loop(0, blocks, back, 0)
    d_normed = acc_ref[...]
    unit = unit_ref[...]
    dvec_ref[1:2] = over_rows(d_normed * unit)
    dvec_ref[2:3] = over_rows(d_normed)
    d_first = normalize_back(d_normed, unit, r_ref[...], ln1_gain)
    first_ref[...] = d_first
    e_first = d_first.astype(BF16)
    dvec_ref[0:1] = over_rows(e_first.astype(F32))
    grad[:, out_at:down_at] = mm(seq_ref[...], e_first).astype(BF16)
    put(out_at, 0, 2 * blocks).start()
    d_seq = mm_nt(w[:, out_at:down_at], e_first).astype(BF16)
    dseq_ref[...] = d_seq
    product = d_seq.astype(F32) * seq_ref[...].astype(F32)
    n_head, groups, _ = delta_ref.shape
    for n in range(n_head):
        for g in range(groups):
            first = (n * groups + g) * HEAD_DIM
            delta_ref[n, g : g + 1] = over_rows(product[first : first + HEAD_DIM])

    def done(c, carry):
        put(0, c, c).wait()
        put(down_at, c, blocks + c).wait()
        return carry

    lax.fori_loop(0, blocks, done, 0)
    put(out_at, 0, 2 * blocks).wait()


def dense(x, seq_t, cotangent, vectors, in_bias, weights, blocks, n_head):
    tok, width = x.shape
    ff = blocks * width
    return pl.pallas_call(
        functools.partial(dense_body, blocks=blocks),
        out_shape=(
            jax.ShapeDtypeStruct((tok, width), BF16),
            jax.ShapeDtypeStruct((tok, width), F32),
            jax.ShapeDtypeStruct((width, tok), BF16),
            jax.ShapeDtypeStruct((n_head, width // n_head // HEAD_DIM, tok), F32),
            jax.ShapeDtypeStruct((8, width), F32),
            jax.ShapeDtypeStruct((1, ff), F32),
            jax.ShapeDtypeStruct(weights.shape, BF16),
        ),
        in_specs=[VMEM] * 5 + [ANY],
        out_specs=(VMEM,) * 6 + (ANY,),
        scratch_shapes=[
            pltpu.VMEM(weights.shape, BF16),
            pltpu.VMEM(weights.shape, BF16),
            pltpu.VMEM((tok, width), F32),
            pltpu.VMEM((tok, 1), F32),
            pltpu.VMEM((tok, width), F32),
            pltpu.VMEM((tok, width), BF16),
            pltpu.VMEM((tok, width), F32),
            pltpu.VMEM((tok, ff), F32),
            pltpu.VMEM((tok, ff), BF16),
            pltpu.VMEM((tok, width), BF16),
            pltpu.SemaphoreType.DMA((3,)),
            pltpu.SemaphoreType.DMA((2 * blocks + 1,)),
        ],
        compiler_params=pltpu.CompilerParams(vmem_limit_bytes=58 << 20),
        cost_estimate=pl.CostEstimate(flops=17_000_000_000, bytes_accessed=30_000_000, transcendentals=3_000_000),
        name="dense",
    )(x, seq_t, cotangent, vectors, in_bias, weights)


def window_of(segments, blk, rows, tile):
    padded = jnp.concatenate(
        [jnp.full((rows,), -1, jnp.int32), segments, jnp.full((rows,), 1 << 30, jnp.int32)]
    )
    seg = lax.dynamic_slice_in_dim(padded, blk * rows, 3 * rows, 0)
    own = seg[rows : 2 * rows]
    below = jnp.sum((seg[None, :] < own[::tile][:, None]).astype(jnp.int32), axis=1)
    upto = jnp.sum((seg[None, :] <= own[tile - 1 :: tile][:, None]).astype(jnp.int32), axis=1)
    return seg[None], below // tile, (upto - 1) // tile + 1


def shift(value, steps):
    count = lax.axis_size("blk")
    first, last = max(0, -steps), min(count, count - steps)
    return lax.ppermute(value, "blk", [(source, source + steps) for source in range(first, last)])


def body(
    inputs, segments, cotangent, w_qkv, q_bias, v_bias, w_out, out_bias, ln1_gain, ln1_bias, w_in, in_bias, w_down,
    down_bias, ln2_gain, ln2_bias
):
    n_blk, n_head = lax.axis_size("blk"), lax.axis_size("head")
    count = n_blk * n_head
    blk, head = place()
    tok, width = inputs.shape
    rows = tok * n_head
    per = w_qkv.shape[0]
    ff = w_in.shape[1]
    blocks = ff // width
    cut = width // n_head
    groups = cut // HEAD_DIM
    down_per = w_down.shape[0]

    unit = down_per // blocks

    def reorder(values):
        return values.reshape(-1, count, blocks, unit).transpose(0, 2, 1, 3).reshape(values.shape)

    def restore(values):
        return values.reshape(-1, blocks, count, unit).transpose(0, 2, 1, 3).reshape(values.shape)

    down = w_down.reshape(blocks, unit, width).transpose(1, 0, 2).reshape(unit, ff)
    whole = lax.all_gather(jnp.concatenate([reorder(w_in), w_out, down], axis=1), BOTH, axis=0, tiled=True)

    small = (q_bias, v_bias, out_bias, ln1_gain, ln1_bias, down_bias, ln2_gain, ln2_bias, in_bias)
    bias_row = jnp.concatenate(small)
    small_cols = 3 * cut
    bias_pad = jnp.zeros((BIAS_ROWS, small_cols), BF16).at[0, : bias_row.shape[0]].set(bias_row)
    columns = w_qkv.reshape(per, 3, n_head, cut).transpose(2, 0, 1, 3).reshape(n_head, per, 3 * cut)
    to_send = jnp.concatenate([columns, jnp.broadcast_to(bias_pad[None], (n_head, BIAS_ROWS, small_cols))], axis=1)
    x_win, got = collect(inputs, to_send, n_blk, n_head)
    x_win = x_win.reshape(3 * rows, width)
    got = got.reshape(count, *got.shape[2:])
    w_mine = got[:, :per].reshape(width, 3 * cut)
    all_small = got[:, per, : bias_row.shape[0]].astype(F32)
    offsets = [0]
    for vec in small:
        offsets.append(offsets[-1] + vec.shape[0])
    (f_q_bias, f_v_bias, f_out_bias, f_ln1_gain, f_ln1_bias, f_down_bias, f_ln2_gain, f_ln2_bias, f_in_bias) = (
        all_small[:, a:b].reshape(-1) for a, b in zip(offsets[:-1], offsets[1:])
    )
    mine = lambda vec: lax.dynamic_slice_in_dim(vec, head * cut, cut, 0)
    qkv_bias = jnp.concatenate([mine(f_q_bias), jnp.zeros((cut,), F32), mine(f_v_bias)])

    qkv, turned = project(x_win, w_mine, qkv_bias[:, None], tok)
    qkv = qkv.reshape(3 * groups, HEAD_DIM, 3 * rows)
    seg, lo, hi = window_of(segments, blk, rows, tok)
    attended, lse = attend(qkv, seg, lo, hi, groups, rows, tok)
    seq_t, lse_lo, lse_hi = to_tokens(attended, lse, n_blk, n_head)
    seq_t = seq_t.reshape(width, tok)

    vectors = jnp.stack([f_out_bias, f_ln1_gain, f_ln1_bias, f_down_bias, f_ln2_gain, f_ln2_bias] + [f_out_bias] * 2)
    outputs, d_first, d_seq_t, d_part, d_vectors, d_in_bias, grads = dense(
        inputs, seq_t, cotangent, vectors, reorder(f_in_bias)[None], whole, blocks, n_head
    )
    d_out_bias, d_ln1_gain, d_ln1_bias, d_down_bias, d_ln2_gain, d_ln2_bias = (d_vectors[n] for n in range(6))
    d_in_bias = restore(d_in_bias[0])
    d_out, delta, delta_lo, delta_hi = to_heads(d_seq_t.reshape(n_head, cut, tok), d_part, n_blk, n_head)
    delta, delta_lo, delta_hi = (a.transpose(1, 0, 2).reshape(groups, rows) for a in (delta, delta_lo, delta_hi))

    owned = lax.psum_scatter(grads, BOTH, scatter_dimension=0, tiled=True).astype(F32)

    do_lo, do_hi = shift(d_out, 1), shift(d_out, -1)
    dq, dk, dv = own_grads(qkv, d_out, lse, delta, seg, lo, hi, groups, rows, tok)
    d_qkv = outer_grads(
        qkv, do_lo, do_hi, lse_lo, lse_hi, delta_lo, delta_hi, seg, dq, dk, dv, lo, hi, groups, rows, tok
    ).reshape(3 * cut, rows)

    d_w_qkv, d_part, d_biases = project_back(d_qkv, x_win, turned, tok)
    d_biases = d_biases[:, 0]
    place_own = lambda vec: lax.dynamic_update_slice_in_dim(jnp.zeros((width,), F32), vec, head * cut, 0)
    vectors = (
        place_own(d_biases[:cut]), place_own(d_biases[2 * cut :]), d_out_bias, d_ln1_gain, d_ln1_bias, d_down_bias, d_ln2_gain,
        d_ln2_bias, d_in_bias,
    )
    table = jnp.concatenate([vec.reshape(count, -1) for vec in vectors], axis=1)
    lanes = 128
    table_rows = -(-table.shape[1] // (8 * lanes)) * 8
    table = jnp.pad(table, ((0, 0), (0, table_rows * lanes - table.shape[1])))
    d_inputs, w_rows, sums = finish(
        d_part.reshape(n_head, tok, width), d_first, d_w_qkv.reshape(n_blk, n_head, per, 3 * cut),
        table.reshape(n_blk, n_head, table_rows, lanes), n_blk, n_head,
    )
    own_w_qkv = w_rows.transpose(1, 0, 2).reshape(per, 3 * width)
    sums = sums.reshape(-1)
    (o_q_bias, o_v_bias, o_out_bias, o_ln1_gain, o_ln1_bias, o_down_bias, o_ln2_gain, o_ln2_bias, o_in_bias) = (
        sums[a:b] for a, b in zip(offsets[:-1], offsets[1:])
    )
    own_w_in = restore(owned[:, :ff])
    own_w_out = owned[:, ff : ff + width]
    own_w_down = owned[:, ff + width :].reshape(unit, blocks, width).transpose(1, 0, 2).reshape(down_per, width)
    return (
        outputs, d_inputs, own_w_qkv, o_q_bias, o_v_bias, own_w_out, o_out_bias, o_ln1_gain, o_ln1_bias,
        own_w_in, o_in_bias, own_w_down, o_down_bias, o_ln2_gain, o_ln2_bias,
    )


def solution(mesh):
    rows, vec = P(BOTH, None), P(BOTH)
    placed = (rows, P(), rows, rows, vec, vec, rows, vec, vec, vec, rows, vec, rows, vec, vec, vec)
    return jax.shard_map(
        body,
        mesh=mesh,
        in_specs=placed,
        out_specs=(rows, rows, rows, vec, vec, rows, vec, vec, vec, rows, vec, rows, vec, vec, vec),
        check_vma=False,
    )
```

profile of v0, /device:TPU:0, one launch (start us, length us, event | category | flops | bytes accessed | tf_op | source)
XLA Modules:
  0.0 385.4 jit_solution(1285778376388659898)
XLA Ops:
  7.4 2.2 reshape.167
  9.7 1.3 reshape.168
  13.5 59.4 %collect.1 = (bf16[3,4,512,768]{3,2,1,0:T(8,128)(2,1)}, bf16[8,4,32,576]{3,2,1,0:T(8,128)(2,1)}) custom-call(bf16[512,768]{1,0:T(8,128)(2,1)} %x_ref.3, bf16[4,32,576]{2,1,0:T(8,128)(2,1)} %pad_maximum_fusion.1.w_ref), custom_call_target="tpu_custom_call" | custom-call | tf_op jit(solution)/shard_map/collect/pallas_call | solution.py:417
  73.9 1.3 slice.161
  77.6 3.7 copy-done.8
  81.3 8.7 %project.1 = (bf16[576,6144]{1,0:T(8,128)(2,1)S(1)}, bf16[576,768]{1,0:T(8,128)(2,1)S(1)}) custom-call(bf16[6144,768]{1,0:T(8,128)(2,1)S(1)} %bitcast.59, bf16[768,576]{1,0:T(8,128)(2,1)S(1)} %bitcast.50, f32[576,1]{1,0:T(8,128)S(1)} %broadcast_in_dim.35.bias_ref), custom_call_target="tpu_custom_call" | custom-call | flops 5435817984 | bytes 20000000 | tf_op jit(solution)/shard_map/project/pallas_call | solution.py:696
  90.0 3.0 copy-done.16
  93.9 26.0 %attend.1 = (bf16[4,192,512]{2,1,0:T(8,128)(2,1)S(1)}, f32[3,2048]{1,0:T(4,128)S(1)}) custom-call(s32[4]{0:T(128)S(1)} %get-tuple-element.113.lo_ref, s32[4]{0:T(128)S(1)} %get-tuple-element.114.hi_ref, bf16[9,64,6144]{2,1,0:T(8,128)(2,1)} %bitcast.64, s32[1,6144]{1,0:T(1,128)S(1)} %bitcast.54), custom_call_target="tpu_custom_call" | custom-call | flops 30000001024 | bytes 12000000 | tf_op jit(solution)/shard_map/attend/pallas_call | solution.py:106
  121.4 38.9 %to_tokens.1 = (bf16[4,192,512]{2,1,0:T(8,128)(2,1)}, f32[3,2048]{1,0:T(4,128)}, f32[3,2048]{1,0:T(4,128)}) custom-call(bf16[4,192,512]{2,1,0:T(8,128)(2,1)} %copy-done.5, f32[3,2048]{1,0:T(4,128)} %copy-done.6), custom_call_target="tpu_custom_call" | custom-call | tf_op jit(solution)/shard_map/to_tokens/pallas_call | solution.py:603
  161.0 29.8 %dense.1 = (bf16[512,768]{1,0:T(8,128)(2,1)}, f32[512,768]{1,0:T(8,128)}, bf16[768,512]{1,0:T(8,128)(2,1)}, f32[4,3,512]{2,1,0:T(4,128)}, f32[8,768]{1,0:T(8,128...) custom-call(bf16[512,768]{1,0:T(8,128)(2,1)} %x_ref.3, bf16[768,512]{1,0:T(8,128)(2,1)} %bitcast.82, ...), custom_call_target="tpu_custom_call" | custom-call | flops 16999999488 | bytes 30000000 | tf_op jit(solution)/shard_map/dense/pallas_call | solution.py:881
  190.8 18.0 %to_heads.1 = (bf16[192,2048]{1,0:T(8,128)(2,1)}, f32[4,3,512]{2,1,0:T(4,128)}, f32[4,3,512]{2,1,0:T(4,128)}, f32[4,3,512]{2,1,0:T(4,128)}) custom-call(bf16[4,192,512]{2,1,0:T(8,128)(2,1)} %bitcast.73, f32[4,3,512]{2,1,0:T(4,128)} %get-tuple-element.64.dpart_ref), custom_call_target="tpu_custom_call" | custom-call | tf_op jit(solution)/shard_map/to_heads/pallas_call | solution.py:665
  208.9 4.0 %collective-permute-start = (bf16[192,2048]{1,0:T(8,128)(2,1)}, bf16[192,2048]{1,0:T(8,128)(2,1)S(1)}, u32[]{:S(2)}, u32[]{:S(2)}) collective-permute-start(bf16[192,2048]{1,0:T(8,128)(2,1)} %get-tuple-element.65.do_ref), channel_id=1, source_target_pairs={{0,4},{4,8},{8,12},{12,16},{16,20},{20,24},{24,28},{1,5},{5,9},{9,... | collective-permute-start | bytes 2359304 | tf_op jit(solution)/shard_map/ppermute | solution.py:928
  212.9 1.3 collective-permute-start.1
  216.2 39.6 %own_grads.1 = (bf16[3,64,2048]{2,1,0:T(8,128)(2,1)S(1)}, f32[3,2048,64]{2,1,0:T(8,128)}, f32[3,2048,64]{2,1,0:T(8,128)}) custom-call(s32[4]{0:T(128)S(1)} %get-tuple-element.113.lo_ref, s32[4]{0:T(128)S(1)} %get-tuple-element.114.hi_ref, bf16[9,64,6144]{2,1,0:T(8,128)(2,1)} %bitcast.65, bf16[192,2048]{1,0:T(8,128)(2,1)S(1)} %copy-done.10, ...), custom_call_target="tpu_custom_call" | custom-call | flops 60000002048 | bytes 20000000 | tf_op jit(solution)/shard_map/own_grads/pallas_call | solution.py:172
  258.7 12.3 %outer_grads.1 = bf16[9,64,2048]{2,1,0:T(8,128)(2,1)} custom-call(s32[4]{0:T(128)S(1)} %get-tuple-element.113.lo_ref, s32[4]{0:T(128)S(1)} %get-tuple-element.114.hi_ref, bf16[9,64,6144]{2,1,0:T(8,128)(2,1)} %bitcast.66, bf16[192,2048]{1,0:T(8,128)(2,1)S(1)} %collective-permute-done.do_lo_ref, bf16[192,2048]{1,0:T(8,128)(2,1)S(1)} %collective-permute-done.1.do_hi_ref, ...), custom_call_target="tpu_custom_call" | custom-call | flops 20000000000 | bytes 20000000 | tf_op jit(solution)/shard_map/outer_grads/pallas_call | solution.py:240
  271.0 3.8 copy-done.9
  274.8 1.7 copy-done.17
  276.6 6.3 %project_back.1 = (bf16[768,576]{1,0:T(8,128)(2,1)S(1)}, bf16[2048,768]{1,0:T(8,128)(2,1)S(1)}, f32[576,1]{1,0:T(8,128)S(1)}) custom-call(bf16[576,2048]{1,0:T(8,128)(2,1)S(1)} %bitcast.67, bf16[6144,768]{1,0:T(8,128)(2,1)S(1)} %bitcast.60, bf16[576,768]{1,0:T(8,128)(2,1)S(1)} %copy-done.19), custom_call_target="tpu_custom_call" | custom-call | flops 3623878656 | bytes 12000000 | tf_op jit(solution)/shard_map/project_back/pallas_call | solution.py:738
  285.1 1.4 copy-done
  286.5 1.2 copy-done.2
  287.7 76.4 %finish.1 = (bf16[512,768]{1,0:T(8,128)(2,1)S(1)}, f32[3,24,768]{2,1,0:T(8,128)S(1)}, f32[8,128]{1,0:T(8,128)S(1)}) custom-call(bf16[4,512,768]{2,1,0:T(8,128)(2,1)S(1)} %bitcast.49, f32[512,768]{1,0:T(8,128)S(1)} %copy-done, bf16[8,4,24,576]{3,2,1,0:T(8,128)(2,1)S(1)} %bitcast.51, f32[8,4,8,128]{3,2,1,0:T(8,128)S(1)} %bitcast.52), custom_call_target="tpu_custom_call" | custom-call | tf_op jit(solution)/shard_map/finish/pallas_call | solution.py:495
  369.0 2.4 copy.56
  371.4 4.0 %reshape.184 = f32[24,3072]{1,0:T(8,128)} reshape(f32[24,32,4,24]{3,2,1,0:T(4,128)} %copy.56) | data formatting | bytes 589824 | tf_op jit(solution)/shard_map/reshape | solution.py:953
  376.3 1.4 slice.172
  (145 shorter events, 22.5 us)
Async XLA Ops:
  7.2 4.8 %copy-start.23 = (s32[16384]{0:T(1024)S(1)}, s32[16384]{0:T(1024)}, u32[]{:S(2)}) copy-start(s32[16384]{0:T(1024)} %param.19) | copy-start | bytes 196612
  7.2 5.0 %copy-start.22 = (bf16[24,2304]{1,0:T(8,128)(2,1)S(1)}, bf16[24,2304]{1,0:T(8,128)(2,1)}, u32[]{:S(2)}) copy-start(bf16[24,2304]{1,0:T(8,128)(2,1)} %param.21) | copy-start | bytes 331780
  7.2 5.4 %copy-start.27 = (bf16[24]{0:T(256)(128)(2,1)S(1)}, bf16[24]{0:T(256)(128)(2,1)}, u32[]{:S(2)}) copy-start(bf16[24]{0:T(256)(128)(2,1)} %param.22) | copy-start | bytes 148
  7.2 5.4 %copy-start.28 = (bf16[24]{0:T(256)(128)(2,1)S(1)}, bf16[24]{0:T(256)(128)(2,1)}, u32[]{:S(2)}) copy-start(bf16[24]{0:T(256)(128)(2,1)} %param.23) | copy-start | bytes 148
  7.2 5.4 %copy-start.29 = (bf16[24]{0:T(256)(128)(2,1)S(1)}, bf16[24]{0:T(256)(128)(2,1)}, u32[]{:S(2)}) copy-start(bf16[24]{0:T(256)(128)(2,1)} %param.25) | copy-start | bytes 148
  7.3 5.4 %copy-start.30 = (bf16[24]{0:T(256)(128)(2,1)S(1)}, bf16[24]{0:T(256)(128)(2,1)}, u32[]{:S(2)}) copy-start(bf16[24]{0:T(256)(128)(2,1)} %param.26) | copy-start | bytes 148
  7.3 5.4 %copy-start.31 = (bf16[24]{0:T(256)(128)(2,1)S(1)}, bf16[24]{0:T(256)(128)(2,1)}, u32[]{:S(2)}) copy-start(bf16[24]{0:T(256)(128)(2,1)} %param.27) | copy-start | bytes 148
  7.3 5.4 %copy-start.35 = (bf16[96]{0:T(256)(128)(2,1)S(1)}, bf16[96]{0:T(256)(128)(2,1)}, u32[]{:S(2)}) copy-start(bf16[96]{0:T(256)(128)(2,1)} %param.29) | copy-start | bytes 580
  7.3 5.4 %copy-start.32 = (bf16[24]{0:T(256)(128)(2,1)S(1)}, bf16[24]{0:T(256)(128)(2,1)}, u32[]{:S(2)}) copy-start(bf16[24]{0:T(256)(128)(2,1)} %param.31) | copy-start | bytes 148
  7.3 5.4 %copy-start.33 = (bf16[24]{0:T(256)(128)(2,1)S(1)}, bf16[24]{0:T(256)(128)(2,1)}, u32[]{:S(2)}) copy-start(bf16[24]{0:T(256)(128)(2,1)} %param.32) | copy-start | bytes 148
  7.3 5.4 %copy-start.34 = (bf16[24]{0:T(256)(128)(2,1)S(1)}, bf16[24]{0:T(256)(128)(2,1)}, u32[]{:S(2)}) copy-start(bf16[24]{0:T(256)(128)(2,1)} %param.33) | copy-start | bytes 148
  7.3 153.7 %all-gather.2.cloned.1.call-start = ((), (), s32[]{:S(2)}) async-start(), calls=%async_computation.1 | async-start | bytes 10948608 | tf_op jit(solution)/shard_map/all_gather | solution.py:956
  11.9 355.0 %reduce-scatter.2.cloned.1.call-start = ((), (), s32[]{:S(2)}) async-start(), calls=%async_computation.2 | async-start | bytes 10948608 | tf_op jit(solution)/shard_map/reduce_scatter | solution.py:994
  190.8 23.4 %copy-start.7 = (f32[3,2048]{1,0:T(4,128)S(1)}, f32[3,2048]{1,0:T(4,128)}, u32[]{:S(2)}) copy-start(f32[3,2048]{1,0:T(4,128)} %copy-done.6) | copy-start | bytes 73732
  208.9 49.8 %collective-permute-start = (bf16[192,2048]{1,0:T(8,128)(2,1)}, bf16[192,2048]{1,0:T(8,128)(2,1)S(1)}, u32[]{:S(2)}, u32[]{:S(2)}) collective-permute-start(bf16[192,2048]{1,0:T(8,128)(2,1)} %get-tuple-element.65.do_ref), channel_id=1, source_target_pairs={{0,4},{4,8},{8,12},{12,16},{16,20},{20,24},{24,28},{1,5},{5,9},{9,... | collective-permute-start | bytes 2359304 | tf_op jit(solution)/shard_map/ppermute | solution.py:928
  212.9 45.8 %collective-permute-start.1 = (bf16[192,2048]{1,0:T(8,128)(2,1)}, bf16[192,2048]{1,0:T(8,128)(2,1)S(1)}, u32[]{:S(2)}, u32[]{:S(2)}) collective-permute-start(bf16[192,2048]{1,0:T(8,128)(2,1)} %get-tuple-element.65.do_ref), channel_id=1, source_target_pairs={{4,0},{8,4},{12,8},{16,12},{20,16},{24,20},{28,24},{5,1},{9,5},{13... | collective-permute-start | bytes 2359304 | tf_op jit(solution)/shard_map/ppermute | solution.py:928
  216.2 41.0 %copy-start.26 = (f32[1,3072]{1,0:T(1,128)S(1)}, f32[1,3072]{1,0:T(1,128)}, u32[]{:S(2)}) copy-start(f32[1,3072]{1,0:T(1,128)} %get-tuple-element.80) | copy-start | bytes 36868
  216.2 41.9 %copy-start.25 = (f32[8,768]{1,0:T(8,128)S(1)}, f32[8,768]{1,0:T(8,128)}, u32[]{:S(2)}) copy-start(f32[8,768]{1,0:T(8,128)} %get-tuple-element.79) | copy-start | bytes 73732
  216.2 42.5 %copy-start.11 = (f32[3,2048]{1,0:T(4,128)S(1)}, f32[3,2048]{1,0:T(4,128)}, u32[]{:S(2)}) copy-start(f32[3,2048]{1,0:T(4,128)} %get-tuple-element.66.lse_lo_ref) | copy-start | bytes 73732
  216.2 42.5 %copy-start.12 = (f32[3,2048]{1,0:T(4,128)S(1)}, f32[3,2048]{1,0:T(4,128)}, u32[]{:S(2)}) copy-start(f32[3,2048]{1,0:T(4,128)} %get-tuple-element.67.lse_hi_ref) | copy-start | bytes 73732
  216.2 42.5 %copy-start.13 = (f32[4,3,512]{2,1,0:T(4,128)S(1)}, f32[4,3,512]{2,1,0:T(4,128)}, u32[]{:S(2)}) copy-start(f32[4,3,512]{2,1,0:T(4,128)} %get-tuple-element.68) | copy-start | bytes 73732
  216.2 42.5 %copy-start.14 = (f32[4,3,512]{2,1,0:T(4,128)S(1)}, f32[4,3,512]{2,1,0:T(4,128)}, u32[]{:S(2)}) copy-start(f32[4,3,512]{2,1,0:T(4,128)} %get-tuple-element.69) | copy-start | bytes 73732
  258.7 12.3 %copy-start.19 = (bf16[576,768]{1,0:T(8,128)(2,1)S(1)}, bf16[576,768]{1,0:T(8,128)(2,1)}, u32[]{:S(2)}) copy-start(bf16[576,768]{1,0:T(8,128)(2,1)} %copy-done.18) | copy-start | bytes 2654212
  369.0 8.7 %copy-start.4 = (bf16[512,768]{1,0:T(8,128)(2,1)S(1)}, bf16[512,768]{1,0:T(8,128)(2,1)}, u32[]{:S(2)}) copy-start(bf16[512,768]{1,0:T(8,128)(2,1)} %copy-done.3) | copy-start | bytes 2359300
  (16 other events, 29.6 us)
Sparse Core Ops, SparseCore 0:
  12.0 117.2 all-gather.1
  191.0 161.2 reduce-scatter.1
where the time goes:
time: 380 us; the launch traced here: 385 us
  Pallas kernels  315 us (83%)
  local copies, waits for them, and re-layouts  47.2 us (12%)
  between operations  14.9 us (4%)
  starting transfers between devices  5.38 us (1%)
    pallas_call x1, Pallas kernels, finish(): pl.pallas_call(functools.partial(finish_body, n_blk, n_head), out_shape=(...  76.4 us
    pallas_call x1, Pallas kernels, collect(): pl.pallas_call(functools.partial(collect_body, n_blk, n_head, chunks), ou...  59.4 us
    pallas_call x1, Pallas kernels, own_grads(): pl.pallas_call(functools.partial(own_grads_body, groups=groups, rows=rows...  39.6 us
    pallas_call x1, Pallas kernels, to_tokens(): pl.pallas_call(functools.partial(to_tokens_body, n_blk, n_head), out_shap...  38.9 us
    pallas_call x1, Pallas kernels, dense(): pl.pallas_call(functools.partial(dense_body, blocks=blocks), out_shape=(j...  29.8 us
    pallas_call x1, Pallas kernels, attend(): pl.pallas_call(functools.partial(attend_body, groups=groups, rows=rows, t...  26 us
    unnamed x76, local copies, waits for them, and re-layouts  22.9 us
    pallas_call x1, Pallas kernels, to_heads(): pl.pallas_call(functools.partial(to_heads_body, n_blk, n_head), out_shape...  18 us
  transfers between devices with their start and end apart: 4, of which 0 were waited for; matrix products, arithmetic and copies ran while one was open for 3% of the time, Pallas kernels for 74%

commit v1 on v0

--- a/solution.py
+++ b/solution.py
@@ -34,6 +34,10 @@
     return lax.dot_general(a, b, (((1,), (1,)), ((), ())), preferred_element_type=F32)
 
 
+def feature_rows(n):
+    return slice(n * HEAD_DIM, (n + 1) * HEAD_DIM)
+
+
 def column(row):
     return jnp.broadcast_to(row, (8, row.shape[1])).T[:, :1]
 
@@ -42,22 +46,65 @@
     return column(seg_ref[:, keys]) == seg_ref[:, queries]
 
 
-def attend_body(lo_ref, hi_ref, qkv_ref, seg_ref, out_ref, lse_ref, *, groups, rows, tile):
+def project_window(first, last, per, got_ref, x_hbm, qkv_ref, qkv_hbm, turned_ref, w_ref, x_buf, x_sem, out_sem, tile):
+    def fetch(j):
+        slot = lax.rem(j, 2)
+        at = pl.ds(pl.multiple_of(j * tile, tile), tile)
+        return pltpu.make_async_copy(x_hbm.at[at], x_buf.at[slot], x_sem.at[slot])
+
+    fetch(first).start()
+    for n in range(got_ref.shape[0]):
+        w_ref[n * per : (n + 1) * per] = got_ref[n, :per].astype(F32)
+    turned_ref[...] = w_ref[...].T.astype(BF16)
+    bias = column(jnp.sum(got_ref[:, per + 1 : per + 2].astype(F32), axis=0))
+
+    def keep(j):
+        at = pl.ds(pl.multiple_of(j * tile, tile), tile)
+        return pltpu.make_async_copy(qkv_ref.at[:, at], qkv_hbm.at[:, at], out_sem.at[j])
+
+    def one(j, c):
+        @pl.when(j + 1 < last)
+        def _():
+            fetch(j + 1).start()
+
+        fetch(j).wait()
+        at = pl.ds(pl.multiple_of(j * tile, tile), tile)
+        qkv_ref[:, at] = (mm_nt(turned_ref[...], x_buf[lax.rem(j, 2)]) + bias).astype(BF16)
+        keep(j).start()
+        return c
+
+    def done(j, c):
+        keep(j).wait()
+        return c
+
+    lax.fori_loop(first, last, one, 0)
+    return lambda: lax.fori_loop(first, last, done, 0)
+
+
+def attend_body(
+    lo_ref, hi_ref, seg_ref, got_ref, x_hbm, out_ref, lse_ref, turned_ref, qkv_hbm, qkv_ref, w_ref, x_buf, x_sem, out_sem, *,
+    groups, rows, tile, per
+):
+    count = rows // tile
+    wait_kept = project_window(
+        lo_ref[0], hi_ref[count - 1], per, got_ref, x_hbm, qkv_ref, qkv_hbm, turned_ref, w_ref, x_buf, x_sem, out_sem, tile
+    )
+
     def one_query(i, mild):
         at = pl.ds(pl.multiple_of(i * tile, tile), tile)
         win = pl.ds(pl.multiple_of(rows + i * tile, tile), tile)
-        queries = [qkv_ref[h, :, win] * BF16(SCALE) for h in range(groups)]
+        queries = [qkv_ref[feature_rows(h), win] * BF16(SCALE) for h in range(groups)]
 
         def one_key(j, state):
             keys = pl.ds(pl.multiple_of(j * tile, tile), tile)
             same = same_document(seg_ref, keys, win)
             new = []
-            ahead = mm_tn(qkv_ref[groups, :, keys], queries[0])
+            ahead = mm_tn(qkv_ref[feature_rows(groups), keys], queries[0])
             for h in range(groups):
                 scores = jnp.where(same, ahead, NEG)
                 if h + 1 < groups:
-                    ahead = mm_tn(qkv_ref[groups + h + 1, :, keys], queries[h + 1])
-                value = qkv_ref[2 * groups + h, :, keys]
+                    ahead = mm_tn(qkv_ref[feature_rows(groups + h + 1), keys], queries[h + 1])
+                value = qkv_ref[feature_rows(2 * groups + h), keys]
                 top, total, acc = state[h]
                 if mild:
                     weights = jnp.exp(scores)
@@ -84,37 +131,49 @@
         def grow(j, best):
             at = pl.ds(pl.multiple_of(j * tile, tile), tile)
             for h in range(groups):
-                values = qkv_ref[part * groups + h, :, at].astype(F32)
+                values = qkv_ref[feature_rows(part * groups + h), at].astype(F32)
                 best = jnp.maximum(best, jnp.sum(values * values, axis=0, keepdims=True))
             return best
 
         return jnp.max(lax.fori_loop(first, last, grow, jnp.zeros((1, tile), F32)))
 
-    count = rows // tile
     reach = longest(0, count, 2 * count) * longest(1, lo_ref[0], hi_ref[count - 1])
     is_mild = reach <= (MILD / SCALE) ** 2
     for mild in (True, False):
 
         @pl.when(is_mild == mild)
         def _():
-            @pl.loop(0, rows // tile)
+            @pl.loop(0, count)
             def _(i):
                 one_query(i, mild)
 
-
-def attend(qkv, seg, lo, hi, groups, rows, tile):
+    wait_kept()
+
+
+def attend(x_win, got, seg, lo, hi, groups, rows, tile, per):
+    width = x_win.shape[1]
+    wide = got.shape[2]
     return pl.pallas_call(
-        functools.partial(attend_body, groups=groups, rows=rows, tile=tile),
+        functools.partial(attend_body, groups=groups, rows=rows, tile=tile, per=per),
         out_shape=(
             jax.ShapeDtypeStruct((rows // tile, groups * HEAD_DIM, tile), BF16),
             jax.ShapeDtypeStruct((groups, rows), F32),
+            jax.ShapeDtypeStruct((wide, width), BF16),
+            jax.ShapeDtypeStruct((wide, 3 * rows), BF16),
         ),
-        in_specs=[SMEM, SMEM, VMEM, VMEM],
-        out_specs=(VMEM, VMEM),
+        in_specs=[SMEM, SMEM, VMEM, VMEM, ANY],
+        out_specs=(VMEM, VMEM, VMEM, ANY),
+        scratch_shapes=[
+            pltpu.VMEM((wide, 3 * rows), BF16),
+            pltpu.VMEM((width, wide), F32),
+            pltpu.VMEM((2, tile, width), BF16),
+            pltpu.SemaphoreType.DMA((2,)),
+            pltpu.SemaphoreType.DMA((3 * rows // tile,)),
+        ],
         compiler_params=pltpu.CompilerParams(vmem_limit_bytes=48 << 20),
-        cost_estimate=pl.CostEstimate(flops=30_000_000_000, bytes_accessed=12_000_000, transcendentals=15_000_000),
+        cost_estimate=pl.CostEstimate(flops=36_000_000_000, bytes_accessed=24_000_000, transcendentals=15_000_000),
         name="attend",
-    )(lo, hi, qkv, seg)
+    )(lo, hi, seg, got, x_win)
 
 
 def own_grads_body(
@@ -135,8 +194,8 @@
             same = same_document(seg_ref, keys, win)
 
             def products(h):
-                query = qkv_ref[h, :, win] * BF16(SCALE)
-                return query, mm_tn(qkv_ref[groups + h, :, keys], query), mm_tn(qkv_ref[2 * groups + h, :, keys], do_ref[h * HEAD_DIM : (h + 1) * HEAD_DIM, at])
+                query = qkv_ref[feature_rows(h), win] * BF16(SCALE)
+                return query, mm_tn(qkv_ref[feature_rows(groups + h), keys], query), mm_tn(qkv_ref[feature_rows(2 * groups + h), keys], do_ref[feature_rows(h), at])
 
             ahead = products(0)
             for h in range(groups):
@@ -145,9 +204,9 @@
                     ahead = products(h + 1)
                 weights = jnp.exp(jnp.where(same, scores - lse_ref[h : h + 1, at], NEG))
                 d_scores = (weights * (d_weights - delta_ref[h : h + 1, at])).astype(BF16)
-                acc_ref[h] += mm(qkv_ref[groups + h, :, keys], d_scores)
+                acc_ref[h] += mm(qkv_ref[feature_rows(groups + h), keys], d_scores)
                 if own:
-                    dv_ref[h, mine, :] += mm_nt(weights.astype(BF16), do_ref[h * HEAD_DIM : (h + 1) * HEAD_DIM, at])
+                    dv_ref[h, mine, :] += mm_nt(weights.astype(BF16), do_ref[feature_rows(h), at])
                     dk_ref[h, mine, :] += mm_nt(d_scores, query)
 
         def inside(j, c):
@@ -186,11 +245,14 @@
 
 
 def outer_grads_body(
-    lo_ref, hi_ref, qkv_ref, do_lo_ref, do_hi_ref, lse_lo_ref, lse_hi_ref, delta_lo_ref, delta_hi_ref, seg_ref, dq_ref, dk_ref, dv_ref, out_ref, dk_acc,
-    dv_acc, *, groups, rows, tile
+    lo_ref, hi_ref, qkv_ref, do_lo_ref, do_hi_ref, lse_lo_ref, lse_hi_ref, delta_lo_ref, delta_hi_ref, seg_ref, dq_ref, dk_ref,
+    dv_ref, turned_ref, x_hbm, dw_ref, part_ref, sum_ref, out_ref, dk_acc, dv_acc, dw_acc, x_buf, x_sem, *, groups, rows, tile
 ):
+    fetch = pltpu.make_async_copy(x_hbm.at[pl.ds(rows, rows)], x_buf, x_sem)
+    fetch.start()
     count = rows // tile
-    out_ref[:groups] = dq_ref[...]
+    for h in range(groups):
+        out_ref[feature_rows(h)] = dq_ref[h]
 
     def one_key(j, _):
         mine = pl.ds(pl.multiple_of(j * tile, tile), tile)
@@ -204,8 +266,8 @@
             same = same_document(seg_ref, keys, win)
 
             def products(h):
-                query = qkv_ref[h, :, win] * BF16(SCALE)
-                return query, mm_tn(qkv_ref[groups + h, :, keys], query), mm_tn(qkv_ref[2 * groups + h, :, keys], do_ref[h * HEAD_DIM : (h + 1) * HEAD_DIM, at])
+                query = qkv_ref[feature_rows(h), win] * BF16(SCALE)
+                return query, mm_tn(qkv_ref[feature_rows(groups + h), keys], query), mm_tn(qkv_ref[feature_rows(2 * groups + h), keys], do_ref[feature_rows(h), at])
 
             ahead = products(0)
             for h in range(groups):
@@ -214,7 +276,7 @@
                     ahead = products(h + 1)
                 weights = jnp.exp(jnp.where(same, scores - lse_ref[h : h + 1, at], NEG))
                 d_scores = (weights * (d_weights - delta_ref[h : h + 1, at])).astype(BF16)
-                dv_acc[h] += mm_nt(weights.astype(BF16), do_ref[h * HEAD_DIM : (h + 1) * HEAD_DIM, at])
+                dv_acc[h] += mm_nt(weights.astype(BF16), do_ref[feature_rows(h), at])
                 dk_acc[h] += mm_nt(d_scores, query)
 
         def before(i, c):
@@ -229,24 +291,52 @@
         lax.fori_loop(lo, jnp.minimum(hi, count), before, 0)
         lax.fori_loop(jnp.maximum(lo, 2 * count), hi, after, 0)
         for h in range(groups):
-            out_ref[groups + h, :, mine] = dk_acc[h].T.astype(BF16)
-            out_ref[2 * groups + h, :, mine] = dv_acc[h].T.astype(BF16)
+            out_ref[feature_rows(groups + h), mine] = dk_acc[h].T.astype(BF16)
+            out_ref[feature_rows(2 * groups + h), mine] = dv_acc[h].T.astype(BF16)
         return 0
 
     lax.fori_loop(0, count, one_key, 0)
-
-
-def outer_grads(qkv, do_lo, do_hi, lse_lo, lse_hi, delta_lo, delta_hi, seg, dq, dk, dv, lo, hi, groups, rows, tile):
+    fetch.wait()
+    dw_acc[...] = jnp.zeros_like(dw_acc)
+    sum_ref[...] = jnp.zeros_like(sum_ref)
+
+    def back(j, _):
+        mine = pl.ds(pl.multiple_of(j * tile, tile), tile)
+        d = out_ref[:, mine]
+        part_ref[mine, :] = mm_tn(d, turned_ref[...]).astype(BF16)
+        dw_acc[...] += mm(d, x_buf[mine, :])
+        sum_ref[...] += jnp.sum(d.astype(F32), axis=1, keepdims=True)
+        return 0
+
+    lax.fori_loop(0, count, back, 0)
+    dw_ref[...] = dw_acc[...].T.astype(BF16)
+
+
+def outer_grads(
+    qkv, do_lo, do_hi, lse_lo, lse_hi, delta_lo, delta_hi, seg, dq, dk, dv, turned, x_win, lo, hi, groups, rows, tile
+):
+    wide, width = turned.shape
     return pl.pallas_call(
         functools.partial(outer_grads_body, groups=groups, rows=rows, tile=tile),
-        out_shape=jax.ShapeDtypeStruct((3 * groups, HEAD_DIM, rows), BF16),
-        in_specs=[SMEM, SMEM] + [VMEM] * 11,
-        out_specs=VMEM,
-        scratch_shapes=[pltpu.VMEM((groups, tile, HEAD_DIM), F32)] * 2,
-        compiler_params=pltpu.CompilerParams(vmem_limit_bytes=52 << 20),
-        cost_estimate=pl.CostEstimate(flops=20_000_000_000, bytes_accessed=20_000_000, transcendentals=5_000_000),
+        out_shape=(
+            jax.ShapeDtypeStruct((width, wide), BF16),
+            jax.ShapeDtypeStruct((rows, width), BF16),
+            jax.ShapeDtypeStruct((wide, 1), F32),
+        ),
+        in_specs=[SMEM, SMEM] + [VMEM] * 12 + [ANY],
+        out_specs=(VMEM,) * 3,
+        scratch_shapes=[
+            pltpu.VMEM((wide, rows), BF16),
+            pltpu.VMEM((groups, tile, HEAD_DIM), F32),
+            pltpu.VMEM((groups, tile, HEAD_DIM), F32),
+            pltpu.VMEM((wide, width), F32),
+            pltpu.VMEM((rows, width), BF16),
+            pltpu.SemaphoreType.DMA,
+        ],
+        compiler_params=pltpu.CompilerParams(vmem_limit_bytes=54 << 20),
+        cost_estimate=pl.CostEstimate(flops=24_000_000_000, bytes_accessed=24_000_000, transcendentals=5_000_000),
         name="outer_grads",
-    )(lo, hi, qkv, do_lo, do_hi, lse_lo, lse_hi, delta_lo, delta_hi, seg, dq, dk, dv)
+    )(lo, hi, qkv, do_lo, do_hi, lse_lo, lse_hi, delta_lo, delta_hi, seg, dq, dk, dv, turned, x_win)
 
 
 def place():
@@ -479,10 +569,12 @@
     wait_w2()
     wait_t2()
     dt_ref[...] = jnp.sum(t_end[...], axis=0)
-    parts, cut = dw_ref.shape[0], dw_ref.shape[2] // n_head
+    parts = 3
+    cut = dw_ref.shape[1] // (parts * n_head)
     for h in range(n_head):
         for p in range(parts):
-            dw_ref[p, :, h * cut : (h + 1) * cut] = w_end[h, :, p * cut : (p + 1) * cut]
+            first = (p * n_head + h) * cut
+            dw_ref[:, first : first + cut] = w_end[h, :, p * cut : (p + 1) * cut]
     for_row.wait()
     out_ref[...] = (
         first_ref[...] + part_ref[head].astype(F32) + near[0].astype(F32) + far_in[...].astype(F32)
@@ -496,7 +588,7 @@
         functools.partial(finish_body, n_blk, n_head),
         out_shape=(
             jax.ShapeDtypeStruct((rows, width), BF16),
-            jax.ShapeDtypeStruct((3, per, width), F32),
+            jax.ShapeDtypeStruct((per, 3 * width), F32),
             jax.ShapeDtypeStruct(table.shape[2:], F32),
         ),
         in_specs=[VMEM] * 4,
@@ -681,83 +773,114 @@
     )(d_seq, d_part)
 
 
-def project_body(x_ref, w_ref, bias_ref, out_ref, turned_ref):
-    @pl.when(pl.program_id(0) == 0)
-    def _():
-        turned_ref[...] = w_ref[...].T
-
-    out_ref[...] = (mm_nt(turned_ref[...], x_ref[...]) + bias_ref[...]).astype(BF16)
-
-
-def project(x, w, bias, tile):
-    rows, width = x.shape
-    wide = w.shape[1]
-    whole = lambda i: (0, 0)
+def regroup(values, outer, inner, unit):
+    if unit % 8:
+        return values.reshape(-1, outer, inner, unit).transpose(0, 2, 1, 3).reshape(values.shape)
+    at = lambda o, i: slice((o * inner + i) * unit, (o * inner + i + 1) * unit)
+    return jnp.concatenate([values[:, at(o, i)] for i in range(inner) for o in range(outer)], axis=1)
+
+
+def pack_body(*refs, count, blocks, n_head):
+    (in_ref, mid_ref, down_ref, qkv_ref), vectors, (packed_ref, send_ref) = refs[:4], refs[4:-2], refs[-2:]
+    unit, width = mid_ref.shape
+    ff = blocks * width
+    packed_ref[:, :ff] = regroup(in_ref[...].astype(F32), count, blocks, unit).astype(BF16)
+    packed_ref[:, ff : ff + width] = mid_ref[...]
+    for n in range(blocks):
+        packed_ref[:, ff + width * (n + 1) : ff + width * (n + 2)] = down_ref[n * unit : (n + 1) * unit]
+
+    cut = width // n_head
+    vectors = [ref[...].astype(F32) for ref in vectors]
+    joined = jnp.concatenate(vectors, axis=1)
+    wide = 3 * cut
+    pieces = jnp.concatenate([joined, jnp.zeros((1, wide - joined.shape[1]), F32)], axis=1)
+    blk, head = place()
+    me = blk * n_head + head
+    spots = cut // unit
+
+    def in_place(vec):
+        return jnp.concatenate([jnp.where(lax.rem(me, spots) == n, vec, 0.0) for n in range(spots)], axis=1)
+
+    placed = jnp.concatenate([in_place(vectors[0]), jnp.zeros((1, cut), F32), in_place(vectors[1])], axis=1)
+    weights = qkv_ref[...].astype(F32)
+    rest = jnp.zeros((BIAS_ROWS - 2, wide), F32)
+    for h in range(n_head):
+        columns = jnp.concatenate([weights[:, p * width + h * cut : p * width + (h + 1) * cut] for p in range(3)], axis=1)
+        mine = jnp.where(me // spots == h, placed, 0.0)
+        send_ref[h] = jnp.concatenate([columns, pieces, mine, rest], axis=0).astype(BF16)
+
+
+def pack(w_in, w_out, w_down, w_qkv, vectors, count, n_head):
+    unit, width = w_out.shape
+    blocks = w_down.shape[0] // unit
+    cut = width // n_head
+    if unit % 8:
+        down = w_down.reshape(blocks, unit, width).transpose(1, 0, 2).reshape(unit, -1)
+        joined = jnp.concatenate(vectors)
+        blk, head = place()
+        me = blk * n_head + head
+        spots = cut // unit
+        zeros = jnp.zeros((cut,), BF16)
+        at = lax.rem(me, spots) * unit
+        placed = jnp.concatenate(
+            [
+                lax.dynamic_update_slice_in_dim(zeros, vectors[0], at, 0),
+                zeros,
+                lax.dynamic_update_slice_in_dim(zeros, vectors[1], at, 0),
+            ]
+        )
+        owner = (jnp.arange(n_head) == me // spots)[:, None]
+        rows = jnp.stack(
+            [
+                jnp.broadcast_to(jnp.pad(joined, (0, 3 * cut - joined.shape[0]))[None], (n_head, 3 * cut)),
+                jnp.where(owner, placed[None], jnp.zeros((), BF16)),
+            ]
+            + [jnp.zeros((n_head, 3 * cut), BF16)] * (BIAS_ROWS - 2),
+            axis=1,
+        )
+        columns = w_qkv.reshape(unit, 3, n_head, cut).transpose(2, 0, 1, 3).reshape(n_head, unit, 3 * cut)
+        packed = jnp.concatenate([regroup(w_in, count, blocks, unit), w_out, down], axis=1)
+        return packed, jnp.concatenate([columns, rows], axis=1)
     return pl.pallas_call(
-        project_body,
-        grid=(rows // tile,),
-        out_shape=(jax.ShapeDtypeStruct((wide, rows), BF16), jax.ShapeDtypeStruct((wide, width), BF16)),
-        in_specs=[
-            pl.BlockSpec((tile, width), lambda i: (i, 0)),
-            pl.BlockSpec((width, wide), whole),
-            pl.BlockSpec((wide, 1), whole),
-        ],
-        out_specs=(pl.BlockSpec((wide, tile), lambda i: (0, i)), pl.BlockSpec((wide, width), whole)),
-        compiler_params=pltpu.CompilerParams(vmem_limit_bytes=32 << 20),
-        cost_estimate=pl.CostEstimate(flops=2 * rows * width * wide, bytes_accessed=20_000_000, transcendentals=0),
-        name="project",
-    )(x, w, bias)
-
-
-def project_back_body(d_ref, x_ref, turned_ref, dw_ref, part_ref, sum_ref, acc_ref):
-    step = pl.program_id(0)
-    d = d_ref[...]
-    part_ref[...] = mm_tn(d, turned_ref[...]).astype(BF16)
-    product = mm(d, x_ref[...])
-    total = jnp.sum(d.astype(F32), axis=1, keepdims=True)
-
-    @pl.when(step == 0)
-    def _():
-        acc_ref[...] = product
-        sum_ref[...] = total
-
-    @pl.when(step > 0)
-    def _():
-        acc_ref[...] += product
-        sum_ref[...] += total
-
-    @pl.when(step == pl.num_programs(0) - 1)
-    def _():
-        dw_ref[...] = acc_ref[...].T.astype(BF16)
-
-
-def project_back(d_qkv, x_win, turned, tile):
-    wide, rows = d_qkv.shape
-    width = x_win.shape[1]
-    whole = lambda i: (0, 0)
+        functools.partial(pack_body, count=count, blocks=blocks, n_head=n_head),
+        out_shape=(
+            jax.ShapeDtypeStruct((unit, 2 * w_in.shape[1] + width), BF16),
+            jax.ShapeDtypeStruct((n_head, unit + BIAS_ROWS, 3 * cut), BF16),
+        ),
+        in_specs=[VMEM] * (4 + len(vectors)),
+        out_specs=(VMEM, VMEM),
+        name="pack",
+    )(w_in, w_out, w_down, w_qkv, *(vec[None] for vec in vectors))
+
+
+def unpack_body(packed_ref, in_ref, mid_ref, down_ref, *, count, blocks):
+    unit, width = mid_ref.shape
+    ff = blocks * width
+    in_ref[...] = regroup(packed_ref[:, :ff].astype(F32), blocks, count, unit)
+    mid_ref[...] = packed_ref[:, ff : ff + width].astype(F32)
+    for n in range(blocks):
+        down_ref[n * unit : (n + 1) * unit] = packed_ref[:, ff + width * (n + 1) : ff + width * (n + 2)].astype(F32)
+
+
+def unpack(packed, width, count):
+    unit = packed.shape[0]
+    blocks = (packed.shape[1] // width - 1) // 2
+    ff = blocks * width
+    if unit % 8:
+        packed = packed.astype(F32)
+        down = packed[:, ff + width :].reshape(unit, blocks, width).transpose(1, 0, 2).reshape(-1, width)
+        return regroup(packed[:, :ff], blocks, count, unit), packed[:, ff : ff + width], down
     return pl.pallas_call(
-        project_back_body,
-        grid=(rows // tile,),
+        functools.partial(unpack_body, count=count, blocks=blocks),
         out_shape=(
-            jax.ShapeDtypeStruct((width, wide), BF16),
-            jax.ShapeDtypeStruct((rows, width), BF16),
-            jax.ShapeDtypeStruct((wide, 1), F32),
+            jax.ShapeDtypeStruct((unit, ff), F32),
+            jax.ShapeDtypeStruct((unit, width), F32),
+            jax.ShapeDtypeStruct((unit * blocks, width), F32),
         ),
-        in_specs=[
-            pl.BlockSpec((wide, tile), lambda i: (0, i)),
-            pl.BlockSpec((tile, width), lambda i: (rows // tile + i, 0)),
-            pl.BlockSpec((wide, width), whole),
-        ],
-        out_specs=(
-            pl.BlockSpec((width, wide), whole),
-            pl.BlockSpec((tile, width), lambda i: (i, 0)),
-            pl.BlockSpec((wide, 1), whole),
-        ),
-        scratch_shapes=[pltpu.VMEM((wide, width), F32)],
-        compiler_params=pltpu.CompilerParams(vmem_limit_bytes=32 << 20),
-        cost_estimate=pl.CostEstimate(flops=4 * rows * width * wide, bytes_accessed=12_000_000, transcendentals=0),
-        name="project_back",
-    )(d_qkv, x_win, turned)
+        in_specs=[VMEM],
+        out_specs=(VMEM,) * 3,
+        name="unpack",
+    )(packed)
 
 
 def normalize(values):
@@ -942,64 +1065,42 @@
     blocks = ff // width
     cut = width // n_head
     groups = cut // HEAD_DIM
-    down_per = w_down.shape[0]
-
-    unit = down_per // blocks
-
-    def reorder(values):
-        return values.reshape(-1, count, blocks, unit).transpose(0, 2, 1, 3).reshape(values.shape)
-
-    def restore(values):
-        return values.reshape(-1, blocks, count, unit).transpose(0, 2, 1, 3).reshape(values.shape)
-
-    down = w_down.reshape(blocks, unit, width).transpose(1, 0, 2).reshape(unit, ff)
-    whole = lax.all_gather(jnp.concatenate([reorder(w_in), w_out, down], axis=1), BOTH, axis=0, tiled=True)
 
     small = (q_bias, v_bias, out_bias, ln1_gain, ln1_bias, down_bias, ln2_gain, ln2_bias, in_bias)
-    bias_row = jnp.concatenate(small)
-    small_cols = 3 * cut
-    bias_pad = jnp.zeros((BIAS_ROWS, small_cols), BF16).at[0, : bias_row.shape[0]].set(bias_row)
-    columns = w_qkv.reshape(per, 3, n_head, cut).transpose(2, 0, 1, 3).reshape(n_head, per, 3 * cut)
-    to_send = jnp.concatenate([columns, jnp.broadcast_to(bias_pad[None], (n_head, BIAS_ROWS, small_cols))], axis=1)
+    packed, to_send = pack(w_in, w_out, w_down, w_qkv, small, count, n_head)
+    whole = lax.all_gather(packed, BOTH, axis=0, tiled=True)
+
     x_win, got = collect(inputs, to_send, n_blk, n_head)
     x_win = x_win.reshape(3 * rows, width)
     got = got.reshape(count, *got.shape[2:])
-    w_mine = got[:, :per].reshape(width, 3 * cut)
-    all_small = got[:, per, : bias_row.shape[0]].astype(F32)
+    all_small = got[:, per, : sum(vec.shape[0] for vec in small)].astype(F32)
     offsets = [0]
     for vec in small:
         offsets.append(offsets[-1] + vec.shape[0])
-    (f_q_bias, f_v_bias, f_out_bias, f_ln1_gain, f_ln1_bias, f_down_bias, f_ln2_gain, f_ln2_bias, f_in_bias) = (
+    (_, _, f_out_bias, f_ln1_gain, f_ln1_bias, f_down_bias, f_ln2_gain, f_ln2_bias, f_in_bias) = (
         all_small[:, a:b].reshape(-1) for a, b in zip(offsets[:-1], offsets[1:])
     )
-    mine = lambda vec: lax.dynamic_slice_in_dim(vec, head * cut, cut, 0)
-    qkv_bias = jnp.concatenate([mine(f_q_bias), jnp.zeros((cut,), F32), mine(f_v_bias)])
-
-    qkv, turned = project(x_win, w_mine, qkv_bias[:, None], tok)
-    qkv = qkv.reshape(3 * groups, HEAD_DIM, 3 * rows)
     seg, lo, hi = window_of(segments, blk, rows, tok)
-    attended, lse = attend(qkv, seg, lo, hi, groups, rows, tok)
+    attended, lse, turned, qkv = attend(x_win, got, seg, lo, hi, groups, rows, tok, per)
     seq_t, lse_lo, lse_hi = to_tokens(attended, lse, n_blk, n_head)
     seq_t = seq_t.reshape(width, tok)
 
     vectors = jnp.stack([f_out_bias, f_ln1_gain, f_ln1_bias, f_down_bias, f_ln2_gain, f_ln2_bias] + [f_out_bias] * 2)
     outputs, d_first, d_seq_t, d_part, d_vectors, d_in_bias, grads = dense(
-        inputs, seq_t, cotangent, vectors, reorder(f_in_bias)[None], whole, blocks, n_head
+        inputs, seq_t, cotangent, vectors, regroup(f_in_bias[None], count, blocks, per), whole, blocks, n_head
     )
     d_out_bias, d_ln1_gain, d_ln1_bias, d_down_bias, d_ln2_gain, d_ln2_bias = (d_vectors[n] for n in range(6))
-    d_in_bias = restore(d_in_bias[0])
+    d_in_bias = regroup(d_in_bias, blocks, count, per)[0]
     d_out, delta, delta_lo, delta_hi = to_heads(d_seq_t.reshape(n_head, cut, tok), d_part, n_blk, n_head)
     delta, delta_lo, delta_hi = (a.transpose(1, 0, 2).reshape(groups, rows) for a in (delta, delta_lo, delta_hi))
 
-    owned = lax.psum_scatter(grads, BOTH, scatter_dimension=0, tiled=True).astype(F32)
+    owned = lax.psum_scatter(grads, BOTH, scatter_dimension=0, tiled=True)
 
     do_lo, do_hi = shift(d_out, 1), shift(d_out, -1)
     dq, dk, dv = own_grads(qkv, d_out, lse, delta, seg, lo, hi, groups, rows, tok)
-    d_qkv = outer_grads(
-        qkv, do_lo, do_hi, lse_lo, lse_hi, delta_lo, delta_hi, seg, dq, dk, dv, lo, hi, groups, rows, tok
-    ).reshape(3 * cut, rows)
-
-    d_w_qkv, d_part, d_biases = project_back(d_qkv, x_win, turned, tok)
+    d_w_qkv, d_part, d_biases = outer_grads(
+        qkv, do_lo, do_hi, lse_lo, lse_hi, delta_lo, delta_hi, seg, dq, dk, dv, turned, x_win, lo, hi, groups, rows, tok
+    )
     d_biases = d_biases[:, 0]
     place_own = lambda vec: lax.dynamic_update_slice_in_dim(jnp.zeros((width,), F32), vec, head * cut, 0)
     vectors = (
@@ -1010,18 +1111,15 @@
     lanes = 128
     table_rows = -(-table.shape[1] // (8 * lanes)) * 8
     table = jnp.pad(table, ((0, 0), (0, table_rows * lanes - table.shape[1])))
-    d_inputs, w_rows, sums = finish(
+    d_inputs, own_w_qkv, sums = finish(
         d_part.reshape(n_head, tok, width), d_first, d_w_qkv.reshape(n_blk, n_head, per, 3 * cut),
         table.reshape(n_blk, n_head, table_rows, lanes), n_blk, n_head,
     )
-    own_w_qkv = w_rows.transpose(1, 0, 2).reshape(per, 3 * width)
     sums = sums.reshape(-1)
     (o_q_bias, o_v_bias, o_out_bias, o_ln1_gain, o_ln1_bias, o_down_bias, o_ln2_gain, o_ln2_bias, o_in_bias) = (
         sums[a:b] for a, b in zip(offsets[:-1], offsets[1:])
     )
-    own_w_in = restore(owned[:, :ff])
-    own_w_out = owned[:, ff : ff + width]
-    own_w_down = owned[:, ff + width :].reshape(unit, blocks, width).transpose(1, 0, 2).reshape(down_per, width)
+    own_w_in, own_w_out, own_w_down = unpack(owned, width, count)
     return (
         outputs, d_inputs, own_w_qkv, o_q_bias, o_v_bias, own_w_out, o_out_bias, o_ln1_gain, o_ln1_bias,
         own_w_in, o_in_bias, own_w_down, o_down_bias, o_ln2_gain, o_ln2_bias,

time: 380 us -> 364 us (0.958); the launches traced: 385 us -> 362 us
  local copies, waits for them, and re-layouts: 47.2 us -> 20.5 us
    pallas_call x1, Pallas kernels: 12.3 us -> 27.3 us  [outer_grads(): pl.pallas_call(functools.partial(outer_grads_body, groups=groups, rows=ro...]
    pallas_call x1, Pallas kernels: 76.4 us -> 61.6 us  [finish(): pl.pallas_call(functools.partial(finish_body, n_blk, n_head), out_shape=(...]
    pallas_call x2, Pallas kernels: 15 us -> 4.19 us  [the longest x1 2.17 us: pack(): pl.pallas_call(functools.partial(pack_body, count=count, blocks=blocks, n...]
    unnamed x76 -> x41, local copies, waits for them, and re-layouts: 22.9 us -> 12.5 us
    reshape x12 -> x0, local copies, waits for them, and re-layouts: 10 us -> none  [the longest x2 5.1 us: restore(): values.reshape(-1, blocks, count, unit).transpose(0, 2, 1, 3)]
    pallas_call x1, Pallas kernels: 26 us -> 34.8 us  [attend(): pl.pallas_call(functools.partial(attend_body, groups=groups, rows=rows, t...]
    pallas_call x1, Pallas kernels: 38.9 us -> 43.8 us  [to_tokens(): pl.pallas_call(functools.partial(to_tokens_body, n_blk, n_head), out_shap...]
  transfers between devices with their start and end apart: 4 -> 4, of which waited for: 0 -> 0; matrix products, arithmetic and copies ran while one was open for 3% -> 3% of each run, Pallas kernels for 74% -> 79%
where the time goes in v1:
time: 364 us; the launch traced here: 362 us
  Pallas kernels  318 us (87%)
  local copies, waits for them, and re-layouts  20.5 us (6%)
  between operations  14.6 us (4%)
  starting transfers between devices  5.97 us (2%)
    pallas_call x1, Pallas kernels, finish(): pl.pallas_call(functools.partial(finish_body, n_blk, n_head), out_shape=(...  61.6 us
    pallas_call x1, Pallas kernels, collect(): pl.pallas_call(functools.partial(collect_body, n_blk, n_head, chunks), ou...  60.1 us
    pallas_call x1, Pallas kernels, to_tokens(): pl.pallas_call(functools.partial(to_tokens_body, n_blk, n_head), out_shap...  43.8 us
    pallas_call x1, Pallas kernels, own_grads(): pl.pallas_call(functools.partial(own_grads_body, groups=groups, rows=rows...  41 us
    pallas_call x1, Pallas kernels, attend(): pl.pallas_call(functools.partial(attend_body, groups=groups, rows=rows, t...  34.8 us
    pallas_call x1, Pallas kernels, dense(): pl.pallas_call(functools.partial(dense_body, blocks=blocks), out_shape=(j...  29.8 us
    pallas_call x1, Pallas kernels, outer_grads(): pl.pallas_call(functools.partial(outer_grads_body, groups=groups, rows=ro...  27.3 us
    pallas_call x1, Pallas kernels, to_heads(): pl.pallas_call(functools.partial(to_heads_body, n_blk, n_head), out_shape...  16 us
  transfers between devices with their start and end apart: 4, of which 0 were waited for; matrix products, arithmetic and copies ran while one was open for 3% of the time, Pallas kernels for 79%

profile of v1, /device:TPU:0, one launch (start us, length us, event | category | flops | bytes accessed | tf_op | source)
XLA Modules:
  0.0 362.2 jit_solution(349633653926492908)
XLA Ops:
  7.2 2.2 pack.1
  10.4 60.1 %collect.1 = (bf16[3,4,512,768]{3,2,1,0:T(8,128)(2,1)}, bf16[8,4,32,576]{3,2,1,0:T(8,128)(2,1)}) custom-call(bf16[512,768]{1,0:T(8,128)(2,1)} %x_ref.3, bf16[4,32,576]{2,1,0:T(8,128)(2,1)} %get-tuple-element.49.w_ref), custom_call_target="tpu_custom_call" | custom-call | tf_op jit(solution)/shard_map/collect/pallas_call | solution.py:507
  70.5 1.0 slice_convert_fusion
  72.6 1.3 copy-done.7
  73.9 34.8 %attend.1 = (bf16[4,192,512]{2,1,0:T(8,128)(2,1)S(1)}, f32[3,2048]{1,0:T(4,128)S(1)}, bf16[576,768]{1,0:T(8,128)(2,1)S(1)}, bf16[576,6144]{1,0:T(8,128)(2,1)}) custom-call(s32[4]{0:T(128)S(1)} %get-tuple-element.363.lo_ref, s32[4]{0:T(128)S(1)} %get-tuple-element.364.hi_ref, s32[1,6144]{1,0:T(1,128)S(1)} %bitcast.36, bf16[32,32,576]{2,1,0:T(8,128)(2,1)S(1)} %bitcast.42, ...), custom_call_target="tpu_custom_call" | custom-call | flops 35999997952 | bytes 24000000 | tf_op jit(solution)/shard_map/attend/pallas_call | solution.py:156
  108.7 0.9 copy-done.3
  110.2 1.0 copy-done.12
  111.2 43.8 %to_tokens.1 = (bf16[4,192,512]{2,1,0:T(8,128)(2,1)}, f32[3,2048]{1,0:T(4,128)}, f32[3,2048]{1,0:T(4,128)}) custom-call(bf16[4,192,512]{2,1,0:T(8,128)(2,1)} %copy-done.3, f32[3,2048]{1,0:T(4,128)} %copy-done.5), custom_call_target="tpu_custom_call" | custom-call | tf_op jit(solution)/shard_map/to_tokens/pallas_call | solution.py:695
  156.3 0.9 concatenate.13.inb_ref
  157.2 29.8 %dense.1 = (bf16[512,768]{1,0:T(8,128)(2,1)}, f32[512,768]{1,0:T(8,128)}, bf16[768,512]{1,0:T(8,128)(2,1)}, f32[4,3,512]{2,1,0:T(4,128)}, f32[8,768]{1,0:T(8,128...) custom-call(bf16[512,768]{1,0:T(8,128)(2,1)} %x_ref.3, bf16[768,512]{1,0:T(8,128)(2,1)} %bitcast.58, ...), custom_call_target="tpu_custom_call" | custom-call | flops 16999999488 | bytes 30000000 | tf_op jit(solution)/shard_map/dense/pallas_call | solution.py:1004
  187.0 16.0 %to_heads.1 = (bf16[192,2048]{1,0:T(8,128)(2,1)}, f32[4,3,512]{2,1,0:T(4,128)}, f32[4,3,512]{2,1,0:T(4,128)}, f32[4,3,512]{2,1,0:T(4,128)}) custom-call(bf16[4,192,512]{2,1,0:T(8,128)(2,1)} %bitcast.44, f32[4,3,512]{2,1,0:T(4,128)} %get-tuple-element.59.dpart_ref), custom_call_target="tpu_custom_call" | custom-call | tf_op jit(solution)/shard_map/to_heads/pallas_call | solution.py:757
  203.0 1.3 collective-permute-start.1
  204.3 4.6 %collective-permute-start = (bf16[192,2048]{1,0:T(8,128)(2,1)}, bf16[192,2048]{1,0:T(8,128)(2,1)S(1)}, u32[]{:S(2)}, u32[]{:S(2)}) collective-permute-start(bf16[192,2048]{1,0:T(8,128)(2,1)} %get-tuple-element.60.do_ref), channel_id=1, source_target_pairs={{0,4},{4,8},{8,12},{12,16},{16,20},{20,24},{24,28},{1,5},{5,9},{9,... | collective-permute-start | bytes 2359304 | tf_op jit(solution)/shard_map/ppermute | solution.py:1051
  209.3 1.2 copy-done.10
  211.2 41.0 %own_grads.1 = (bf16[3,64,2048]{2,1,0:T(8,128)(2,1)S(1)}, f32[3,2048,64]{2,1,0:T(8,128)}, f32[3,2048,64]{2,1,0:T(8,128)}) custom-call(s32[4]{0:T(128)S(1)} %get-tuple-element.363.lo_ref, s32[4]{0:T(128)S(1)} %get-tuple-element.364.hi_ref, bf16[576,6144]{1,0:T(8,128)(2,1)} %get-tuple-element.57.qkv_ref, bf16[192,2048]{1,0:T(8,128)(2,1)S(1)} %copy-done.10, ...), custom_call_target="tpu_custom_call" | custom-call | flops 60000002048 | bytes 20000000 | tf_op jit(solution)/shard_map/own_grads/pallas_call | solution.py:231
  252.2 0.9 copy-done.13
  255.5 0.9 copy-done.16
  256.6 27.3 %outer_grads.1 = (bf16[768,576]{1,0:T(8,128)(2,1)}, bf16[2048,768]{1,0:T(8,128)(2,1)}, f32[576,1]{1,0:T(8,128)}) custom-call(s32[4]{0:T(128)} %copy-done.8, s32[4]{0:T(128)} %copy-done.9, bf16[576,6144]{1,0:T(8,128)(2,1)} %get-tuple-element.57.qkv_ref, bf16[192,2048]{1,0:T(8,128)(2,1)} %copy-done.17, bf16[192,2048]{1,0:T(8,128)(2,1)} %copy-done.16, ...), custom_call_target="tpu_custom_call" | custom-call | flops 24000000000 | bytes 24000000 | tf_op jit(solution)/shard_map/outer_grads/pallas_call | solution.py:319
  283.9 1.1 slice_reduce_fusion
  285.9 1.9 copy-done
  287.8 1.2 copy-done.2
  289.0 61.6 %finish.1 = (bf16[512,768]{1,0:T(8,128)(2,1)S(1)}, f32[24,2304]{1,0:T(8,128)S(1)}, f32[8,128]{1,0:T(8,128)S(1)}) custom-call(bf16[4,512,768]{2,1,0:T(8,128)(2,1)S(1)} %bitcast.33, f32[512,768]{1,0:T(8,128)S(1)} %copy-done.1, bf16[8,4,24,576]{3,2,1,0:T(8,128)(2,1)S(1)} %bitcast.34, f32[8,4,8,128]{3,2,1,0:T(8,128)S(1)} %bitcast.35), custom_call_target="tpu_custom_call" | custom-call | tf_op jit(solution)/shard_map/finish/pallas_call | solution.py:587
  351.8 2.0 unpack.1
  353.8 0.9 copy.39
  (92 shorter events, 10.3 us)
Async XLA Ops:
  7.2 150.0 %all-gather.2.cloned.1.call-start = ((), (), s32[]{:S(2)}) async-start(), calls=%async_computation.1 | async-start | bytes 10948608 | tf_op jit(solution)/shard_map/all_gather | solution.py:1071
  9.4 342.3 %reduce-scatter.2.cloned.1.call-start = ((), (), s32[]{:S(2)}) async-start(), calls=%async_computation.2 | async-start | bytes 10948608 | tf_op jit(solution)/shard_map/reduce_scatter | solution.py:1097
  10.3 199.0 %copy-start.4 = (s32[6144]{0:T(1024)}, s32[6144]{0:T(1024)S(1)}, u32[]{:S(2)}) copy-start(s32[6144]{0:T(1024)S(1)} %fusion.1) | copy-start | bytes 73732
  72.6 136.7 %copy-start.8 = (s32[4]{0:T(128)}, s32[4]{0:T(128)S(1)}, u32[]{:S(2)}) copy-start(s32[4]{0:T(128)S(1)} %get-tuple-element.363.lo_ref) | copy-start | bytes 52
  72.6 136.7 %copy-start.9 = (s32[4]{0:T(128)}, s32[4]{0:T(128)S(1)}, u32[]{:S(2)}) copy-start(s32[4]{0:T(128)S(1)} %get-tuple-element.364.hi_ref) | copy-start | bytes 52
  72.6 1.3 copy-start.7
  108.7 0.9 copy-start.3
  109.6 0.6 copy-start.5
  110.2 1.0 copy-start.12
  186.9 22.0 %copy-start.14 = (f32[1,3072]{1,0:T(1,128)S(1)}, f32[1,3072]{1,0:T(1,128)}, u32[]{:S(2)}) copy-start(f32[1,3072]{1,0:T(1,128)} %get-tuple-element.75) | copy-start | bytes 36868
  186.9 22.3 %copy-start.6 = (f32[3,2048]{1,0:T(4,128)S(1)}, f32[3,2048]{1,0:T(4,128)}, u32[]{:S(2)}) copy-start(f32[3,2048]{1,0:T(4,128)} %copy-done.5) | copy-start | bytes 73732
  203.0 52.5 %collective-permute-start.1 = (bf16[192,2048]{1,0:T(8,128)(2,1)}, bf16[192,2048]{1,0:T(8,128)(2,1)S(1)}, u32[]{:S(2)}, u32[]{:S(2)}) collective-permute-start(bf16[192,2048]{1,0:T(8,128)(2,1)} %get-tuple-element.60.do_ref), channel_id=1, source_target_pairs={{4,0},{8,4},{12,8},{16,12},{20,16},{24,20},{28,24},{5,1},{9,5},{13... | collective-permute-start | bytes 2359304 | tf_op jit(solution)/shard_map/ppermute | solution.py:1051
  204.3 51.2 %collective-permute-start = (bf16[192,2048]{1,0:T(8,128)(2,1)}, bf16[192,2048]{1,0:T(8,128)(2,1)S(1)}, u32[]{:S(2)}, u32[]{:S(2)}) collective-permute-start(bf16[192,2048]{1,0:T(8,128)(2,1)} %get-tuple-element.60.do_ref), channel_id=1, source_target_pairs={{0,4},{4,8},{8,12},{12,16},{16,20},{20,24},{24,28},{1,5},{5,9},{9,... | collective-permute-start | bytes 2359304 | tf_op jit(solution)/shard_map/ppermute | solution.py:1051
  209.3 1.2 copy-start.10
  210.4 0.8 copy-start.11
  211.2 43.7 %copy-start.15 = (f32[8,768]{1,0:T(8,128)S(1)}, f32[8,768]{1,0:T(8,128)}, u32[]{:S(2)}) copy-start(f32[8,768]{1,0:T(8,128)} %get-tuple-element.74) | copy-start | bytes 73732
  252.2 0.9 copy-start.13
  255.5 0.9 copy-start.16
  255.5 1.1 copy-start.17
  256.6 29.2 %copy-start.1 = (f32[512,768]{1,0:T(8,128)S(1)}, f32[512,768]{1,0:T(8,128)}, u32[]{:S(2)}) copy-start(f32[512,768]{1,0:T(8,128)} %get-tuple-element.71.first_ref) | copy-start | bytes 4718596
  285.9 1.9 copy-start
  287.8 1.2 copy-start.2
Sparse Core Ops, SparseCore 0:
  11.5 114.1 all-gather.1
  187.1 151.6 reduce-scatter.1

commit v2 on v1

--- a/solution.py
+++ b/solution.py
@@ -22,6 +22,10 @@
 ANY = pl.BlockSpec(memory_space=pl.ANY)
 
 
+def in_hbm(array):
+    return pltpu.with_memory_space_constraint(array, pltpu.HBM)
+
+
 def mm(a, b):
     return jnp.dot(a, b, preferred_element_type=F32)
 
@@ -46,49 +50,55 @@
     return column(seg_ref[:, keys]) == seg_ref[:, queries]
 
 
-def project_window(first, last, per, got_ref, x_hbm, qkv_ref, qkv_hbm, turned_ref, w_ref, x_buf, x_sem, out_sem, tile):
-    def fetch(j):
-        slot = lax.rem(j, 2)
-        at = pl.ds(pl.multiple_of(j * tile, tile), tile)
-        return pltpu.make_async_copy(x_hbm.at[at], x_buf.at[slot], x_sem.at[slot])
-
-    fetch(first).start()
-    for n in range(got_ref.shape[0]):
-        w_ref[n * per : (n + 1) * per] = got_ref[n, :per].astype(F32)
-    turned_ref[...] = w_ref[...].T.astype(BF16)
-    bias = column(jnp.sum(got_ref[:, per + 1 : per + 2].astype(F32), axis=0))
-
-    def keep(j):
-        at = pl.ds(pl.multiple_of(j * tile, tile), tile)
-        return pltpu.make_async_copy(qkv_ref.at[:, at], qkv_hbm.at[:, at], out_sem.at[j])
-
-    def one(j, c):
-        @pl.when(j + 1 < last)
-        def _():
-            fetch(j + 1).start()
-
-        fetch(j).wait()
-        at = pl.ds(pl.multiple_of(j * tile, tile), tile)
-        qkv_ref[:, at] = (mm_nt(turned_ref[...], x_buf[lax.rem(j, 2)]) + bias).astype(BF16)
-        keep(j).start()
-        return c
-
-    def done(j, c):
-        keep(j).wait()
-        return c
-
-    lax.fori_loop(first, last, one, 0)
-    return lambda: lax.fori_loop(first, last, done, 0)
-
-
 def attend_body(
-    lo_ref, hi_ref, seg_ref, got_ref, x_hbm, out_ref, lse_ref, turned_ref, qkv_hbm, qkv_ref, w_ref, x_buf, x_sem, out_sem, *,
-    groups, rows, tile, per
+    lo_ref, hi_ref, seg_ref, bias_ref, turned_hbm, own_hbm, x_hbm, out_hbm, lse_hbm, qkv_hbm, qkv_ref, x_buf, out_ref, lse_ref,
+    turned_ref, x_sem, own_sem, out_sem, result_sem, *, groups, rows, tile
 ):
     count = rows // tile
-    wait_kept = project_window(
-        lo_ref[0], hi_ref[count - 1], per, got_ref, x_hbm, qkv_ref, qkv_hbm, turned_ref, w_ref, x_buf, x_sem, out_sem, tile
-    )
+    own = pl.ds(rows, rows)
+    load_turned = pltpu.make_async_copy(turned_hbm, turned_ref, own_sem.at[0])
+    load_own = pltpu.make_async_copy(own_hbm, qkv_ref.at[:, own], own_sem.at[1])
+    keep_own = pltpu.make_async_copy(qkv_ref.at[:, own], qkv_hbm.at[:, own], own_sem.at[2])
+
+    before = count - jnp.minimum(lo_ref[0], count)
+    tiles = before + jnp.maximum(hi_ref[count - 1] - 2 * count, 0)
+
+    def span(t):
+        j = jnp.where(t < before, count - before + t, 2 * count + t - before)
+        return pl.ds(pl.multiple_of(j * tile, tile), tile)
+
+    def fetch(t):
+        slot = lax.rem(t, 2)
+        return pltpu.make_async_copy(x_hbm.at[span(t)], x_buf.at[slot], x_sem.at[slot])
+
+    def keep(t):
+        return pltpu.make_async_copy(qkv_ref.at[:, span(t)], qkv_hbm.at[:, span(t)], out_sem.at[t])
+
+    load_turned.start()
+
+    @pl.when(tiles > 0)
+    def _():
+        fetch(0).start()
+
+    load_own.start()
+    load_turned.wait()
+
+    def project(t, c):
+        @pl.when(t + 1 < tiles)
+        def _():
+            fetch(t + 1).start()
+
+        fetch(t).wait()
+        qkv_ref[:, span(t)] = (mm_nt(turned_ref[...], x_buf[lax.rem(t, 2)]) + bias_ref[...]).astype(BF16)
+        keep(t).start()
+        return c
+
+    lax.fori_loop(0, tiles, project, 0)
+    load_own.wait()
+    keep_own.start()
+
+    def put_out(i):
+        return pltpu.make_async_copy(out_ref.at[i], out_hbm.at[i], result_sem.at[i])
 
     def one_query(i, mild):
         at = pl.ds(pl.multiple_of(i * tile, tile), tile)
@@ -126,6 +136,7 @@
             top, total, acc = state[h]
             out_ref[i, h * HEAD_DIM : (h + 1) * HEAD_DIM, :] = (acc / total).astype(BF16)
             lse_ref[h : h + 1, at] = top + jnp.log(total)
+        put_out(i).start()
 
     def longest(part, first, last):
         def grow(j, best):
@@ -147,41 +158,72 @@
             def _(i):
                 one_query(i, mild)
 
-    wait_kept()
-
-
-def attend(x_win, got, seg, lo, hi, groups, rows, tile, per):
-    width = x_win.shape[1]
-    wide = got.shape[2]
+    put_lse = pltpu.make_async_copy(lse_ref, lse_hbm, result_sem.at[count])
+    put_lse.start()
+    for i in range(count):
+        put_out(i).wait()
+    put_lse.wait()
+    keep_own.wait()
+
+    def done(t, c):
+        keep(t).wait()
+        return c
+
+    lax.fori_loop(0, tiles, done, 0)
+
+
+def attend(x_win, own, turned, bias, seg, lo, hi, groups, rows, tile):
+    wide, width = turned.shape
     return pl.pallas_call(
-        functools.partial(attend_body, groups=groups, rows=rows, tile=tile, per=per),
+        functools.partial(attend_body, groups=groups, rows=rows, tile=tile),
         out_shape=(
-            jax.ShapeDtypeStruct((rows // tile, groups * HEAD_DIM, tile), BF16),
-            jax.ShapeDtypeStruct((groups, rows), F32),
-            jax.ShapeDtypeStruct((wide, width), BF16),
-            jax.ShapeDtypeStruct((wide, 3 * rows), BF16),
+            pltpu.HBM((rows // tile, groups * HEAD_DIM, tile), BF16),
+            pltpu.HBM((groups, rows), F32),
+            pltpu.HBM((wide, 3 * rows), BF16),
         ),
-        in_specs=[SMEM, SMEM, VMEM, VMEM, ANY],
-        out_specs=(VMEM, VMEM, VMEM, ANY),
+        in_specs=[SMEM, SMEM, VMEM, VMEM, ANY, ANY, ANY],
+        out_specs=(ANY,) * 3,
         scratch_shapes=[
             pltpu.VMEM((wide, 3 * rows), BF16),
-            pltpu.VMEM((width, wide), F32),
             pltpu.VMEM((2, tile, width), BF16),
+            pltpu.VMEM((rows // tile, groups * HEAD_DIM, tile), BF16),
+            pltpu.VMEM((groups, rows), F32),
+            pltpu.VMEM((wide, width), BF16),
             pltpu.SemaphoreType.DMA((2,)),
-            pltpu.SemaphoreType.DMA((3 * rows // tile,)),
+            pltpu.SemaphoreType.DMA((3,)),
+            pltpu.SemaphoreType.DMA((2 * rows // tile,)),
+            pltpu.SemaphoreType.DMA((rows // tile + 1,)),
         ],
-        compiler_params=pltpu.CompilerParams(vmem_limit_bytes=48 << 20),
+        compiler_params=pltpu.CompilerParams(vmem_limit_bytes=32 << 20),
         cost_estimate=pl.CostEstimate(flops=36_000_000_000, bytes_accessed=24_000_000, transcendentals=15_000_000),
         name="attend",
-    )(lo, hi, seg, got, x_win)
+    )(lo, hi, seg, bias, in_hbm(turned), in_hbm(own), in_hbm(x_win))
 
 
 def own_grads_body(
-    lo_ref, hi_ref, qkv_ref, do_ref, lse_ref, delta_ref, seg_ref, dq_ref, dk_ref, dv_ref, acc_ref, *, groups, rows, tile
+    lo_ref, hi_ref, qkv_hbm, do_hbm, lse_ref, delta_ref, seg_ref, dq_hbm, dk_hbm, dv_hbm, qkv_ref, do_ref, dq_ref, dk_ref, dv_ref,
+    acc_ref, in_sem, dq_sem, out_sem, *, groups, rows, tile
 ):
     count = rows // tile
+    q_rows, kv_rows = pl.ds(0, groups * HEAD_DIM), pl.ds(groups * HEAD_DIM, 2 * groups * HEAD_DIM)
+    before, own, after = (pl.ds(n * rows, rows) for n in range(3))
+
+    def load(features, tokens, n):
+        copy = pltpu.make_async_copy(qkv_hbm.at[features, tokens], qkv_ref.at[features, tokens], in_sem.at[n])
+        copy.start()
+        return copy
+
+    first = [load(kv_rows, own, 0), load(q_rows, own, 1), pltpu.make_async_copy(do_hbm, do_ref, in_sem.at[2])]
+    first[2].start()
+    later = [load(kv_rows, before, 3), load(kv_rows, after, 4)]
     dk_ref[...] = jnp.zeros_like(dk_ref)
     dv_ref[...] = jnp.zeros_like(dv_ref)
+    for copy in first:
+        copy.wait()
+
+    def put_dq(i):
+        at = pl.ds(pl.multiple_of(i * tile, tile), tile)
+        return pltpu.make_async_copy(dq_ref.at[:, :, at], dq_hbm.at[:, :, at], dq_sem.at[i])
 
     def one_query(i, _):
         at = pl.ds(pl.multiple_of(i * tile, tile), tile)
@@ -219,46 +261,93 @@
 
         lo, hi = lo_ref[i], hi_ref[i]
         lax.fori_loop(jnp.maximum(lo, count), jnp.minimum(hi, 2 * count), inside, 0)
+
+        @pl.when(i == 0)
+        def _():
+            for copy in later:
+                copy.wait()
+
         lax.fori_loop(lo, jnp.minimum(hi, count), outside, 0)
         lax.fori_loop(jnp.maximum(lo, 2 * count), hi, outside, 0)
         dq_ref[:, :, at] = (acc_ref[...] * SCALE).astype(BF16)
+        put_dq(i).start()
         return 0
 
     lax.fori_loop(0, count, one_query, 0)
+    results = [pltpu.make_async_copy(dk_ref, dk_hbm, out_sem.at[0]), pltpu.make_async_copy(dv_ref, dv_hbm, out_sem.at[1])]
+    for copy in results:
+        copy.start()
+    for copy in results + [put_dq(i) for i in range(count)]:
+        copy.wait()
 
 
 def own_grads(qkv, d_out, lse, delta, seg, lo, hi, groups, rows, tile):
     return pl.pallas_call(
         functools.partial(own_grads_body, groups=groups, rows=rows, tile=tile),
         out_shape=(
-            jax.ShapeDtypeStruct((groups, HEAD_DIM, rows), BF16),
-            jax.ShapeDtypeStruct((groups, rows, HEAD_DIM), F32),
-            jax.ShapeDtypeStruct((groups, rows, HEAD_DIM), F32),
+            pltpu.HBM((groups, HEAD_DIM, rows), BF16),
+            pltpu.HBM((groups, rows, HEAD_DIM), F32),
+            pltpu.HBM((groups, rows, HEAD_DIM), F32),
         ),
-        in_specs=[SMEM, SMEM] + [VMEM] * 5,
-        out_specs=(VMEM,) * 3,
-        scratch_shapes=[pltpu.VMEM((groups, HEAD_DIM, tile), F32)],
-        compiler_params=pltpu.CompilerParams(vmem_limit_bytes=52 << 20),
+        in_specs=[SMEM, SMEM, ANY, ANY, VMEM, VMEM, VMEM],
+        out_specs=(ANY,) * 3,
+        scratch_shapes=[
+            pltpu.VMEM(qkv.shape, BF16),
+            pltpu.VMEM(d_out.shape, BF16),
+            pltpu.VMEM((groups, HEAD_DIM, rows), BF16),
+            pltpu.VMEM((groups, rows, HEAD_DIM), F32),
+            pltpu.VMEM((groups, rows, HEAD_DIM), F32),
+            pltpu.VMEM((groups, HEAD_DIM, tile), F32),
+            pltpu.SemaphoreType.DMA((5,)),
+            pltpu.SemaphoreType.DMA((rows // tile,)),
+            pltpu.SemaphoreType.DMA((2,)),
+        ],
+        compiler_params=pltpu.CompilerParams(vmem_limit_bytes=36 << 20),
         cost_estimate=pl.CostEstimate(flops=60_000_000_000, bytes_accessed=20_000_000, transcendentals=15_000_000),
         name="own_grads",
-    )(lo, hi, qkv, d_out, lse, delta, seg)
+    )(lo, hi, in_hbm(qkv), in_hbm(d_out), lse, delta, seg)
 
 
 def outer_grads_body(
-    lo_ref, hi_ref, qkv_ref, do_lo_ref, do_hi_ref, lse_lo_ref, lse_hi_ref, delta_lo_ref, delta_hi_ref, seg_ref, dq_ref, dk_ref,
-    dv_ref, turned_ref, x_hbm, dw_ref, part_ref, sum_ref, out_ref, dk_acc, dv_acc, dw_acc, x_buf, x_sem, *, groups, rows, tile
+    lo_ref, hi_ref, qkv_hbm, do_lo_ref, do_hi_ref, lse_lo_ref, lse_hi_ref, delta_lo_ref, delta_hi_ref, seg_ref, dq_hbm, dk_hbm,
+    dv_hbm, turned_hbm, x_hbm, dw_hbm, part_hbm, sum_ref, qkv_ref, out_ref, dk_acc, dv_acc, dw_acc, x_buf,
+    turned_ref, dw_ref, part_ref, in_sem, tile_sem, out_sem, *, groups, rows, tile
 ):
-    fetch = pltpu.make_async_copy(x_hbm.at[pl.ds(rows, rows)], x_buf, x_sem)
-    fetch.start()
     count = rows // tile
-    for h in range(groups):
-        out_ref[feature_rows(h)] = dq_ref[h]
+    features = groups * HEAD_DIM
+    q_rows, kv_rows = pl.ds(0, features), pl.ds(features, 2 * features)
+    before, own, after = (pl.ds(n * rows, rows) for n in range(3))
+
+    def load(src, dst, sem):
+        copy = pltpu.make_async_copy(src, dst, sem)
+        copy.start()
+        return copy
+
+    def sums(j):
+        at = pl.ds(pl.multiple_of(j * tile, tile), tile)
+        return (
+            pltpu.make_async_copy(dk_hbm.at[:, at], dk_acc.at[:, at], tile_sem.at[0, j]),
+            pltpu.make_async_copy(dv_hbm.at[:, at], dv_acc.at[:, at], tile_sem.at[1, j]),
+        )
+
+    first = [
+        load(qkv_hbm.at[kv_rows, own], qkv_ref.at[kv_rows, own], in_sem.at[0]),
+        load(qkv_hbm.at[q_rows, before], qkv_ref.at[q_rows, before], in_sem.at[1]),
+        load(qkv_hbm.at[q_rows, after], qkv_ref.at[q_rows, after], in_sem.at[2]),
+    ]
+    for j in range(count):
+        for copy in sums(j):
+            copy.start()
+    later = [load(turned_hbm, turned_ref, in_sem.at[3]), load(x_hbm.at[own], x_buf, in_sem.at[4])]
+    later += [load(dq_hbm.at[h], out_ref.at[feature_rows(h)], in_sem.at[5 + h]) for h in range(groups)]
+    for copy in first:
+        copy.wait()
 
     def one_key(j, _):
         mine = pl.ds(pl.multiple_of(j * tile, tile), tile)
         keys = pl.ds(pl.multiple_of(rows + j * tile, tile), tile)
-        dk_acc[...] = dk_ref[:, mine, :]
-        dv_acc[...] = dv_ref[:, mine, :]
+        for copy in sums(j):
+            copy.wait()
 
         def pair(i, base, do_ref, lse_ref, delta_ref):
             at = pl.ds(pl.multiple_of((i - base) * tile, tile), tile)
@@ -276,8 +365,8 @@
                     ahead = products(h + 1)
                 weights = jnp.exp(jnp.where(same, scores - lse_ref[h : h + 1, at], NEG))
                 d_scores = (weights * (d_weights - delta_ref[h : h + 1, at])).astype(BF16)
-                dv_acc[h] += mm_nt(weights.astype(BF16), do_ref[feature_rows(h), at])
-                dk_acc[h] += mm_nt(d_scores, query)
+                dv_acc[h, mine, :] += mm_nt(weights.astype(BF16), do_ref[feature_rows(h), at])
+                dk_acc[h, mine, :] += mm_nt(d_scores, query)
 
         def before(i, c):
             pair(i, 0, do_lo_ref, lse_lo_ref, delta_lo_ref)
@@ -291,25 +380,34 @@
         lax.fori_loop(lo, jnp.minimum(hi, count), before, 0)
         lax.fori_loop(jnp.maximum(lo, 2 * count), hi, after, 0)
         for h in range(groups):
-            out_ref[feature_rows(groups + h), mine] = dk_acc[h].T.astype(BF16)
-            out_ref[feature_rows(2 * groups + h), mine] = dv_acc[h].T.astype(BF16)
+            out_ref[feature_rows(groups + h), mine] = dk_acc[h, mine, :].T.astype(BF16)
+            out_ref[feature_rows(2 * groups + h), mine] = dv_acc[h, mine, :].T.astype(BF16)
         return 0
 
     lax.fori_loop(0, count, one_key, 0)
-    fetch.wait()
+    for copy in later:
+        copy.wait()
     dw_acc[...] = jnp.zeros_like(dw_acc)
     sum_ref[...] = jnp.zeros_like(sum_ref)
+
+    def put_part(j):
+        at = pl.ds(pl.multiple_of(j * tile, tile), tile)
+        return pltpu.make_async_copy(part_ref.at[at], part_hbm.at[at], out_sem.at[j])
 
     def back(j, _):
         mine = pl.ds(pl.multiple_of(j * tile, tile), tile)
         d = out_ref[:, mine]
         part_ref[mine, :] = mm_tn(d, turned_ref[...]).astype(BF16)
+        put_part(j).start()
         dw_acc[...] += mm(d, x_buf[mine, :])
         sum_ref[...] += jnp.sum(d.astype(F32), axis=1, keepdims=True)
         return 0
 
     lax.fori_loop(0, count, back, 0)
     dw_ref[...] = dw_acc[...].T.astype(BF16)
+    load(dw_ref, dw_hbm, out_sem.at[count]).wait()
+    for j in range(count):
+        put_part(j).wait()
 
 
 def outer_grads(
@@ -319,24 +417,30 @@
     return pl.pallas_call(
         functools.partial(outer_grads_body, groups=groups, rows=rows, tile=tile),
         out_shape=(
-            jax.ShapeDtypeStruct((width, wide), BF16),
-            jax.ShapeDtypeStruct((rows, width), BF16),
+            pltpu.HBM((width, wide), BF16),
+            pltpu.HBM((rows, width), BF16),
             jax.ShapeDtypeStruct((wide, 1), F32),
         ),
-        in_specs=[SMEM, SMEM] + [VMEM] * 12 + [ANY],
-        out_specs=(VMEM,) * 3,
+        in_specs=[SMEM, SMEM, ANY] + [VMEM] * 7 + [ANY] * 5,
+        out_specs=(ANY, ANY, VMEM),
         scratch_shapes=[
+            pltpu.VMEM(qkv.shape, BF16),
             pltpu.VMEM((wide, rows), BF16),
-            pltpu.VMEM((groups, tile, HEAD_DIM), F32),
-            pltpu.VMEM((groups, tile, HEAD_DIM), F32),
+            pltpu.VMEM((groups, rows, HEAD_DIM), F32),
+            pltpu.VMEM((groups, rows, HEAD_DIM), F32),
             pltpu.VMEM((wide, width), F32),
             pltpu.VMEM((rows, width), BF16),
-            pltpu.SemaphoreType.DMA,
+            pltpu.VMEM((wide, width), BF16),
+            pltpu.VMEM((width, wide), BF16),
+            pltpu.VMEM((rows, width), BF16),
+            pltpu.SemaphoreType.DMA((5 + groups,)),
+            pltpu.SemaphoreType.DMA((2, rows // tile)),
+            pltpu.SemaphoreType.DMA((rows // tile + 1,)),
         ],
-        compiler_params=pltpu.CompilerParams(vmem_limit_bytes=54 << 20),
+        compiler_params=pltpu.CompilerParams(vmem_limit_bytes=44 << 20),
         cost_estimate=pl.CostEstimate(flops=24_000_000_000, bytes_accessed=24_000_000, transcendentals=5_000_000),
         name="outer_grads",
-    )(lo, hi, qkv, do_lo, do_hi, lse_lo, lse_hi, delta_lo, delta_hi, seg, dq, dk, dv, turned, x_win)
+    )(lo, hi, in_hbm(qkv), do_lo, do_hi, lse_lo, lse_hi, delta_lo, delta_hi, seg, in_hbm(dq), in_hbm(dk), in_hbm(dv), in_hbm(turned), in_hbm(x_win))
 
 
 def place():
@@ -390,7 +494,8 @@
 
 
 def collect_body(
-    n_blk, n_head, chunks, x_ref, w_ref, xw_ref, wr_ref, local_sem, near_send, near_recv, w_send, w_recv, x_send, x_recv
+    n_blk, n_head, chunks, x_ref, w_ref, xw_ref, wr_ref, qkv_hbm, turned_hbm, bias_ref, vec_ref, inb_ref, x_own, got_ref, w_full, turned_ref, qkv_ref,
+    local_sem, near_send, near_recv, w_send, w_recv, x_send, x_recv
 ):
     blk, head = place()
     rows = x_ref.shape[0] // chunks
@@ -465,6 +570,49 @@
                 on_core.start()
 
     for c in range(chunks):
+        arrived(1, core, c)
+        arrived(1, far, c)
+    keep_x.wait()
+    load_x = pltpu.make_async_copy(xw_ref.at[1], x_own, local_sem.at[0])
+    load_x.start()
+    wait_w()
+    load_w = pltpu.make_async_copy(wr_ref, got_ref, local_sem.at[1])
+    load_w.start()
+    load_w.wait()
+    per = w_full.shape[0] // (n_blk * n_head)
+    bias = jnp.zeros((1, w_full.shape[1]), F32)
+    for b in range(n_blk):
+        for h in range(n_head):
+            first = (b * n_head + h) * per
+            w_full[first : first + per] = got_ref[b, h, :per].astype(F32)
+            bias = bias + got_ref[b, h, per + 1 : per + 2].astype(F32)
+    turned_ref[...] = w_full[...].T.astype(BF16)
+    bias_ref[...] = column(bias)
+    keep_turned = pltpu.make_async_copy(turned_ref, turned_hbm, local_sem.at[1])
+    keep_turned.start()
+    load_x.wait()
+    tok = x_ref.shape[0]
+
+    def project(n, c):
+        at = pl.ds(pl.multiple_of(n * tok, tok), tok)
+        qkv_ref[:, at] = (mm_nt(turned_ref[...], x_own[n]) + bias_ref[...]).astype(BF16)
+        return c
+
+    lax.fori_loop(0, n_head, project, 0)
+    keep_qkv = pltpu.make_async_copy(qkv_ref, qkv_hbm, local_sem.at[0])
+    keep_qkv.start()
+
+    vec_ref[...] = jnp.zeros_like(vec_ref)
+    if per % 8 == 0:
+        pieces = [got_ref[b, h, per : per + 1].astype(F32) for b in range(n_blk) for h in range(n_head)]
+        for n in range(2, 8):
+            vec_ref[n - 2 : n - 1] = jnp.concatenate([row[:, n * per : (n + 1) * per] for row in pieces], axis=1)
+        hidden = inb_ref.shape[1] // len(pieces)
+        inb_ref[...] = jnp.concatenate([row[:, 8 * per : 8 * per + hidden] for row in pieces], axis=1)
+    else:
+        inb_ref[...] = jnp.zeros_like(inb_ref)
+
+    for c in range(chunks):
         for slot, there, n in ((0, has_before, 7), (2, has_after, 10)):
             relay = send(xw_ref.at[slot, row, part(c)], slot, row, c, n, (blk, core))
             halo.append((there, relay))
@@ -475,8 +623,6 @@
                 relay.start()
 
     for c in range(chunks):
-        arrived(1, core, c)
-        arrived(1, far, c)
         for slot, there in ((0, has_before), (2, has_after)):
 
             @pl.when(there)
@@ -484,8 +630,8 @@
                 arrived(slot, core, c)
                 arrived(slot, far, c)
 
-    keep_x.wait()
-    wait_w()
+    keep_turned.wait()
+    keep_qkv.wait()
     for copy in started:
         copy.wait_send()
     for there, copies in ((has_after, to_after), (has_before, to_before)):
@@ -502,17 +648,30 @@
             copy.wait_send()
 
 
-def collect(x, w, n_blk, n_head):
+def collect(x, w, ff, n_blk, n_head):
     chunks = 2
+    tok, width = x.shape
+    wide = w.shape[2]
+    rows = n_head * tok
     return pl.pallas_call(
         functools.partial(collect_body, n_blk, n_head, chunks),
         out_shape=(
-            jax.ShapeDtypeStruct((3, n_head, *x.shape), x.dtype),
-            jax.ShapeDtypeStruct((n_blk, *w.shape), w.dtype),
+            pltpu.HBM((3, n_head, *x.shape), x.dtype),
+            pltpu.HBM((n_blk, *w.shape), w.dtype),
+            pltpu.HBM((wide, rows), BF16),
+            pltpu.HBM((wide, width), BF16),
+            jax.ShapeDtypeStruct((wide, 1), F32),
+            jax.ShapeDtypeStruct((8, width), F32),
+            jax.ShapeDtypeStruct((1, ff), F32),
         ),
         in_specs=[ANY, ANY],
-        out_specs=(ANY, ANY),
+        out_specs=(ANY,) * 4 + (VMEM,) * 3,
         scratch_shapes=[
+            pltpu.VMEM((n_head, tok, width), x.dtype),
+            pltpu.VMEM((n_blk, *w.shape), w.dtype),
+            pltpu.VMEM((width, wide), F32),
+            pltpu.VMEM((wide, width), BF16),
+            pltpu.VMEM((wide, rows), BF16),
             pltpu.SemaphoreType.DMA((2,)),
             pltpu.SemaphoreType.DMA((n_head,)),
             pltpu.SemaphoreType.DMA((n_head,)),
@@ -521,17 +680,28 @@
             pltpu.SemaphoreType.DMA((11, chunks)),
             pltpu.SemaphoreType.DMA((3, n_head, chunks)),
         ],
-        compiler_params=pltpu.CompilerParams(collective_id=0, has_side_effects=True),
+        compiler_params=pltpu.CompilerParams(collective_id=0, has_side_effects=True, vmem_limit_bytes=32 << 20),
         name="collect",
-    )(x, w)
+    )(in_hbm(x), in_hbm(w))
 
 
 def finish_body(
-    n_blk, n_head, part_ref, first_ref, w_ref, t_ref, out_ref, dw_ref, dt_ref, near, mine, far_in, w_in, t_in, w_sum, t_sum, w_end,
-    t_end, x_send, x_recv, w_send, w_recv, t_send, t_recv, w_send2, w_recv2, t_send2, t_recv2
+    n_blk, n_head, part_ref, first_hbm, w_ref, t_ref, out_ref, dw_ref, dt_ref, part_row, part_own, first_ref, w_own, near, mine,
+    far_in, w_in, t_in, w_sum, t_sum, w_end, t_end, load_sem, x_send, x_recv, w_send, w_recv, t_send, t_recv, w_send2, w_recv2,
+    t_send2, t_recv2
 ):
     blk, head = place()
     core, row, far = head ^ 1, head ^ 2, head ^ 3
+
+    def load(src, dst, n):
+        copy = pltpu.make_async_copy(src, dst, load_sem.at[n])
+        copy.start()
+        return copy
+
+    loads = [
+        load(part_ref.at[row], part_row, 0), load(w_ref.at[blk], w_own, 1), load(part_ref.at[head], part_own, 2),
+        load(first_hbm, first_ref, 3),
+    ]
     greet_cross(n_blk, n_head)
 
     def send(src, dst, n, to):
@@ -545,13 +715,15 @@
     for_core.start()
     wait_w = spread(0, n_blk, lambda b: w_ref.at[b], w_in.at[blk], w_send, w_recv)
     wait_t = spread(0, n_blk, lambda b: t_ref.at[b], t_in.at[blk], t_send, t_recv)
+    loads[0].wait()
     for_far.wait()
-    mine[...] = (part_ref[row].astype(F32) + near[1].astype(F32)).astype(BF16)
+    mine[...] = (part_row[...].astype(F32) + near[1].astype(F32)).astype(BF16)
     for_row = send(mine, far_in, 2, (blk, row))
     for_row.start()
     wait_w()
     wait_t()
-    w_sum[...] = w_ref[blk].astype(F32)
+    loads[1].wait()
+    w_sum[...] = w_own[...].astype(F32)
     t_sum[...] = t_ref[blk]
 
     def add(step, c):
@@ -575,9 +747,11 @@
         for p in range(parts):
             first = (p * n_head + h) * cut
             dw_ref[:, first : first + cut] = w_end[h, :, p * cut : (p + 1) * cut]
+    loads[2].wait()
+    loads[3].wait()
     for_row.wait()
     out_ref[...] = (
-        first_ref[...] + part_ref[head].astype(F32) + near[0].astype(F32) + far_in[...].astype(F32)
+        first_ref[...] + part_own[...].astype(F32) + near[0].astype(F32) + far_in[...].astype(F32)
     ).astype(BF16)
 
 
@@ -591,9 +765,13 @@
             jax.ShapeDtypeStruct((per, 3 * width), F32),
             jax.ShapeDtypeStruct(table.shape[2:], F32),
         ),
-        in_specs=[VMEM] * 4,
+        in_specs=[ANY, ANY, ANY, VMEM],
         out_specs=(VMEM,) * 3,
         scratch_shapes=[
+            pltpu.VMEM((rows, width), BF16),
+            pltpu.VMEM((rows, width), BF16),
+            pltpu.VMEM((rows, width), F32),
+            pltpu.VMEM(w.shape[1:], w.dtype),
             pltpu.VMEM((2, rows, width), BF16),
             pltpu.VMEM((rows, width), BF16),
             pltpu.VMEM((rows, width), BF16),
@@ -603,6 +781,7 @@
             pltpu.VMEM(table.shape[1:], F32),
             pltpu.VMEM(w.shape[1:], F32),
             pltpu.VMEM(table.shape[1:], F32),
+            pltpu.SemaphoreType.DMA((4,)),
             pltpu.SemaphoreType.DMA((3,)),
             pltpu.SemaphoreType.DMA((3,)),
         ]
@@ -610,7 +789,7 @@
         + [pltpu.SemaphoreType.DMA((n_head,))] * 4,
         compiler_params=pltpu.CompilerParams(collective_id=1, has_side_effects=True, vmem_limit_bytes=40 << 20),
         name="finish",
-    )(part, d_first, w, table)
+    )(in_hbm(part), in_hbm(d_first), in_hbm(w), table)
 
 
 def greet(n_blk, n_head):
@@ -706,7 +885,7 @@
         ],
         compiler_params=pltpu.CompilerParams(collective_id=2, has_side_effects=True),
         name="to_tokens",
-    )(out, lse)
+    )(in_hbm(out), in_hbm(lse))
 
 
 def to_heads_body(
@@ -770,7 +949,7 @@
         ],
         compiler_params=pltpu.CompilerParams(collective_id=3, has_side_effects=True),
         name="to_heads",
-    )(d_seq, d_part)
+    )(in_hbm(d_seq), in_hbm(d_part))
 
 
 def regroup(values, outer, inner, unit):
@@ -902,8 +1081,8 @@
 
 
 def dense_body(
-    x_ref, seq_ref, cot_ref, vec_ref, inb_ref, w_hbm, out_ref, first_ref, dseq_ref, delta_ref, dvec_ref, dinb_ref, grad_hbm, w, grad,
-    unit_ref, r_ref, normed_ref, low_ref, acc_ref, slope_ref, act_ref, e_ref, w_sem, grad_sem, *, blocks
+    x_ref, seq_ref, cot_ref, vec_ref, inb_ref, w_hbm, out_ref, first_ref, dseq_ref, delta_ref, dvec_ref, dinb_ref, grad_hbm, bias_ref, dbias_ref, w, grad,
+    unit_ref, r_ref, normed_ref, low_ref, acc_ref, slope_ref, act_ref, e_ref, w_sem, grad_sem, *, blocks, count
 ):
     width = x_ref.shape[1]
     out_at, down_at = blocks * width, (blocks + 1) * width
@@ -921,6 +1100,8 @@
         at = cols(first, c)
         return pltpu.make_async_copy(grad.at[:, at], grad_hbm.at[:, at], grad_sem.at[n])
 
+    piece = width // count
+    bias_ref[...] = inb_ref[...] if piece % 8 else regroup(inb_ref[...], count, blocks, piece)
     w_out_here = fetch(out_at, width, 0)
     w_in_here = fetch(0, out_at, 1)
     w_down_here = fetch(down_at, blocks * width, 2)
@@ -938,7 +1119,7 @@
 
     def up_down(c, carry):
         at = cols(0, c)
-        hidden = mm(low_ref[...], w[:, at]) + inb_ref[:, at]
+        hidden = mm(low_ref[...], w[:, at]) + bias_ref[:, at]
         phi = 0.5 + 0.5 * lax.erf(hidden * (2.0**-0.5))
         act = (hidden * phi).astype(BF16)
         act_ref[:, at] = act
@@ -946,7 +1127,7 @@
         acc_ref[...] += mm(act, w[:, cols(down_at, c)])
         return carry
 
-    lax.fori_loop(0, blocks, up_down, 0)
+    lax.fori_loop(0, blocks, up_down, 0, unroll=2)
     unit2, r2 = normalize(acc_ref[...])
     out_ref[...] = (unit2 * ln2_gain + ln2_bias).astype(BF16)
     dy = cot_ref[...].astype(F32)
@@ -961,7 +1142,7 @@
         at, down = cols(0, c), cols(down_at, c)
         e = e_ref[...]
         d_hidden = (mm_nt(e, w[:, down]) * slope_ref[:, at]).astype(BF16)
-        dinb_ref[:, at] = over_rows(d_hidden.astype(F32))
+        dbias_ref[:, at] = over_rows(d_hidden.astype(F32))
         acc_ref[...] += mm_nt(d_hidden, w[:, at])
         grad[:, at] = mm_tn(low_ref[...], d_hidden).astype(BF16)
         put(0, c, c).start()
@@ -969,7 +1150,7 @@
         put(down_at, c, blocks + c).start()
         return carry
 
-    lax.fori_loop(0, blocks, back, 0)
+    lax.fori_loop(0, blocks, back, 0, unroll=2)
     d_normed = acc_ref[...]
     unit = unit_ref[...]
     dvec_ref[1:2] = over_rows(d_normed * unit)
@@ -989,6 +1170,8 @@
             first = (n * groups + g) * HEAD_DIM
             delta_ref[n, g : g + 1] = over_rows(product[first : first + HEAD_DIM])
 
+    dinb_ref[...] = dbias_ref[...] if piece % 8 else regroup(dbias_ref[...], blocks, count, piece)
+
     def done(c, carry):
         put(0, c, c).wait()
         put(down_at, c, blocks + c).wait()
@@ -998,11 +1181,11 @@
     put(out_at, 0, 2 * blocks).wait()
 
 
-def dense(x, seq_t, cotangent, vectors, in_bias, weights, blocks, n_head):
+def dense(x, seq_t, cotangent, vectors, in_bias, weights, blocks, n_head, count):
     tok, width = x.shape
     ff = blocks * width
     return pl.pallas_call(
-        functools.partial(dense_body, blocks=blocks),
+        functools.partial(dense_body, blocks=blocks, count=count),
         out_shape=(
             jax.ShapeDtypeStruct((tok, width), BF16),
             jax.ShapeDtypeStruct((tok, width), F32),
@@ -1015,6 +1198,8 @@
         in_specs=[VMEM] * 5 + [ANY],
         out_specs=(VMEM,) * 6 + (ANY,),
         scratch_shapes=[
+            pltpu.VMEM((1, ff), F32),
+            pltpu.VMEM((1, ff), F32),
             pltpu.VMEM(weights.shape, BF16),
             pltpu.VMEM(weights.shape, BF16),
             pltpu.VMEM((tok, width), F32),
@@ -1070,27 +1255,29 @@
     packed, to_send = pack(w_in, w_out, w_down, w_qkv, small, count, n_head)
     whole = lax.all_gather(packed, BOTH, axis=0, tiled=True)
 
-    x_win, got = collect(inputs, to_send, n_blk, n_head)
+    x_win, got, own_qkv, turned, qkv_bias, vectors, hidden_bias = collect(inputs, to_send, ff, n_blk, n_head)
     x_win = x_win.reshape(3 * rows, width)
-    got = got.reshape(count, *got.shape[2:])
-    all_small = got[:, per, : sum(vec.shape[0] for vec in small)].astype(F32)
     offsets = [0]
     for vec in small:
         offsets.append(offsets[-1] + vec.shape[0])
-    (_, _, f_out_bias, f_ln1_gain, f_ln1_bias, f_down_bias, f_ln2_gain, f_ln2_bias, f_in_bias) = (
-        all_small[:, a:b].reshape(-1) for a, b in zip(offsets[:-1], offsets[1:])
-    )
+    if per % 8:
+        got = got.reshape(count, *got.shape[2:])
+        all_small = got[:, per, : offsets[-1]].astype(F32)
+        full = [all_small[:, a:b].reshape(-1) for a, b in zip(offsets[:-1], offsets[1:])]
+        vectors = jnp.stack(full[2:8] + full[2:4])
+        hidden_bias = regroup(full[8][None], count, blocks, per)
     seg, lo, hi = window_of(segments, blk, rows, tok)
-    attended, lse, turned, qkv = attend(x_win, got, seg, lo, hi, groups, rows, tok, per)
+    attended, lse, qkv = attend(x_win, own_qkv, turned, qkv_bias, seg, lo, hi, groups, rows, tok)
     seq_t, lse_lo, lse_hi = to_tokens(attended, lse, n_blk, n_head)
     seq_t = seq_t.reshape(width, tok)
 
-    vectors = jnp.stack([f_out_bias, f_ln1_gain, f_ln1_bias, f_down_bias, f_ln2_gain, f_ln2_bias] + [f_out_bias] * 2)
     outputs, d_first, d_seq_t, d_part, d_vectors, d_in_bias, grads = dense(
-        inputs, seq_t, cotangent, vectors, regroup(f_in_bias[None], count, blocks, per), whole, blocks, n_head
+        inputs, seq_t, cotangent, vectors, hidden_bias, whole, blocks, n_head, count
     )
     d_out_bias, d_ln1_gain, d_ln1_bias, d_down_bias, d_ln2_gain, d_ln2_bias = (d_vectors[n] for n in range(6))
-    d_in_bias = regroup(d_in_bias, blocks, count, per)[0]
+    if per % 8:
+        d_in_bias = regroup(d_in_bias, blocks, count, per)
+    d_in_bias = d_in_bias[0]
     d_out, delta, delta_lo, delta_hi = to_heads(d_seq_t.reshape(n_head, cut, tok), d_part, n_blk, n_head)
     delta, delta_lo, delta_hi = (a.transpose(1, 0, 2).reshape(groups, rows) for a in (delta, delta_lo, delta_hi))
 

time: 364 us -> 345 us (0.948)
  local copies, waits for them, and re-layouts: 20.5 us -> 5.79 us
  Pallas kernels: 318 us -> 306 us
  waiting for transfers between devices: 0.04 us -> 10.7 us
    pallas_call x1, Pallas kernels: 43.8 us -> 29.4 us  [to_tokens(): pl.pallas_call(functools.partial(to_tokens_body, n_blk, n_head), out_shap...]
    reduce_scatter x1, waiting for transfers between devices: 0.01 us -> 10.7 us  [body(): owned = lax.psum_scatter(grads, BOTH, scatter_dimension=0, tiled=True)]
    pallas_call x1, Pallas kernels: 41 us -> 51.1 us  [own_grads(): pl.pallas_call(functools.partial(own_grads_body, groups=groups, rows=rows...]
    unnamed x41 -> x24, local copies, waits for them, and re-layouts: 12.5 us -> 2.39 us
    pallas_call x1, Pallas kernels: 27.3 us -> 19.1 us  [outer_grads(): pl.pallas_call(functools.partial(outer_grads_body, groups=groups, rows=ro...]
    pallas_call x1, Pallas kernels: 60.1 us -> 66.9 us  [collect(): pl.pallas_call(functools.partial(collect_body, n_blk, n_head, chunks), ou...]
    pallas_call x1, Pallas kernels: 61.6 us -> 56.1 us  [finish(): pl.pallas_call(functools.partial(finish_body, n_blk, n_head), out_shape=(...]
  transfers between devices with their start and end apart: 4 -> 4, of which waited for: 0 -> 1; matrix products, arithmetic and copies ran while one was open for 3% -> 1% of each run, Pallas kernels for 79% -> 79%
where the time goes in v2:
time: 345 us
  Pallas kernels  306 us (89%)
  between operations  14.4 us (4%)
  waiting for transfers between devices  10.7 us (3%)
  starting transfers between devices  5.97 us (2%)
  local copies, waits for them, and re-layouts  5.79 us (2%)
    pallas_call x1, Pallas kernels, collect(): pl.pallas_call(functools.partial(collect_body, n_blk, n_head, chunks), ou...  66.9 us
    pallas_call x1, Pallas kernels, finish(): pl.pallas_call(functools.partial(finish_body, n_blk, n_head), out_shape=(...  56.1 us
    pallas_call x1, Pallas kernels, own_grads(): pl.pallas_call(functools.partial(own_grads_body, groups=groups, rows=rows...  51.1 us
    pallas_call x1, Pallas kernels, attend(): pl.pallas_call(functools.partial(attend_body, groups=groups, rows=rows, t...  36.6 us
    pallas_call x1, Pallas kernels, to_tokens(): pl.pallas_call(functools.partial(to_tokens_body, n_blk, n_head), out_shap...  29.4 us
    pallas_call x1, Pallas kernels, dense(): pl.pallas_call(functools.partial(dense_body, blocks=blocks, count=count),...  28.8 us
    pallas_call x1, Pallas kernels, outer_grads(): pl.pallas_call(functools.partial(outer_grads_body, groups=groups, rows=ro...  19.1 us
    pallas_call x1, Pallas kernels, to_heads(): pl.pallas_call(functools.partial(to_heads_body, n_blk, n_head), out_shape...  14 us
  transfers between devices with their start and end apart: 4, of which 1 were waited for; matrix products, arithmetic and copies ran while one was open for 1% of the time, Pallas kernels for 79%

profile of v2, /device:TPU:0, one launch (start us, length us, event | category | flops | bytes accessed | tf_op | source)
XLA Modules:
  0.0 344.9 jit_solution(10825232975324748931)
XLA Ops:
  7.2 2.2 pack.1
  9.5 0.8 fusion.1
  10.4 66.9 %collect.1 = (bf16[3,4,512,768]{3,2,1,0:T(8,128)(2,1)}, bf16[8,4,32,576]{3,2,1,0:T(8,128)(2,1)}, bf16[576,2048]{1,0:T(8,128)(2,1)}, bf16[576,768]{1,0:T(8,128)(2...) custom-call(bf16[512,768]{1,0:T(8,128)(2,1)} %x_ref.3, ...), custom_call_target="tpu_custom_call" | custom-call | tf_op jit(solution)/shard_map/collect/pallas_call | solution.py:656
  77.4 0.3 convert_reduce_fusion
  77.7 36.6 %attend.1 = (bf16[4,192,512]{2,1,0:T(8,128)(2,1)}, f32[3,2048]{1,0:T(4,128)}, bf16[576,6144]{1,0:T(8,128)(2,1)}) custom-call(s32[4]{0:T(128)S(1)} %get-tuple-element.107.lo_ref, s32[4]{0:T(128)S(1)} %get-tuple-element.108.hi_ref, s32[1,6144]{1,0:T(1,128)S(1)} %bitcast.30, f32[576,1]{1,0:T(8,128)S(1)} %get-tuple-element.53.bias_ref, ...), custom_call_target="tpu_custom_call" | custom-call | flops 35999997952 | bytes 24000000 | tf_op jit(solution)/shard_map/attend/pallas_call | solution.py:177
  114.3 29.4 %to_tokens.1 = (bf16[4,192,512]{2,1,0:T(8,128)(2,1)}, f32[3,2048]{1,0:T(4,128)}, f32[3,2048]{1,0:T(4,128)}) custom-call(bf16[4,192,512]{2,1,0:T(8,128)(2,1)} %get-tuple-element.57.out_ref, f32[3,2048]{1,0:T(4,128)} %get-tuple-element.58.lse_ref), custom_call_target="tpu_custom_call" | custom-call | tf_op jit(solution)/shard_map/to_tokens/pallas_call | solution.py:874
  143.8 28.8 %dense.1 = (bf16[512,768]{1,0:T(8,128)(2,1)}, f32[512,768]{1,0:T(8,128)}, bf16[768,512]{1,0:T(8,128)(2,1)}, f32[4,3,512]{2,1,0:T(4,128)}, f32[8,768]{1,0:T(8,128...) custom-call(bf16[512,768]{1,0:T(8,128)(2,1)} %x_ref.3, bf16[768,512]{1,0:T(8,128)(2,1)} %bitcast.52, ...), custom_call_target="tpu_custom_call" | custom-call | flops 16999999488 | bytes 30000000 | tf_op jit(solution)/shard_map/dense/pallas_call | solution.py:1187
  172.6 14.0 %to_heads.1 = (bf16[192,2048]{1,0:T(8,128)(2,1)}, f32[4,3,512]{2,1,0:T(4,128)}, f32[4,3,512]{2,1,0:T(4,128)}, f32[4,3,512]{2,1,0:T(4,128)}) custom-call(bf16[4,192,512]{2,1,0:T(8,128)(2,1)} %bitcast.40, f32[4,3,512]{2,1,0:T(4,128)} %get-tuple-element.66.dpart_ref), custom_call_target="tpu_custom_call" | custom-call | tf_op jit(solution)/shard_map/to_heads/pallas_call | solution.py:936
  186.6 1.3 collective-permute-start.1
  187.9 4.6 %collective-permute-start = (bf16[192,2048]{1,0:T(8,128)(2,1)}, bf16[192,2048]{1,0:T(8,128)(2,1)S(1)}, u32[]{:S(2)}, u32[]{:S(2)}) collective-permute-start(bf16[192,2048]{1,0:T(8,128)(2,1)} %get-tuple-element.67.do_hbm), channel_id=1, source_target_pairs={{0,4},{4,8},{8,12},{12,16},{16,20},{20,24},{24,28},{1,5},{5,9},{9,... | collective-permute-start | bytes 2359304 | tf_op jit(solution)/shard_map/ppermute | solution.py:1236
  192.5 0.8 copy-done.5
  193.3 51.1 %own_grads.1 = (bf16[3,64,2048]{2,1,0:T(8,128)(2,1)}, f32[3,2048,64]{2,1,0:T(8,128)}, f32[3,2048,64]{2,1,0:T(8,128)}) custom-call(s32[4]{0:T(128)S(1)} %get-tuple-element.107.lo_ref, s32[4]{0:T(128)S(1)} %get-tuple-element.108.hi_ref, bf16[576,6144]{1,0:T(8,128)(2,1)} %get-tuple-element.64.qkv_hbm, bf16[192,2048]{1,0:T(8,128)(2,1)} %get-tuple-element.67.do_hbm, ...), custom_call_target="tpu_custom_call" | custom-call | flops 60000002048 | bytes 20000000 | tf_op jit(solution)/shard_map/own_grads/pallas_call | solution.py:285
  244.4 0.5 broadcast.48
  244.9 0.7 reduce.19
  246.3 19.1 %outer_grads.1 = (bf16[768,576]{1,0:T(8,128)(2,1)}, bf16[2048,768]{1,0:T(8,128)(2,1)}, f32[576,1]{1,0:T(8,128)S(1)}) custom-call(s32[4]{0:T(128)S(1)} %get-tuple-element.107.lo_ref, s32[4]{0:T(128)S(1)} %get-tuple-element.108.hi_ref, bf16[576,6144]{1,0:T(8,128)(2,1)} %get-tuple-element.64.qkv_hbm, bf16[192,2048]{1,0:T(8,128)(2,1)S(1)} %collective-permute-done.do_lo_ref, ...), custom_call_target="tpu_custom_call" | custom-call | flops 24000000000 | bytes 24000000 | tf_op jit(solution)/shard_map/outer_grads/pallas_call | solution.py:417
  265.6 0.2 dynamic_update_slice.6
  266.0 0.2 dynamic_update_slice.7
  266.4 56.1 %finish.1 = (bf16[512,768]{1,0:T(8,128)(2,1)S(1)}, f32[24,2304]{1,0:T(8,128)S(1)}, f32[8,128]{1,0:T(8,128)S(1)}) custom-call(bf16[4,512,768]{2,1,0:T(8,128)(2,1)} %bitcast.38, f32[512,768]{1,0:T(8,128)} %get-tuple-element.77.first_hbm, bf16[8,4,24,576]{3,2,1,0:T(8,128)(2,1)} %bitcast.39, f32[8,4,8,128]{3,2,1,0:T(8,128)S(1)} %bitcast.29), custom_call_target="tpu_custom_call" | custom-call | tf_op jit(solution)/shard_map/finish/pallas_call | solution.py:761
  322.6 0.6 slice.84
  323.2 0.6 fusion.3
  323.8 10.7 %reduce-scatter.2.cloned.1.call-done.packed_ref = bf16[24,6912]{1,0:T(8,128)(2,1)} async-done(((bf16[768,6912]{1,0:T(8,128)(2,1)}), bf16[24,6912]{1,0:T(8,128)(2,1)}) %reduce-scatter.2.cloned.1.call-update) | async-done | bytes 331792 | tf_op jit(solution)/shard_map/reduce_scatter | solution.py:1284
  334.5 2.0 unpack.1
  336.5 0.9 copy.36
  337.4 0.7 copy.37
  (48 shorter events, 1.4 us)
Async XLA Ops:
  7.2 136.6 %all-gather.2.cloned.1.call-start = ((), (), s32[]{:S(2)}) async-start(), calls=%async_computation.1 | async-start | bytes 10948608 | tf_op jit(solution)/shard_map/all_gather | solution.py:1256
  9.4 325.0 %reduce-scatter.2.cloned.1.call-start = ((), (), s32[]{:S(2)}) async-start(), calls=%async_computation.2 | async-start | bytes 10948608 | tf_op jit(solution)/shard_map/reduce_scatter | solution.py:1284
  77.4 36.9 %copy-start.6 = (f32[8,768]{1,0:T(8,128)}, f32[8,768]{1,0:T(8,128)S(1)}, u32[]{:S(2)}) copy-start(f32[8,768]{1,0:T(8,128)S(1)} %get-tuple-element.60.vec_ref) | copy-start | bytes 73732
  77.4 36.9 %copy-start.7 = (f32[1,3072]{1,0:T(1,128)}, f32[1,3072]{1,0:T(1,128)S(1)}, u32[]{:S(2)}) copy-start(f32[1,3072]{1,0:T(1,128)S(1)} %get-tuple-element.61.inb_ref) | copy-start | bytes 36868
  172.6 19.9 %copy-start = (f32[3,2048]{1,0:T(4,128)S(1)}, f32[3,2048]{1,0:T(4,128)}, u32[]{:S(2)}) copy-start(f32[3,2048]{1,0:T(4,128)} %get-tuple-element.58.lse_ref) | copy-start | bytes 73732
  186.6 59.7 %collective-permute-start.1 = (bf16[192,2048]{1,0:T(8,128)(2,1)}, bf16[192,2048]{1,0:T(8,128)(2,1)S(1)}, u32[]{:S(2)}, u32[]{:S(2)}) collective-permute-start(bf16[192,2048]{1,0:T(8,128)(2,1)} %get-tuple-element.67.do_hbm), channel_id=1, source_target_pairs={{4,0},{8,4},{12,8},{16,12},{20,16},{24,20},{28,24},{5,1},{9,5},{13... | collective-permute-start | bytes 2359304 | tf_op jit(solution)/shard_map/ppermute | solution.py:1236
  187.9 58.4 %collective-permute-start = (bf16[192,2048]{1,0:T(8,128)(2,1)}, bf16[192,2048]{1,0:T(8,128)(2,1)S(1)}, u32[]{:S(2)}, u32[]{:S(2)}) collective-permute-start(bf16[192,2048]{1,0:T(8,128)(2,1)} %get-tuple-element.67.do_hbm), channel_id=1, source_target_pairs={{0,4},{4,8},{8,12},{12,16},{16,20},{20,24},{24,28},{1,5},{5,9},{9,... | collective-permute-start | bytes 2359304 | tf_op jit(solution)/shard_map/ppermute | solution.py:1236
  192.5 0.8 copy-start.5
  193.3 51.6 %copy-start.9 = (f32[1,3072]{1,0:T(1,128)S(1)}, f32[1,3072]{1,0:T(1,128)}, u32[]{:S(2)}) copy-start(f32[1,3072]{1,0:T(1,128)} %get-tuple-element.81) | copy-start | bytes 36868
  193.3 52.4 %copy-start.8 = (f32[8,768]{1,0:T(8,128)S(1)}, f32[8,768]{1,0:T(8,128)}, u32[]{:S(2)}) copy-start(f32[8,768]{1,0:T(8,128)} %get-tuple-element.80) | copy-start | bytes 73732
  193.3 53.0 %copy-start.1 = (f32[3,2048]{1,0:T(4,128)S(1)}, f32[3,2048]{1,0:T(4,128)}, u32[]{:S(2)}) copy-start(f32[3,2048]{1,0:T(4,128)} %get-tuple-element.68.lse_lo_ref) | copy-start | bytes 73732
  193.3 53.0 %copy-start.2 = (f32[3,2048]{1,0:T(4,128)S(1)}, f32[3,2048]{1,0:T(4,128)}, u32[]{:S(2)}) copy-start(f32[3,2048]{1,0:T(4,128)} %get-tuple-element.69.lse_hi_ref) | copy-start | bytes 73732
  193.3 53.0 %copy-start.3 = (f32[4,3,512]{2,1,0:T(4,128)S(1)}, f32[4,3,512]{2,1,0:T(4,128)}, u32[]{:S(2)}) copy-start(f32[4,3,512]{2,1,0:T(4,128)} %get-tuple-element.70) | copy-start | bytes 73732
  193.3 53.0 %copy-start.4 = (f32[4,3,512]{2,1,0:T(4,128)S(1)}, f32[4,3,512]{2,1,0:T(4,128)}, u32[]{:S(2)}) copy-start(f32[4,3,512]{2,1,0:T(4,128)} %get-tuple-element.71) | copy-start | bytes 73732
Sparse Core Ops, SparseCore 0:
  11.5 114.1 all-gather.1
  172.7 161.6 reduce-scatter.1

commit v3 on v2

--- a/solution.py
+++ b/solution.py
@@ -105,16 +105,21 @@
         win = pl.ds(pl.multiple_of(rows + i * tile, tile), tile)
         queries = [qkv_ref[feature_rows(h), win] * BF16(SCALE) for h in range(groups)]
 
-        def one_key(j, state):
-            keys = pl.ds(pl.multiple_of(j * tile, tile), tile)
-            same = same_document(seg_ref, keys, win)
-            new = []
-            ahead = mm_tn(qkv_ref[feature_rows(groups), keys], queries[0])
-            for h in range(groups):
-                scores = jnp.where(same, ahead, NEG)
-                if h + 1 < groups:
-                    ahead = mm_tn(qkv_ref[feature_rows(groups + h + 1), keys], queries[h + 1])
-                value = qkv_ref[feature_rows(2 * groups + h), keys]
+        def meet(tiles, state):
+            keys = [pl.ds(pl.multiple_of(j * tile, tile), tile) for j in tiles]
+            same = [same_document(seg_ref, at, win) for at in keys]
+            steps = [(n, h) for n in range(len(tiles)) for h in range(groups)]
+
+            def product(n, h):
+                return mm_tn(qkv_ref[feature_rows(groups + h), keys[n]], queries[h])
+
+            state = list(state)
+            ahead = product(*steps[0])
+            for at, (n, h) in enumerate(steps):
+                scores = jnp.where(same[n], ahead, NEG)
+                if at + 1 < len(steps):
+                    ahead = product(*steps[at + 1])
+                value = qkv_ref[feature_rows(2 * groups + h), keys[n]]
                 top, total, acc = state[h]
                 if mild:
                     weights = jnp.exp(scores)
@@ -124,14 +129,21 @@
                     fade = jnp.exp(top - peak)
                     total, acc, top = total * fade, acc * fade, peak
                 total = total + jnp.sum(weights, axis=0, keepdims=True)
-                new.append((top, total, acc + mm(value, weights.astype(BF16))))
-            return tuple(new)
+                state[h] = (top, total, acc + mm(value, weights.astype(BF16)))
+            return tuple(state)
 
         zero = tuple(
             (jnp.full((1, tile), 0.0 if mild else NEG, F32), jnp.zeros((1, tile), F32), jnp.zeros((HEAD_DIM, tile), F32))
             for _ in range(groups)
         )
-        state = lax.fori_loop(lo_ref[i], hi_ref[i], one_key, zero)
+        lo, hi = lo_ref[i], hi_ref[i]
+        start = lo
+        state = zero
+        if mild:
+            pairs = (hi - lo) // 2
+            state = lax.fori_loop(0, pairs, lambda t, c: meet([lo + 2 * t, lo + 2 * t + 1], c), state)
+            start = lo + 2 * pairs
+        state = lax.fori_loop(start, hi, lambda j, c: meet([j], c), state)
         for h in range(groups):
             top, total, acc = state[h]
             out_ref[i, h * HEAD_DIM : (h + 1) * HEAD_DIM, :] = (acc / total).astype(BF16)
@@ -216,69 +228,81 @@
     first = [load(kv_rows, own, 0), load(q_rows, own, 1), pltpu.make_async_copy(do_hbm, do_ref, in_sem.at[2])]
     first[2].start()
     later = [load(kv_rows, before, 3), load(kv_rows, after, 4)]
-    dk_ref[...] = jnp.zeros_like(dk_ref)
-    dv_ref[...] = jnp.zeros_like(dv_ref)
+    acc_ref[...] = jnp.zeros_like(acc_ref)
     for copy in first:
         copy.wait()
 
+    def tokens(n):
+        return pl.ds(pl.multiple_of(n * tile, tile), tile)
+
     def put_dq(i):
-        at = pl.ds(pl.multiple_of(i * tile, tile), tile)
-        return pltpu.make_async_copy(dq_ref.at[:, :, at], dq_hbm.at[:, :, at], dq_sem.at[i])
+        return pltpu.make_async_copy(dq_ref.at[:, :, tokens(i)], dq_hbm.at[:, :, tokens(i)], dq_sem.at[i])
+
+    def put_sums(j):
+        return (
+            pltpu.make_async_copy(dk_ref.at[:, tokens(j)], dk_hbm.at[:, tokens(j)], out_sem.at[0, j]),
+            pltpu.make_async_copy(dv_ref.at[:, tokens(j)], dv_hbm.at[:, tokens(j)], out_sem.at[1, j]),
+        )
+
+    def pair(i, j, mine):
+        at, win, keys = tokens(i), tokens(count + i), tokens(j)
+        same = same_document(seg_ref, keys, win)
+
+        def products(h):
+            query = qkv_ref[feature_rows(h), win] * BF16(SCALE)
+            return (
+                query,
+                mm_tn(qkv_ref[feature_rows(groups + h), keys], query),
+                mm_tn(qkv_ref[feature_rows(2 * groups + h), keys], do_ref[feature_rows(h), at]),
+            )
+
+        ahead = products(0)
+        for h in range(groups):
+            query, scores, d_weights = ahead
+            if h + 1 < groups:
+                ahead = products(h + 1)
+            weights = jnp.exp(jnp.where(same, scores - lse_ref[h : h + 1, at], NEG))
+            d_scores = (weights * (d_weights - delta_ref[h : h + 1, at])).astype(BF16)
+            acc_ref[h, :, at] += mm(qkv_ref[feature_rows(groups + h), keys], d_scores)
+            if mine is not None:
+                dv_ref[h, tokens(mine), :] += mm_nt(weights.astype(BF16), do_ref[feature_rows(h), at])
+                dk_ref[h, tokens(mine), :] += mm_nt(d_scores, query)
+
+    def one_key(j, _):
+        dk_ref[:, tokens(j), :] = jnp.zeros((groups, tile, HEAD_DIM), F32)
+        dv_ref[:, tokens(j), :] = jnp.zeros((groups, tile, HEAD_DIM), F32)
+
+        def inside(i, c):
+            pair(i - count, count + j, j)
+            return c
+
+        lax.fori_loop(jnp.maximum(lo_ref[j], count), jnp.minimum(hi_ref[j], 2 * count), inside, 0)
+        for copy in put_sums(j):
+            copy.start()
+        return 0
+
+    lax.fori_loop(0, count, one_key, 0)
+    for copy in later:
+        copy.wait()
 
     def one_query(i, _):
-        at = pl.ds(pl.multiple_of(i * tile, tile), tile)
-        win = pl.ds(pl.multiple_of(rows + i * tile, tile), tile)
-        acc_ref[...] = jnp.zeros_like(acc_ref)
-
-        def pair(j, own):
-            keys = pl.ds(pl.multiple_of(j * tile, tile), tile)
-            mine = pl.ds(pl.multiple_of((j - count) * tile, tile), tile)
-            same = same_document(seg_ref, keys, win)
-
-            def products(h):
-                query = qkv_ref[feature_rows(h), win] * BF16(SCALE)
-                return query, mm_tn(qkv_ref[feature_rows(groups + h), keys], query), mm_tn(qkv_ref[feature_rows(2 * groups + h), keys], do_ref[feature_rows(h), at])
-
-            ahead = products(0)
-            for h in range(groups):
-                query, scores, d_weights = ahead
-                if h + 1 < groups:
-                    ahead = products(h + 1)
-                weights = jnp.exp(jnp.where(same, scores - lse_ref[h : h + 1, at], NEG))
-                d_scores = (weights * (d_weights - delta_ref[h : h + 1, at])).astype(BF16)
-                acc_ref[h] += mm(qkv_ref[feature_rows(groups + h), keys], d_scores)
-                if own:
-                    dv_ref[h, mine, :] += mm_nt(weights.astype(BF16), do_ref[feature_rows(h), at])
-                    dk_ref[h, mine, :] += mm_nt(d_scores, query)
-
-        def inside(j, c):
-            pair(j, True)
+        low = count - jnp.minimum(lo_ref[i], count)
+        high = jnp.maximum(hi_ref[i] - 2 * count, 0)
+
+        def outside(t, c):
+            pair(i, jnp.where(t < low, count - low + t, 2 * count + t - low), None)
             return c
 
-        def outside(j, c):
-            pair(j, False)
-            return c
-
-        lo, hi = lo_ref[i], hi_ref[i]
-        lax.fori_loop(jnp.maximum(lo, count), jnp.minimum(hi, 2 * count), inside, 0)
-
-        @pl.when(i == 0)
-        def _():
-            for copy in later:
-                copy.wait()
-
-        lax.fori_loop(lo, jnp.minimum(hi, count), outside, 0)
-        lax.fori_loop(jnp.maximum(lo, 2 * count), hi, outside, 0)
-        dq_ref[:, :, at] = (acc_ref[...] * SCALE).astype(BF16)
+        lax.fori_loop(0, low + high, outside, 0)
+        dq_ref[:, :, tokens(i)] = (acc_ref[:, :, tokens(i)] * SCALE).astype(BF16)
         put_dq(i).start()
         return 0
 
     lax.fori_loop(0, count, one_query, 0)
-    results = [pltpu.make_async_copy(dk_ref, dk_hbm, out_sem.at[0]), pltpu.make_async_copy(dv_ref, dv_hbm, out_sem.at[1])]
-    for copy in results:
-        copy.start()
-    for copy in results + [put_dq(i) for i in range(count)]:
-        copy.wait()
+    for n in range(count):
+        put_dq(n).wait()
+        for copy in put_sums(n):
+            copy.wait()
 
 
 def own_grads(qkv, d_out, lse, delta, seg, lo, hi, groups, rows, tile):
@@ -297,10 +321,10 @@
             pltpu.VMEM((groups, HEAD_DIM, rows), BF16),
             pltpu.VMEM((groups, rows, HEAD_DIM), F32),
             pltpu.VMEM((groups, rows, HEAD_DIM), F32),
-            pltpu.VMEM((groups, HEAD_DIM, tile), F32),
+            pltpu.VMEM((groups, HEAD_DIM, rows), F32),
             pltpu.SemaphoreType.DMA((5,)),
             pltpu.SemaphoreType.DMA((rows // tile,)),
-            pltpu.SemaphoreType.DMA((2,)),
+            pltpu.SemaphoreType.DMA((2, rows // tile)),
         ],
         compiler_params=pltpu.CompilerParams(vmem_limit_bytes=36 << 20),
         cost_estimate=pl.CostEstimate(flops=60_000_000_000, bytes_accessed=20_000_000, transcendentals=15_000_000),

time: 345 us -> 346 us (level); the launches traced: 345 us -> 349 us
  Pallas kernels: 306 us -> 315 us
  waiting for transfers between devices: 10.7 us -> 6.3 us
    pallas_call x1, Pallas kernels: 56.1 us -> 71.6 us  [finish(): pl.pallas_call(functools.partial(finish_body, n_blk, n_head), out_shape=(...]
    pallas_call x1, Pallas kernels: 51.1 us -> 38 us  [own_grads(): pl.pallas_call(functools.partial(own_grads_body, groups=groups, rows=rows...]
    pallas_call x1, Pallas kernels: 19.1 us -> 24.8 us  [outer_grads(): pl.pallas_call(functools.partial(outer_grads_body, groups=groups, rows=ro...]
    reduce_scatter x1, waiting for transfers between devices: 10.7 us -> 6.24 us  [body(): owned = lax.psum_scatter(grads, BOTH, scatter_dimension=0, tiled=True)]
    pallas_call x1, Pallas kernels: 36.6 us -> 32.5 us  [attend(): pl.pallas_call(functools.partial(attend_body, groups=groups, rows=rows, t...]
    pallas_call x1, Pallas kernels: 29.4 us -> 33.1 us  [to_tokens(): pl.pallas_call(functools.partial(to_tokens_body, n_blk, n_head), out_shap...]
  transfers between devices with their start and end apart: 4 -> 4, of which waited for: 1 -> 1; matrix products, arithmetic and copies ran while one was open for 1% -> 1% of each run, Pallas kernels for 79% -> 81%
where the time goes in v3:
time: 346 us; the launch traced here: 349 us
  Pallas kernels  315 us (91%)
  between operations  14.4 us (4%)
  waiting for transfers between devices  6.3 us (2%)
  starting transfers between devices  5.97 us (2%)
  local copies, waits for them, and re-layouts  5.79 us (2%)
    pallas_call x1, Pallas kernels, finish(): pl.pallas_call(functools.partial(finish_body, n_blk, n_head), out_shape=(...  71.6 us
    pallas_call x1, Pallas kernels, collect(): pl.pallas_call(functools.partial(collect_body, n_blk, n_head, chunks), ou...  66.9 us
    pallas_call x1, Pallas kernels, own_grads(): pl.pallas_call(functools.partial(own_grads_body, groups=groups, rows=rows...  38 us
    pallas_call x1, Pallas kernels, to_tokens(): pl.pallas_call(functools.partial(to_tokens_body, n_blk, n_head), out_shap...  33.1 us
    pallas_call x1, Pallas kernels, attend(): pl.pallas_call(functools.partial(attend_body, groups=groups, rows=rows, t...  32.5 us
    pallas_call x1, Pallas kernels, dense(): pl.pallas_call(functools.partial(dense_body, blocks=blocks, count=count),...  28.8 us
    pallas_call x1, Pallas kernels, outer_grads(): pl.pallas_call(functools.partial(outer_grads_body, groups=groups, rows=ro...  24.8 us
    pallas_call x1, Pallas kernels, to_heads(): pl.pallas_call(functools.partial(to_heads_body, n_blk, n_head), out_shape...  15.3 us
  transfers between devices with their start and end apart: 4, of which 1 were waited for; matrix products, arithmetic and copies ran while one was open for 1% of the time, Pallas kernels for 81%

profile of v3, /device:TPU:0, one launch (start us, length us, event | category | flops | bytes accessed | tf_op | source)
XLA Modules:
  0.0 349.4 jit_solution(16315737802779793976)
XLA Ops:
  7.2 2.2 pack.1
  9.5 0.8 fusion.1
  10.4 66.9 %collect.1 = (bf16[3,4,512,768]{3,2,1,0:T(8,128)(2,1)}, bf16[8,4,32,576]{3,2,1,0:T(8,128)(2,1)}, bf16[576,2048]{1,0:T(8,128)(2,1)}, bf16[576,768]{1,0:T(8,128)(2...) custom-call(bf16[512,768]{1,0:T(8,128)(2,1)} %x_ref.3, ...), custom_call_target="tpu_custom_call" | custom-call | tf_op jit(solution)/shard_map/collect/pallas_call | solution.py:680
  77.4 0.3 convert_reduce_fusion
  77.7 32.5 %attend.1 = (bf16[4,192,512]{2,1,0:T(8,128)(2,1)}, f32[3,2048]{1,0:T(4,128)}, bf16[576,6144]{1,0:T(8,128)(2,1)}) custom-call(s32[4]{0:T(128)S(1)} %get-tuple-element.107.lo_ref, s32[4]{0:T(128)S(1)} %get-tuple-element.108.hi_ref, s32[1,6144]{1,0:T(1,128)S(1)} %bitcast.30, f32[576,1]{1,0:T(8,128)S(1)} %get-tuple-element.53.bias_ref, ...), custom_call_target="tpu_custom_call" | custom-call | flops 35999997952 | bytes 24000000 | tf_op jit(solution)/shard_map/attend/pallas_call | solution.py:189
  110.2 33.1 %to_tokens.1 = (bf16[4,192,512]{2,1,0:T(8,128)(2,1)}, f32[3,2048]{1,0:T(4,128)}, f32[3,2048]{1,0:T(4,128)}) custom-call(bf16[4,192,512]{2,1,0:T(8,128)(2,1)} %get-tuple-element.57.out_ref, f32[3,2048]{1,0:T(4,128)} %get-tuple-element.58.lse_ref), custom_call_target="tpu_custom_call" | custom-call | tf_op jit(solution)/shard_map/to_tokens/pallas_call | solution.py:898
  143.4 28.8 %dense.1 = (bf16[512,768]{1,0:T(8,128)(2,1)}, f32[512,768]{1,0:T(8,128)}, bf16[768,512]{1,0:T(8,128)(2,1)}, f32[4,3,512]{2,1,0:T(4,128)}, f32[8,768]{1,0:T(8,128...) custom-call(bf16[512,768]{1,0:T(8,128)(2,1)} %x_ref.3, bf16[768,512]{1,0:T(8,128)(2,1)} %bitcast.52, ...), custom_call_target="tpu_custom_call" | custom-call | flops 16999999488 | bytes 30000000 | tf_op jit(solution)/shard_map/dense/pallas_call | solution.py:1211
  172.2 15.3 %to_heads.1 = (bf16[192,2048]{1,0:T(8,128)(2,1)}, f32[4,3,512]{2,1,0:T(4,128)}, f32[4,3,512]{2,1,0:T(4,128)}, f32[4,3,512]{2,1,0:T(4,128)}) custom-call(bf16[4,192,512]{2,1,0:T(8,128)(2,1)} %bitcast.40, f32[4,3,512]{2,1,0:T(4,128)} %get-tuple-element.66.dpart_ref), custom_call_target="tpu_custom_call" | custom-call | tf_op jit(solution)/shard_map/to_heads/pallas_call | solution.py:960
  187.5 1.3 collective-permute-start.1
  188.8 4.6 %collective-permute-start = (bf16[192,2048]{1,0:T(8,128)(2,1)}, bf16[192,2048]{1,0:T(8,128)(2,1)S(1)}, u32[]{:S(2)}, u32[]{:S(2)}) collective-permute-start(bf16[192,2048]{1,0:T(8,128)(2,1)} %get-tuple-element.67.do_hbm), channel_id=1, source_target_pairs={{0,4},{4,8},{8,12},{12,16},{16,20},{20,24},{24,28},{1,5},{5,9},{9,... | collective-permute-start | bytes 2359304 | tf_op jit(solution)/shard_map/ppermute | solution.py:1260
  193.4 0.8 copy-done.5
  194.2 38.0 %own_grads.1 = (bf16[3,64,2048]{2,1,0:T(8,128)(2,1)}, f32[3,2048,64]{2,1,0:T(8,128)}, f32[3,2048,64]{2,1,0:T(8,128)}) custom-call(s32[4]{0:T(128)S(1)} %get-tuple-element.107.lo_ref, s32[4]{0:T(128)S(1)} %get-tuple-element.108.hi_ref, bf16[576,6144]{1,0:T(8,128)(2,1)} %get-tuple-element.64.qkv_hbm, bf16[192,2048]{1,0:T(8,128)(2,1)} %get-tuple-element.67.do_hbm, ...), custom_call_target="tpu_custom_call" | custom-call | flops 60000002048 | bytes 20000000 | tf_op jit(solution)/shard_map/own_grads/pallas_call | solution.py:309
  232.2 0.5 broadcast.48
  232.7 0.7 reduce.19
  234.1 24.8 %outer_grads.1 = (bf16[768,576]{1,0:T(8,128)(2,1)}, bf16[2048,768]{1,0:T(8,128)(2,1)}, f32[576,1]{1,0:T(8,128)S(1)}) custom-call(s32[4]{0:T(128)S(1)} %get-tuple-element.107.lo_ref, s32[4]{0:T(128)S(1)} %get-tuple-element.108.hi_ref, bf16[576,6144]{1,0:T(8,128)(2,1)} %get-tuple-element.64.qkv_hbm, bf16[192,2048]{1,0:T(8,128)(2,1)S(1)} %collective-permute-done.do_lo_ref, ...), custom_call_target="tpu_custom_call" | custom-call | flops 24000000000 | bytes 24000000 | tf_op jit(solution)/shard_map/outer_grads/pallas_call | solution.py:441
  259.1 0.2 dynamic_update_slice.6
  259.4 0.2 dynamic_update_slice.7
  259.9 71.6 %finish.1 = (bf16[512,768]{1,0:T(8,128)(2,1)S(1)}, f32[24,2304]{1,0:T(8,128)S(1)}, f32[8,128]{1,0:T(8,128)S(1)}) custom-call(bf16[4,512,768]{2,1,0:T(8,128)(2,1)} %bitcast.38, f32[512,768]{1,0:T(8,128)} %get-tuple-element.77.first_hbm, bf16[8,4,24,576]{3,2,1,0:T(8,128)(2,1)} %bitcast.39, f32[8,4,8,128]{3,2,1,0:T(8,128)S(1)} %bitcast.29), custom_call_target="tpu_custom_call" | custom-call | tf_op jit(solution)/shard_map/finish/pallas_call | solution.py:785
  331.5 0.6 slice.84
  332.1 0.6 fusion.3
  332.7 6.2 %reduce-scatter.2.cloned.1.call-done.packed_ref = bf16[24,6912]{1,0:T(8,128)(2,1)} async-done(((bf16[768,6912]{1,0:T(8,128)(2,1)}), bf16[24,6912]{1,0:T(8,128)(2,1)}) %reduce-scatter.2.cloned.1.call-update) | async-done | bytes 331792 | tf_op jit(solution)/shard_map/reduce_scatter | solution.py:1308
  339.0 2.0 unpack.1
  341.0 0.9 copy.36
  341.9 0.7 copy.37
  (48 shorter events, 1.4 us)
Async XLA Ops:
  7.2 136.2 %all-gather.2.cloned.1.call-start = ((), (), s32[]{:S(2)}) async-start(), calls=%async_computation.1 | async-start | bytes 10948608 | tf_op jit(solution)/shard_map/all_gather | solution.py:1280
  9.4 329.6 %reduce-scatter.2.cloned.1.call-start = ((), (), s32[]{:S(2)}) async-start(), calls=%async_computation.2 | async-start | bytes 10948608 | tf_op jit(solution)/shard_map/reduce_scatter | solution.py:1308
  77.4 32.8 %copy-start.6 = (f32[8,768]{1,0:T(8,128)}, f32[8,768]{1,0:T(8,128)S(1)}, u32[]{:S(2)}) copy-start(f32[8,768]{1,0:T(8,128)S(1)} %get-tuple-element.60.vec_ref) | copy-start | bytes 73732
  77.4 32.8 %copy-start.7 = (f32[1,3072]{1,0:T(1,128)}, f32[1,3072]{1,0:T(1,128)S(1)}, u32[]{:S(2)}) copy-start(f32[1,3072]{1,0:T(1,128)S(1)} %get-tuple-element.61.inb_ref) | copy-start | bytes 36868
  172.2 21.2 %copy-start = (f32[3,2048]{1,0:T(4,128)S(1)}, f32[3,2048]{1,0:T(4,128)}, u32[]{:S(2)}) copy-start(f32[3,2048]{1,0:T(4,128)} %get-tuple-element.58.lse_ref) | copy-start | bytes 73732
  187.5 46.5 %collective-permute-start.1 = (bf16[192,2048]{1,0:T(8,128)(2,1)}, bf16[192,2048]{1,0:T(8,128)(2,1)S(1)}, u32[]{:S(2)}, u32[]{:S(2)}) collective-permute-start(bf16[192,2048]{1,0:T(8,128)(2,1)} %get-tuple-element.67.do_hbm), channel_id=1, source_target_pairs={{4,0},{8,4},{12,8},{16,12},{20,16},{24,20},{28,24},{5,1},{9,5},{13... | collective-permute-start | bytes 2359304 | tf_op jit(solution)/shard_map/ppermute | solution.py:1260
  188.8 45.2 %collective-permute-start = (bf16[192,2048]{1,0:T(8,128)(2,1)}, bf16[192,2048]{1,0:T(8,128)(2,1)S(1)}, u32[]{:S(2)}, u32[]{:S(2)}) collective-permute-start(bf16[192,2048]{1,0:T(8,128)(2,1)} %get-tuple-element.67.do_hbm), channel_id=1, source_target_pairs={{0,4},{4,8},{8,12},{12,16},{16,20},{20,24},{24,28},{1,5},{5,9},{9,... | collective-permute-start | bytes 2359304 | tf_op jit(solution)/shard_map/ppermute | solution.py:1260
  193.4 0.8 copy-start.5
  194.2 38.5 %copy-start.9 = (f32[1,3072]{1,0:T(1,128)S(1)}, f32[1,3072]{1,0:T(1,128)}, u32[]{:S(2)}) copy-start(f32[1,3072]{1,0:T(1,128)} %get-tuple-element.81) | copy-start | bytes 36868
  194.2 39.3 %copy-start.8 = (f32[8,768]{1,0:T(8,128)S(1)}, f32[8,768]{1,0:T(8,128)}, u32[]{:S(2)}) copy-start(f32[8,768]{1,0:T(8,128)} %get-tuple-element.80) | copy-start | bytes 73732
  194.2 39.9 %copy-start.1 = (f32[3,2048]{1,0:T(4,128)S(1)}, f32[3,2048]{1,0:T(4,128)}, u32[]{:S(2)}) copy-start(f32[3,2048]{1,0:T(4,128)} %get-tuple-element.68.lse_lo_ref) | copy-start | bytes 73732
  194.2 39.9 %copy-start.2 = (f32[3,2048]{1,0:T(4,128)S(1)}, f32[3,2048]{1,0:T(4,128)}, u32[]{:S(2)}) copy-start(f32[3,2048]{1,0:T(4,128)} %get-tuple-element.69.lse_hi_ref) | copy-start | bytes 73732
  194.2 39.9 %copy-start.3 = (f32[4,3,512]{2,1,0:T(4,128)S(1)}, f32[4,3,512]{2,1,0:T(4,128)}, u32[]{:S(2)}) copy-start(f32[4,3,512]{2,1,0:T(4,128)} %get-tuple-element.70) | copy-start | bytes 73732
  194.2 39.9 %copy-start.4 = (f32[4,3,512]{2,1,0:T(4,128)S(1)}, f32[4,3,512]{2,1,0:T(4,128)}, u32[]{:S(2)}) copy-start(f32[4,3,512]{2,1,0:T(4,128)} %get-tuple-element.71) | copy-start | bytes 73732
Sparse Core Ops, SparseCore 0:
  11.5 114.1 all-gather.1
  172.3 166.5 reduce-scatter.1

commit v4 on v3

--- a/solution.py
+++ b/solution.py
@@ -1151,7 +1151,7 @@
         acc_ref[...] += mm(act, w[:, cols(down_at, c)])
         return carry
 
-    lax.fori_loop(0, blocks, up_down, 0, unroll=2)
+    lax.fori_loop(0, blocks, up_down, 0, unroll=True)
     unit2, r2 = normalize(acc_ref[...])
     out_ref[...] = (unit2 * ln2_gain + ln2_bias).astype(BF16)
     dy = cot_ref[...].astype(F32)

time: 346 us -> 343 us (level); the launches traced: 349 us -> 341 us
  waiting for transfers between devices: 6.3 us -> 0.6 us
    pallas_call x1, Pallas kernels: 33.1 us -> 43.6 us  [to_tokens(): pl.pallas_call(functools.partial(to_tokens_body, n_blk, n_head), out_shap...]
    pallas_call x1, Pallas kernels: 71.6 us -> 81 us  [finish(): pl.pallas_call(functools.partial(finish_body, n_blk, n_head), out_shape=(...]
    pallas_call x1, Pallas kernels: 24.8 us -> 16.4 us  [outer_grads(): pl.pallas_call(functools.partial(outer_grads_body, groups=groups, rows=ro...]
    pallas_call x1, Pallas kernels: 32.5 us -> 24.2 us  [attend(): pl.pallas_call(functools.partial(attend_body, groups=groups, rows=rows, t...]
    pallas_call x1, Pallas kernels: 38 us -> 31.5 us  [own_grads(): pl.pallas_call(functools.partial(own_grads_body, groups=groups, rows=rows...]
    reduce_scatter x1, waiting for transfers between devices: 6.24 us -> 0.54 us  [body(): owned = lax.psum_scatter(grads, BOTH, scatter_dimension=0, tiled=True)]
  transfers between devices with their start and end apart: 4 -> 4, of which waited for: 1 -> 1; matrix products, arithmetic and copies ran while one was open for 1% -> 2% of each run, Pallas kernels for 81% -> 82%
where the time goes in v4:
time: 343 us; the launch traced here: 341 us
  Pallas kernels  313 us (91%)
  between operations  14.4 us (4%)
  starting transfers between devices  5.97 us (2%)
  local copies, waits for them, and re-layouts  5.79 us (2%)
    pallas_call x1, Pallas kernels, finish(): pl.pallas_call(functools.partial(finish_body, n_blk, n_head), out_shape=(...  81 us
    pallas_call x1, Pallas kernels, collect(): pl.pallas_call(functools.partial(collect_body, n_blk, n_head, chunks), ou...  66.9 us
    pallas_call x1, Pallas kernels, to_tokens(): pl.pallas_call(functools.partial(to_tokens_body, n_blk, n_head), out_shap...  43.6 us
    pallas_call x1, Pallas kernels, own_grads(): pl.pallas_call(functools.partial(own_grads_body, groups=groups, rows=rows...  31.5 us
    pallas_call x1, Pallas kernels, dense(): pl.pallas_call(functools.partial(dense_body, blocks=blocks, count=count),...  28.4 us
    pallas_call x1, Pallas kernels, attend(): pl.pallas_call(functools.partial(attend_body, groups=groups, rows=rows, t...  24.2 us
    pallas_call x1, Pallas kernels, to_heads(): pl.pallas_call(functools.partial(to_heads_body, n_blk, n_head), out_shape...  16.9 us
    pallas_call x1, Pallas kernels, outer_grads(): pl.pallas_call(functools.partial(outer_grads_body, groups=groups, rows=ro...  16.4 us
  transfers between devices with their start and end apart: 4, of which 1 were waited for; matrix products, arithmetic and copies ran while one was open for 2% of the time, Pallas kernels for 82%

profile of v4, /device:TPU:0, one launch (start us, length us, event | category | flops | bytes accessed | tf_op | source)
XLA Modules:
  0.0 341.5 jit_solution(14475731958748566561)
XLA Ops:
  7.2 2.2 pack.1
  9.5 0.8 fusion.1
  10.4 66.9 %collect.1 = (bf16[3,4,512,768]{3,2,1,0:T(8,128)(2,1)}, bf16[8,4,32,576]{3,2,1,0:T(8,128)(2,1)}, bf16[576,2048]{1,0:T(8,128)(2,1)}, bf16[576,768]{1,0:T(8,128)(2...) custom-call(bf16[512,768]{1,0:T(8,128)(2,1)} %x_ref.3, ...), custom_call_target="tpu_custom_call" | custom-call | tf_op jit(solution)/shard_map/collect/pallas_call | solution.py:680
  77.4 0.3 convert_reduce_fusion
  77.7 24.2 %attend.1 = (bf16[4,192,512]{2,1,0:T(8,128)(2,1)}, f32[3,2048]{1,0:T(4,128)}, bf16[576,6144]{1,0:T(8,128)(2,1)}) custom-call(s32[4]{0:T(128)S(1)} %get-tuple-element.107.lo_ref, s32[4]{0:T(128)S(1)} %get-tuple-element.108.hi_ref, s32[1,6144]{1,0:T(1,128)S(1)} %bitcast.30, f32[576,1]{1,0:T(8,128)S(1)} %get-tuple-element.53.bias_ref, ...), custom_call_target="tpu_custom_call" | custom-call | flops 35999997952 | bytes 24000000 | tf_op jit(solution)/shard_map/attend/pallas_call | solution.py:189
  101.8 43.6 %to_tokens.1 = (bf16[4,192,512]{2,1,0:T(8,128)(2,1)}, f32[3,2048]{1,0:T(4,128)}, f32[3,2048]{1,0:T(4,128)}) custom-call(bf16[4,192,512]{2,1,0:T(8,128)(2,1)} %get-tuple-element.57.out_ref, f32[3,2048]{1,0:T(4,128)} %get-tuple-element.58.lse_ref), custom_call_target="tpu_custom_call" | custom-call | tf_op jit(solution)/shard_map/to_tokens/pallas_call | solution.py:898
  145.4 28.4 %dense.1 = (bf16[512,768]{1,0:T(8,128)(2,1)}, f32[512,768]{1,0:T(8,128)}, bf16[768,512]{1,0:T(8,128)(2,1)}, f32[4,3,512]{2,1,0:T(4,128)}, f32[8,768]{1,0:T(8,128...) custom-call(bf16[512,768]{1,0:T(8,128)(2,1)} %x_ref.3, bf16[768,512]{1,0:T(8,128)(2,1)} %bitcast.52, ...), custom_call_target="tpu_custom_call" | custom-call | flops 16999999488 | bytes 30000000 | tf_op jit(solution)/shard_map/dense/pallas_call | solution.py:1211
  173.9 16.9 %to_heads.1 = (bf16[192,2048]{1,0:T(8,128)(2,1)}, f32[4,3,512]{2,1,0:T(4,128)}, f32[4,3,512]{2,1,0:T(4,128)}, f32[4,3,512]{2,1,0:T(4,128)}) custom-call(bf16[4,192,512]{2,1,0:T(8,128)(2,1)} %bitcast.40, f32[4,3,512]{2,1,0:T(4,128)} %get-tuple-element.66.dpart_ref), custom_call_target="tpu_custom_call" | custom-call | tf_op jit(solution)/shard_map/to_heads/pallas_call | solution.py:960
  190.8 1.3 collective-permute-start.1
  192.1 4.6 %collective-permute-start = (bf16[192,2048]{1,0:T(8,128)(2,1)}, bf16[192,2048]{1,0:T(8,128)(2,1)S(1)}, u32[]{:S(2)}, u32[]{:S(2)}) collective-permute-start(bf16[192,2048]{1,0:T(8,128)(2,1)} %get-tuple-element.67.do_hbm), channel_id=1, source_target_pairs={{0,4},{4,8},{8,12},{12,16},{16,20},{20,24},{24,28},{1,5},{5,9},{9,... | collective-permute-start | bytes 2359304 | tf_op jit(solution)/shard_map/ppermute | solution.py:1260
  196.7 0.8 copy-done.5
  197.5 31.5 %own_grads.1 = (bf16[3,64,2048]{2,1,0:T(8,128)(2,1)}, f32[3,2048,64]{2,1,0:T(8,128)}, f32[3,2048,64]{2,1,0:T(8,128)}) custom-call(s32[4]{0:T(128)S(1)} %get-tuple-element.107.lo_ref, s32[4]{0:T(128)S(1)} %get-tuple-element.108.hi_ref, bf16[576,6144]{1,0:T(8,128)(2,1)} %get-tuple-element.64.qkv_hbm, bf16[192,2048]{1,0:T(8,128)(2,1)} %get-tuple-element.67.do_hbm, ...), custom_call_target="tpu_custom_call" | custom-call | flops 60000002048 | bytes 20000000 | tf_op jit(solution)/shard_map/own_grads/pallas_call | solution.py:309
  229.0 0.5 broadcast.48
  229.5 0.7 reduce.19
  230.9 16.4 %outer_grads.1 = (bf16[768,576]{1,0:T(8,128)(2,1)}, bf16[2048,768]{1,0:T(8,128)(2,1)}, f32[576,1]{1,0:T(8,128)S(1)}) custom-call(s32[4]{0:T(128)S(1)} %get-tuple-element.107.lo_ref, s32[4]{0:T(128)S(1)} %get-tuple-element.108.hi_ref, bf16[576,6144]{1,0:T(8,128)(2,1)} %get-tuple-element.64.qkv_hbm, bf16[192,2048]{1,0:T(8,128)(2,1)S(1)} %collective-permute-done.do_lo_ref, ...), custom_call_target="tpu_custom_call" | custom-call | flops 24000000000 | bytes 24000000 | tf_op jit(solution)/shard_map/outer_grads/pallas_call | solution.py:441
  247.5 0.2 dynamic_update_slice.6
  247.8 0.2 dynamic_update_slice.7
  248.3 81.0 %finish.1 = (bf16[512,768]{1,0:T(8,128)(2,1)S(1)}, f32[24,2304]{1,0:T(8,128)S(1)}, f32[8,128]{1,0:T(8,128)S(1)}) custom-call(bf16[4,512,768]{2,1,0:T(8,128)(2,1)} %bitcast.38, f32[512,768]{1,0:T(8,128)} %get-tuple-element.77.first_hbm, bf16[8,4,24,576]{3,2,1,0:T(8,128)(2,1)} %bitcast.39, f32[8,4,8,128]{3,2,1,0:T(8,128)S(1)} %bitcast.29), custom_call_target="tpu_custom_call" | custom-call | tf_op jit(solution)/shard_map/finish/pallas_call | solution.py:785
  329.3 0.6 slice.84
  329.9 0.6 fusion.3
  330.5 0.5 reduce-scatter.2.cloned.1.call-done.packed_ref
  331.1 2.0 unpack.1
  333.1 0.9 copy.36
  334.0 0.7 copy.37
  (48 shorter events, 1.4 us)
Async XLA Ops:
  7.2 138.3 %all-gather.2.cloned.1.call-start = ((), (), s32[]{:S(2)}) async-start(), calls=%async_computation.1 | async-start | bytes 10948608 | tf_op jit(solution)/shard_map/all_gather | solution.py:1280
  9.4 321.6 %reduce-scatter.2.cloned.1.call-start = ((), (), s32[]{:S(2)}) async-start(), calls=%async_computation.2 | async-start | bytes 10948608 | tf_op jit(solution)/shard_map/reduce_scatter | solution.py:1308
  77.4 24.5 %copy-start.6 = (f32[8,768]{1,0:T(8,128)}, f32[8,768]{1,0:T(8,128)S(1)}, u32[]{:S(2)}) copy-start(f32[8,768]{1,0:T(8,128)S(1)} %get-tuple-element.60.vec_ref) | copy-start | bytes 73732
  77.4 24.5 %copy-start.7 = (f32[1,3072]{1,0:T(1,128)}, f32[1,3072]{1,0:T(1,128)S(1)}, u32[]{:S(2)}) copy-start(f32[1,3072]{1,0:T(1,128)S(1)} %get-tuple-element.61.inb_ref) | copy-start | bytes 36868
  173.9 22.8 %copy-start = (f32[3,2048]{1,0:T(4,128)S(1)}, f32[3,2048]{1,0:T(4,128)}, u32[]{:S(2)}) copy-start(f32[3,2048]{1,0:T(4,128)} %get-tuple-element.58.lse_ref) | copy-start | bytes 73732
  190.8 40.1 %collective-permute-start.1 = (bf16[192,2048]{1,0:T(8,128)(2,1)}, bf16[192,2048]{1,0:T(8,128)(2,1)S(1)}, u32[]{:S(2)}, u32[]{:S(2)}) collective-permute-start(bf16[192,2048]{1,0:T(8,128)(2,1)} %get-tuple-element.67.do_hbm), channel_id=1, source_target_pairs={{4,0},{8,4},{12,8},{16,12},{20,16},{24,20},{28,24},{5,1},{9,5},{13... | collective-permute-start | bytes 2359304 | tf_op jit(solution)/shard_map/ppermute | solution.py:1260
  192.1 38.8 %collective-permute-start = (bf16[192,2048]{1,0:T(8,128)(2,1)}, bf16[192,2048]{1,0:T(8,128)(2,1)S(1)}, u32[]{:S(2)}, u32[]{:S(2)}) collective-permute-start(bf16[192,2048]{1,0:T(8,128)(2,1)} %get-tuple-element.67.do_hbm), channel_id=1, source_target_pairs={{0,4},{4,8},{8,12},{12,16},{16,20},{20,24},{24,28},{1,5},{5,9},{9,... | collective-permute-start | bytes 2359304 | tf_op jit(solution)/shard_map/ppermute | solution.py:1260
  196.7 0.8 copy-start.5
  197.5 32.1 %copy-start.9 = (f32[1,3072]{1,0:T(1,128)S(1)}, f32[1,3072]{1,0:T(1,128)}, u32[]{:S(2)}) copy-start(f32[1,3072]{1,0:T(1,128)} %get-tuple-element.81) | copy-start | bytes 36868
  197.5 32.8 %copy-start.8 = (f32[8,768]{1,0:T(8,128)S(1)}, f32[8,768]{1,0:T(8,128)}, u32[]{:S(2)}) copy-start(f32[8,768]{1,0:T(8,128)} %get-tuple-element.80) | copy-start | bytes 73732
  197.5 33.4 %copy-start.1 = (f32[3,2048]{1,0:T(4,128)S(1)}, f32[3,2048]{1,0:T(4,128)}, u32[]{:S(2)}) copy-start(f32[3,2048]{1,0:T(4,128)} %get-tuple-element.68.lse_lo_ref) | copy-start | bytes 73732
  197.5 33.4 %copy-start.2 = (f32[3,2048]{1,0:T(4,128)S(1)}, f32[3,2048]{1,0:T(4,128)}, u32[]{:S(2)}) copy-start(f32[3,2048]{1,0:T(4,128)} %get-tuple-element.69.lse_hi_ref) | copy-start | bytes 73732
  197.5 33.4 %copy-start.3 = (f32[4,3,512]{2,1,0:T(4,128)S(1)}, f32[4,3,512]{2,1,0:T(4,128)}, u32[]{:S(2)}) copy-start(f32[4,3,512]{2,1,0:T(4,128)} %get-tuple-element.70) | copy-start | bytes 73732
  197.5 33.4 %copy-start.4 = (f32[4,3,512]{2,1,0:T(4,128)S(1)}, f32[4,3,512]{2,1,0:T(4,128)}, u32[]{:S(2)}) copy-start(f32[4,3,512]{2,1,0:T(4,128)} %get-tuple-element.71) | copy-start | bytes 73732
Sparse Core Ops, SparseCore 0:
  11.5 114.1 all-gather.1
  174.0 156.9 reduce-scatter.1
